TPU v7x, 32 devices: a whole 2x2x4 slice. The times are simulated.
32 devices in a mesh: group: 2 (over x), island: 16 (over z, y, core).
Axes of the slice: x: 2, y: 2, z: 4, core: 2. Of those that a mesh axis runs over, the one named last changes fastest.
Arguments:
- particles: bfloat16 [256, 4, 8192], P(('group', 'island')), parts along dimension 0, may hold values from -6 to 6
- ancestors: int32 [2, 32, 8], P(None, ('group', 'island')), parts along dimension 1, may hold values from 0 to 15, as said below
- migration: int32 [2, 32, 8], P(None, ('group', 'island')), parts along dimension 1, may hold values from 0 to 7, each once within a row
- pattern: int32 [256, 5], P('group'), parts along dimension 0, may hold values from 0 to 127, as said below
- coupling: bfloat16 [256, 5, 4096], P('group'), parts along dimension 0, may hold values from -0.3125 to 0.3125
- cell_rate: float32 [16384], P('group'), parts along dimension 0, may hold values from 0.3 to 3
- current: float32 [8], P('group'), parts along dimension 0, may hold values from -1 to 1
- observed: float32 [8, 8192], P('group'), parts along dimension 0, may hold values from -6 to 6
- noise_seeds: int32 [32, 4], P(('group', 'island')), parts along dimension 0, may hold values from 0 to 1048575
Outputs:
- final_states: bfloat16 [256, 4, 8192], P(('group', 'island')), parts along dimension 0
- evidence: float32 [32], P(('group', 'island')), parts along dimension 0
- log_weight: float32 [2, 256], P(None, ('group', 'island')), parts along dimension 1
There are 2 independent parts, one for each index of `group`. A program takes and returns all parts, laid end to end along the dimension named above; each array names one. Nothing has to cross between parts.
Inputs may be any that keep to these rules, and one draw needn't show every extreme that they name: `ancestors`: each entry indexes the 16 particles of the device's island; at most 2 entries of one device and epoch point to the other device of the island, and in every epoch some device has exactly 2 such entries. `migration`: each row of one device and epoch holds every slot once. `pattern`: row b holds b, (b + 1) mod 128, (b - 1) mod 128 and two more block numbers.
All inputs are finite; a program needn't handle non-finite values.
Results may differ from a plain program's by a relative error of at most 0.0056.
Values may be sent and summed in bfloat16 or wider, within the bound.
No kernel may reach another device: no remote copies, remote signals or barrier semaphores. Data moves between devices by JAX's collectives and lax.ppermute only.
A program may use at most 128 MiB of HBM per device.

v0:
```python
import functools

import jax
import jax.numpy as jnp
from jax import lax
from jax.experimental import pallas as pl
from jax.experimental.pallas import tpu as pltpu
from jax.sharding import PartitionSpec as P

CELLS = 8192
STATES = 4
BLOCK = 64
NEIGH = 5
EPOCHS = 2
STEPS_EPOCH = 2
STEPS = EPOCHS * STEPS_EPOCH
BLOCKS = 128
ROWS = 8
LANES = 128
PAIRS = CELLS // LANES
HALF = BLOCK // 2
NOISE_SCALE = 0.3 * 2.449489742783178 / 16777216.0

VMEM = pl.BlockSpec(memory_space=pltpu.VMEM)
SMEM = pl.BlockSpec(memory_space=pltpu.SMEM)
HBM = pl.BlockSpec(memory_space=pl.ANY)


def params(mib):
    return pltpu.CompilerParams(vmem_limit_bytes=mib << 20)


def from_partner(value):
    pairs = [(source, source ^ 1) for source in range(lax.axis_size("island"))]
    return lax.ppermute(value, "island", pairs)


def from_behind(block):
    count = lax.axis_size("island")
    route = [((i - 2) % count, i) for i in range(count)]
    return lax.ppermute(block, "island", route)


def shifted(hashed):
    return hashed ^ lax.shift_right_logical(hashed, jnp.full(hashed.shape, 16, jnp.int32))


def scramble(hashed):
    hashed = shifted(hashed) * 73244475
    hashed = shifted(hashed) * 73244475
    return shifted(hashed) & 16777215


def noise_kernel(seeds, out):
    row = lax.broadcasted_iota(jnp.int32, (STATES * ROWS, LANES), 0)
    lane = lax.broadcasted_iota(jnp.int32, (STATES * ROWS, LANES), 1)
    counter = 2 * (((row % ROWS) * STATES + row // ROWS) * CELLS + lane)
    for step in range(STEPS):
        start = counter + seeds[0, step] * 40503

        def one(q, carry):
            anchor = start + q * (2 * LANES)
            apart = scramble(anchor) - scramble(anchor + 1)
            out[step, q] = apart.astype(jnp.float32) * NOISE_SCALE
            return carry

        lax.fori_loop(0, PAIRS, one, 0, unroll=4)


def weights_kernel(coupling, out, wide):
    group = 16

    def one(g, carry):
        for k in range(NEIGH):
            for r in range(HALF):
                wide[k, r * group : (r + 1) * group, :] = coupling[
                    k, pl.ds(pl.multiple_of(g * group, group), group), r * LANES : (r + 1) * LANES
                ].astype(jnp.float32)
            for b in range(group):
                picked = wide[k, pl.ds(b, HALF, stride=group), :]
                out[g * group + b, k * HALF : (k + 1) * HALF, :] = picked.astype(jnp.bfloat16)
        return carry

    lax.fori_loop(0, BLOCKS // group, one, 0)


def leaving_kernel(epoch, ancestors, migration, half, local, partner, out, sem):
    chosen = ancestors[epoch, 0, migration[epoch, 0, 0]]
    slot = chosen % ROWS
    is_local = chosen // ROWS == half[0]

    @pl.when(is_local)
    def _():
        copy = pltpu.make_async_copy(local.at[pl.ds(slot, 1)], out, sem)
        copy.start()
        copy.wait()

    @pl.when(jnp.logical_not(is_local))
    def _():
        copy = pltpu.make_async_copy(partner.at[pl.ds(slot, 1)], out, sem)
        copy.start()
        copy.wait()


def epoch_kernel(
    epoch,
    ancestors,
    migration,
    half,
    pattern,
    current,
    temper,
    local,
    partner,
    arriving,
    weights,
    noise,
    cell_rate,
    observed,
    *rest,
):
    if epoch:
        before, states, logliks, gather, natural, spread, unmix, total = rest
    else:
        states, logliks, gather, natural, spread, unmix, total = rest
    lane = lax.broadcasted_iota(jnp.int32, (1, LANES), 1)

    source = lax.broadcasted_iota(jnp.int32, (LANES, 4 * LANES), 0)
    target = lax.broadcasted_iota(jnp.int32, (LANES, 4 * LANES), 1)
    tile = target // LANES
    wanted = (tile // 2) * BLOCK + (target % HALF) * 2 + tile % 2
    unmix[...] = jnp.where(source == wanted, 1.0, 0.0).astype(jnp.bfloat16)

    picks = []
    for j in range(ROWS):
        chosen = ancestors[epoch, 0, j]
        picks.append((chosen % ROWS, chosen // ROWS == half[0], migration[epoch, 0, 0] == j))

    def assemble(q, carry):
        lanes = pl.ds(pl.multiple_of(q * LANES, LANES), LANES)
        for j, (slot, is_local, is_new) in enumerate(picks):
            kept = jnp.where(
                is_local, local[slot, :, lanes].astype(jnp.float32), partner[slot, :, lanes].astype(jnp.float32)
            )
            gather[q, j * STATES : (j + 1) * STATES, :] = jnp.where(
                is_new, arriving[0, :, lanes].astype(jnp.float32), kept
            )
        for c in range(0, STATES, 2):
            two = [gather[q, pl.ds(c + d, ROWS, stride=STATES), :] for d in range(2)]
            natural[q, c * ROWS : (c + 2) * ROWS, :] = jnp.concatenate(two, axis=0).astype(jnp.bfloat16)
        return carry

    lax.fori_loop(0, PAIRS, assemble, 0, unroll=4)

    rows = STATES * ROWS

    def spread_out():
        chunk = 8

        def one(g, carry):
            cells = natural[pl.ds(g * chunk, chunk)].reshape(chunk * rows, LANES)
            placed = jnp.dot(cells, unmix[...], preferred_element_type=jnp.float32).astype(jnp.bfloat16)
            for q in range(chunk):
                for tile in range(4):
                    spread[
                        2 * (g * chunk + q) + tile // 2, (tile % 2) * rows : (tile % 2 + 1) * rows, :
                    ] = placed[q * rows : (q + 1) * rows, tile * LANES : (tile + 1) * LANES]
            return carry

        lax.fori_loop(0, PAIRS // chunk, one, 0)

    def product(b):
        pieces = [spread[pattern[k, b]] for k in range(NEIGH)]
        first = jnp.where(
            lane < HALF,
            pieces[0],
            jnp.where(lane < 2 * HALF, pieces[1], jnp.where(lane < 3 * HALF, pieces[2], pieces[3])),
        )
        both = jnp.concatenate([first, pieces[4][:, :HALF]], axis=1)
        return jnp.dot(both, weights[b], preferred_element_type=jnp.float32)

    for inner in range(STEPS_EPOCH):
        step = epoch * STEPS_EPOCH + inner
        last = inner == STEPS_EPOCH - 1
        now = current[step]
        spread_out()
        total[...] = jnp.zeros_like(total) if inner == 0 else total[...]

        def one(q, carry):
            left = product(2 * q)
            right = product(2 * q + 1)
            inside = jnp.where(lane < BLOCK, left[:rows], right[rows:])
            across = jnp.where(lane < BLOCK, right[:rows], left[rows:])
            coupled = inside + pltpu.roll(across, BLOCK, 1)
            mixed = 0.6 * natural[q].astype(jnp.float32) + 0.8 * coupled
            drawn = noise[step, q]
            charge, over, heat, film = (mixed[c * ROWS : (c + 1) * ROWS] for c in range(STATES))
            rate = cell_rate[pl.ds(q, 1), :]
            seen = observed[step, pl.ds(q, 1), :]
            tanh_over = jnp.tanh(over)
            fade = jnp.exp(-0.5 * jnp.abs(charge))
            warm = 0.6 * jnp.tanh(heat)
            rise = jnp.exp(warm + 2.0 * tanh_over) - jnp.exp(warm - 2.0 * tanh_over)
            reaction = (0.5 * rate) * rise * fade / (1.0 + fade * fade)
            new_charge = charge - 0.25 * reaction + drawn[:ROWS]
            new_over = 0.7 * over + 0.5 * (now - reaction) + drawn[ROWS : 2 * ROWS]
            new_heat = 0.9 * heat + 0.2 * reaction * tanh_over + drawn[2 * ROWS : 3 * ROWS]
            new_film = 0.95 * film + 0.02 * reaction * reaction + drawn[3 * ROWS :]
            predicted = (
                0.5 + 0.5 * jnp.tanh(0.5 * new_charge) - 0.4 * jnp.tanh(new_over) - (0.2 * now) * new_film
            )
            misfit = seen - predicted
            fresh = (new_charge, new_over, new_heat, new_film)
            if last:
                for c in range(STATES):
                    gather[q, pl.ds(c, ROWS, stride=STATES), :] = fresh[c]
            else:
                natural[q] = jnp.concatenate(fresh, axis=0).astype(jnp.bfloat16)
            return carry + misfit * misfit

        total[...] += lax.fori_loop(0, PAIRS, one, jnp.zeros((ROWS, LANES), jnp.float32), unroll=4)

    def finish(q, carry):
        lanes = pl.ds(pl.multiple_of(q * LANES, LANES), LANES)
        for j in range(ROWS):
            states[j, :, lanes] = gather[q, j * STATES : (j + 1) * STATES, :].astype(jnp.bfloat16)
        return carry

    lax.fori_loop(0, PAIRS, finish, 0, unroll=4)

    column = -0.5 * temper[0] * jnp.sum(total[...], axis=1, keepdims=True)
    slots = lax.broadcasted_iota(jnp.int32, (ROWS, LANES), 0)
    across_lanes = jnp.sum(jnp.where(slots == lane, column, 0.0), axis=0, keepdims=True)
    if epoch:
        logliks[0:1, :] = before[0:1, :]
    logliks[epoch : epoch + 1, :] = across_lanes


def weigh_kernel(own, other, log_weight, evidence):
    lane = lax.broadcasted_iota(jnp.int32, (EPOCHS, LANES), 1)
    real = lane < ROWS
    mine, theirs = own[...], other[...]
    peak = jnp.max(jnp.where(real, jnp.maximum(mine, theirs), -jnp.inf), axis=1, keepdims=True)
    shares = jnp.where(real, jnp.exp(mine - peak) + jnp.exp(theirs - peak), 0.0)
    lse = peak + jnp.log(jnp.sum(shares, axis=1, keepdims=True))
    log_weight[...] = (mine - lse)[:, :ROWS]
    per_cell = (lse - jnp.log(jnp.full(lse.shape, 2.0 * ROWS, jnp.float32))) / CELLS
    evidence[...] = jnp.sum(per_cell, axis=0, keepdims=True)


def on_device(
    particles, ancestors, migration, pattern, coupling, cell_rate, current, observed, noise_seeds
):
    position = lax.axis_index("island")
    half = (position % 2).astype(jnp.int32)[None]
    temper = (0.25 * jnp.power(2.0, (position // 2 % 4).astype(jnp.float32)))[None]
    shape = jax.ShapeDtypeStruct

    noise = pl.pallas_call(
        noise_kernel,
        out_shape=shape((STEPS, PAIRS, STATES * ROWS, LANES), jnp.float32),
        in_specs=[SMEM],
        out_specs=VMEM,
        compiler_params=params(2),
        cost_estimate=pl.CostEstimate(flops=30000000, bytes_accessed=12000000, transcendentals=0),
        name="noise",
    )(noise_seeds)
    weights = pl.pallas_call(
        weights_kernel,
        out_shape=shape((BLOCKS, NEIGH * HALF, LANES), jnp.bfloat16),
        in_specs=[VMEM],
        out_specs=VMEM,
        scratch_shapes=[pltpu.VMEM((NEIGH, HALF * 16, LANES), jnp.float32)],
        compiler_params=params(4),
        cost_estimate=pl.CostEstimate(flops=3000000, bytes_accessed=10000000, transcendentals=0),
        name="weights",
    )(coupling.transpose(1, 0, 2))

    states = particles
    logliks = ()
    rates = cell_rate.reshape(PAIRS, LANES)
    seen = observed.reshape(STEPS, PAIRS, LANES)
    for epoch in range(EPOCHS):
        partner = from_partner(states)
        leaving = pl.pallas_call(
            functools.partial(leaving_kernel, epoch),
            out_shape=shape((1, STATES, CELLS), jnp.bfloat16),
            in_specs=[SMEM, SMEM, SMEM, HBM, HBM],
            out_specs=HBM,
            scratch_shapes=[pltpu.SemaphoreType.DMA],
            compiler_params=params(1),
            name="leaving",
        )(ancestors, migration, half, states, partner)
        arriving = from_behind(leaving)
        states, logliks = pl.pallas_call(
            functools.partial(epoch_kernel, epoch),
            out_shape=(
                shape((ROWS, STATES, CELLS), jnp.bfloat16),
                shape((EPOCHS, LANES), jnp.float32),
            ),
            in_specs=[SMEM] * 6 + [VMEM] * (8 if epoch else 7),
            out_specs=(VMEM, VMEM),
            scratch_shapes=[
                pltpu.VMEM((PAIRS, STATES * ROWS, LANES), jnp.float32),
                pltpu.VMEM((PAIRS, STATES * ROWS, LANES), jnp.bfloat16),
                pltpu.VMEM((BLOCKS, 2 * STATES * ROWS, LANES), jnp.bfloat16),
                pltpu.VMEM((LANES, 4 * LANES), jnp.bfloat16),
                pltpu.VMEM((ROWS, LANES), jnp.float32),
            ],
            compiler_params=params(12),
            name="epoch",
        )(
            ancestors,
            migration,
            half,
            pattern.T,
            current,
            temper,
            states,
            partner,
            arriving,
            weights,
            noise,
            rates,
            seen,
            *([logliks] if epoch else []),
        )
    log_weight, evidence = pl.pallas_call(
        weigh_kernel,
        out_shape=(shape((EPOCHS, ROWS), jnp.float32), shape((1, 1), jnp.float32)),
        in_specs=[VMEM, VMEM],
        out_specs=(VMEM, VMEM),
        compiler_params=params(1),
        name="weigh",
    )(logliks, from_partner(logliks))
    return (states, evidence.reshape(1), log_weight)


def solution(mesh):
    return jax.shard_map(
        on_device,
        mesh=mesh,
        in_specs=(
            P(("group", "island"), None, None),
            P(None, ("group", "island"), None),
            P(None, ("group", "island"), None),
            P("group", None),
            P("group", None, None),
            P("group"),
            P("group"),
            P("group", None),
            P(("group", "island"), None),
        ),
        out_specs=(
            P(("group", "island"), None, None),
            P(("group", "island")),
            P(None, ("group", "island")),
        ),
        check_vma=False,
    )
```

profile of v0, /device:TPU:0, one launch (start us, length us, event | category | flops | bytes accessed | tf_op | source)
XLA Modules:
  0.0 66.7 jit_solution(273290531514704081)
XLA Ops:
  0.6 0.5 collective-permute-start
  1.1 1.7 %collective-permute-done.partner = bf16[8,4,8192]{2,1,0:T(4,128)(2,1)S(1)} collective-permute-done((bf16[8,4,8192]{2,1,0:T(4,128)(2,1)}, bf16[8,4,8192]{2,1,0:T(4,128)(2,1)S(1)}, u32[]{:S(2)}, u32[]{:S(2)}) %collective-permute-start) | collective-permute-done | bytes 524320 | tf_op jit(solution)/shard_map/ppermute | solution.py:35
  2.9 0.0 copy-start.1
  2.9 1.0 %copy-done.1 = bf16[8,4,8192]{2,1,0:T(4,128)(2,1)S(1)} copy-done((bf16[8,4,8192]{2,1,0:T(4,128)(2,1)S(1)}, bf16[8,4,8192]{2,1,0:T(4,128)(2,1)}, u32[]{:S(2)}) %copy-start.1) | copy-done | bytes 524312
  3.9 0.0 copy-start.5
  3.9 0.7 %copy-done.5 = s32[2,1,8]{2,1,0:T(1,128)S(1)} copy-done((s32[2,1,8]{2,1,0:T(1,128)S(1)}, s32[2,1,8]{2,1,0:T(1,128)}, u32[]{:S(2)}) %copy-start.5) | copy-done | bytes 88
  4.6 0.0 copy-start.7
  4.6 0.7 %copy-done.7 = s32[2,1,8]{2,1,0:T(1,128)S(1)} copy-done((s32[2,1,8]{2,1,0:T(1,128)S(1)}, s32[2,1,8]{2,1,0:T(1,128)}, u32[]{:S(2)}) %copy-start.7) | copy-done | bytes 88
  5.3 0.7 %leaving.2 = bf16[1,4,8192]{2,1,0:T(4,128)(2,1)S(1)} custom-call(s32[2,1,8]{2,1,0:T(1,128)S(1)} %copy-done.5, s32[2,1,8]{2,1,0:T(1,128)S(1)} %copy-done.7, s32[1]{0:T(128)} %bitcast.half, bf16[8,4,8192]{2,1,0:T(4,128)(2,1)S(1)} %copy-done.1, bf16[8,4,8192]{2,1,0:T(4,128)(2,1)S(1)} %collective-permute-done.partner), custom_call_target="tpu_custom_call" | custom-call | tf_op jit(solution)/shard_map/leaving/pallas_call | solution.py:285
  6.0 2.9 %collective-permute-start.1 = (bf16[1,4,8192]{2,1,0:T(4,128)(2,1)S(1)}, bf16[1,4,8192]{2,1,0:T(4,128)(2,1)S(1)}, u32[]{:S(2)}, u32[]{:S(2)}) collective-permute-start(bf16[1,4,8192]{2,1,0:T(4,128)(2,1)S(1)} %leaving.2), channel_id=1, source_target_pairs={{14,0},{15,1},{0,2},{1,3},{2,4},{3,5},{4,6},{5,7},{6,8},{7,9},{8,1... | collective-permute-start | bytes 196616 | tf_op jit(solution)/shard_map/ppermute | solution.py:41
  8.9 0.9 %copy.14 = f32[1,4,64,128]{3,2,1,0:T(8,128)S(1)} copy(f32[1,4,64,128]{3,1,2,0:T(4,128)} %bitcast.17) | data formatting | bytes 262144
  9.9 0.0 copy-start
  9.9 2.5 %copy-done = bf16[128,5,4096]{2,0,1:T(8,128)(2,1)S(1)} copy-done((bf16[128,5,4096]{2,0,1:T(8,128)(2,1)S(1)}, bf16[128,5,4096]{2,0,1:T(8,128)(2,1)}, u32[]{:S(2)}) %copy-start) | copy-done | bytes 5242904
  12.4 0.0 copy-start.10
  12.4 0.0 copy-start.2
  12.4 0.0 copy-start.3
  12.4 0.0 copy-start.4
  12.4 0.0 copy-start.6
  12.4 0.0 copy-start.8
  12.4 0.0 copy-start.9
  12.4 3.5 %weights.1 = bf16[128,160,128]{2,1,0:T(8,128)(2,1)S(1)} custom-call(bf16[5,128,4096]{2,1,0:T(8,128)(2,1)S(1)} %bitcast.10), custom_call_target="tpu_custom_call" | custom-call | flops 3000000 | bytes 10000000 | tf_op jit(solution)/shard_map/weights/pallas_call | solution.py:268
  16.0 0.0 copy-done.10
  16.0 4.2 %noise.1 = f32[4,64,32,128]{3,2,1,0:T(8,128)S(1)} custom-call(s32[1,4]{1,0:T(1,128)S(1)} %copy-done.10), custom_call_target="tpu_custom_call" | custom-call | flops 30000000 | bytes 12000000 | tf_op jit(solution)/shard_map/noise/pallas_call | solution.py:259
  20.1 0.0 collective-permute-done.1.arriving
  20.2 0.0 copy-done.2
  20.2 0.0 copy-done.3
  20.2 0.0 copy-done.4
  20.2 0.0 copy-done.6
  20.2 0.0 copy-done.8
  20.2 0.0 copy-done.9
  20.2 17.1 %epoch.2 = (bf16[8,4,8192]{2,1,0:T(4,128)(2,1)S(1)}, f32[2,128]{1,0:T(2,128)S(1)}) custom-call(s32[2,1,8]{2,1,0:T(1,128)S(1)} %copy-done.6, s32[2,1,8]{2,1,0:T(1,128)S(1)} %copy-done.8, s32[1]{0:T(128)} %bitcast.half, s32[5,128]{1,0:T(8,128)S(1)} %bitcast.15, f32[4]{0:T(128)S(1)} %copy-done.9, f32[1]{0:T(128)} %bitcast.2.temper, ...), custom_call_target="tpu_custom_call" | custom-call | tf_op jit(solution)/shard_map/epoch/pallas_call | solution.py:295
  37.3 0.0 collective-permute-start.2
  37.3 1.9 %collective-permute-done.2.partner = bf16[8,4,8192]{2,1,0:T(4,128)(2,1)S(1)} collective-permute-done((bf16[8,4,8192]{2,1,0:T(4,128)(2,1)S(1)}, bf16[8,4,8192]{2,1,0:T(4,128)(2,1)S(1)}, u32[]{:S(2)}, u32[]{:S(2)}) %collective-permute-start.2) | collective-permute-done | bytes 524320 | tf_op jit(solution)/shard_map/ppermute | solution.py:35
  39.2 0.7 %leaving.3 = bf16[1,4,8192]{2,1,0:T(4,128)(2,1)S(1)} custom-call(s32[2,1,8]{2,1,0:T(1,128)S(1)} %copy-done.6, s32[2,1,8]{2,1,0:T(1,128)S(1)} %copy-done.8, s32[1]{0:T(128)} %bitcast.half, bf16[8,4,8192]{2,1,0:T(4,128)(2,1)S(1)} %get-tuple-element.9.local, bf16[8,4,8192]{2,1,0:T(4,128)(2,1)S(1)} %collective-permute-done.2.partner), custom_call_target="tpu_custom_call" | custom-call | tf_op jit(solution)/shard_map/leaving/pallas_call | solution.py:285
  39.9 1.6 %collective-permute-start.3 = (bf16[1,4,8192]{2,1,0:T(4,128)(2,1)S(1)}, bf16[1,4,8192]{2,1,0:T(4,128)(2,1)S(1)}, u32[]{:S(2)}, u32[]{:S(2)}) collective-permute-start(bf16[1,4,8192]{2,1,0:T(4,128)(2,1)S(1)} %leaving.3), channel_id=1, source_target_pairs={{14,0},{15,1},{0,2},{1,3},{2,4},{3,5},{4,6},{5,7},{6,8},{7,9},{8,1... | collective-permute-start | bytes 196616 | tf_op jit(solution)/shard_map/ppermute | solution.py:41
  41.5 5.4 %collective-permute-done.3.arriving = bf16[1,4,8192]{2,1,0:T(4,128)(2,1)S(1)} collective-permute-done((bf16[1,4,8192]{2,1,0:T(4,128)(2,1)S(1)}, bf16[1,4,8192]{2,1,0:T(4,128)(2,1)S(1)}, u32[]{:S(2)}, u32[]{:S(2)}) %collective-permute-start.3) | collective-permute-done | bytes 65568 | tf_op jit(solution)/shard_map/ppermute | solution.py:41
  46.9 17.9 %epoch.3 = (bf16[8,4,8192]{2,1,0:T(4,128)(2,1)}, f32[2,128]{1,0:T(2,128)S(1)}) custom-call(s32[2,1,8]{2,1,0:T(1,128)S(1)} %copy-done.6, s32[2,1,8]{2,1,0:T(1,128)S(1)} %copy-done.8, s32[1]{0:T(128)} %bitcast.half, s32[5,128]{1,0:T(8,128)S(1)} %bitcast.16, f32[4]{0:T(128)S(1)} %copy-done.9, f32[1]{0:T(128)} %bitcast.2.temper, ...), custom_call_target="tpu_custom_call" | custom-call | tf_op jit(solution)/shard_map/epoch/pallas_call | solution.py:295
  64.8 0.0 collective-permute-start.4
  64.8 1.1 %collective-permute-done.4.other = f32[2,128]{1,0:T(2,128)S(1)} collective-permute-done((f32[2,128]{1,0:T(2,128)S(1)}, f32[2,128]{1,0:T(2,128)S(1)}, u32[]{:S(2)}, u32[]{:S(2)}) %collective-permute-start.4) | collective-permute-done | bytes 1056 | tf_op jit(solution)/shard_map/ppermute | solution.py:35
  65.9 0.7 %weigh.1 = (f32[2,8]{1,0:T(2,128)}, f32[1,1]{1,0:T(1,128)}) custom-call(f32[2,128]{1,0:T(2,128)S(1)} %get-tuple-element.12.own, f32[2,128]{1,0:T(2,128)S(1)} %collective-permute-done.4.other), custom_call_target="tpu_custom_call" | custom-call | tf_op jit(solution)/shard_map/weigh/pallas_call | solution.py:328
Async XLA Ops:
  0.6 2.3 %collective-permute-start = (bf16[8,4,8192]{2,1,0:T(4,128)(2,1)}, bf16[8,4,8192]{2,1,0:T(4,128)(2,1)S(1)}, u32[]{:S(2)}, u32[]{:S(2)}) collective-permute-start(bf16[8,4,8192]{2,1,0:T(4,128)(2,1)} %local.3), channel_id=1, source_target_pairs={{0,1},{1,0},{2,3},{3,2},{4,5},{5,4},{6,7},{7,6},{8,9},{9,8},{10,11... | collective-permute-start | bytes 1572872 | tf_op jit(solution)/shard_map/ppermute | solution.py:35
  2.9 1.0 %copy-start.1 = (bf16[8,4,8192]{2,1,0:T(4,128)(2,1)S(1)}, bf16[8,4,8192]{2,1,0:T(4,128)(2,1)}, u32[]{:S(2)}) copy-start(bf16[8,4,8192]{2,1,0:T(4,128)(2,1)} %local.3) | copy-start | bytes 1572868
  3.9 0.7 %copy-start.5 = (s32[2,1,8]{2,1,0:T(1,128)S(1)}, s32[2,1,8]{2,1,0:T(1,128)}, u32[]{:S(2)}) copy-start(s32[2,1,8]{2,1,0:T(1,128)} %ancestors.7) | copy-start | bytes 196
  4.6 0.7 %copy-start.7 = (s32[2,1,8]{2,1,0:T(1,128)S(1)}, s32[2,1,8]{2,1,0:T(1,128)}, u32[]{:S(2)}) copy-start(s32[2,1,8]{2,1,0:T(1,128)} %migration.7) | copy-start | bytes 196
  6.0 14.2 %collective-permute-start.1 = (bf16[1,4,8192]{2,1,0:T(4,128)(2,1)S(1)}, bf16[1,4,8192]{2,1,0:T(4,128)(2,1)S(1)}, u32[]{:S(2)}, u32[]{:S(2)}) collective-permute-start(bf16[1,4,8192]{2,1,0:T(4,128)(2,1)S(1)} %leaving.2), channel_id=1, source_target_pairs={{14,0},{15,1},{0,2},{1,3},{2,4},{3,5},{4,6},{5,7},{6,8},{7,9},{8,1... | collective-permute-start | bytes 196616 | tf_op jit(solution)/shard_map/ppermute | solution.py:41
  9.9 2.5 %copy-start = (bf16[128,5,4096]{2,0,1:T(8,128)(2,1)S(1)}, bf16[128,5,4096]{2,0,1:T(8,128)(2,1)}, u32[]{:S(2)}) copy-start(bf16[128,5,4096]{2,0,1:T(8,128)(2,1)} %param.13) | copy-start | bytes 15728644
  12.4 3.6 %copy-start.10 = (s32[1,4]{1,0:T(1,128)S(1)}, s32[1,4]{1,0:T(1,128)}, u32[]{:S(2)}) copy-start(s32[1,4]{1,0:T(1,128)} %seeds.1) | copy-start | bytes 52
  12.4 7.8 %copy-start.2 = (bf16[8,4,8192]{2,1,0:T(4,128)(2,1)S(1)}, bf16[8,4,8192]{2,1,0:T(4,128)(2,1)}, u32[]{:S(2)}) copy-start(bf16[8,4,8192]{2,1,0:T(4,128)(2,1)} %local.3) | copy-start | bytes 1572868
  12.4 7.8 %copy-start.3 = (f32[8192]{0:T(1024)S(1)}, f32[8192]{0:T(1024)}, u32[]{:S(2)}) copy-start(f32[8192]{0:T(1024)} %param.14) | copy-start | bytes 98308
  12.4 7.8 %copy-start.4 = (s32[128,5]{0,1:T(8,128)S(1)}, s32[128,5]{0,1:T(8,128)}, u32[]{:S(2)}) copy-start(s32[128,5]{0,1:T(8,128)} %param.12) | copy-start | bytes 7684
  12.4 7.8 %copy-start.6 = (s32[2,1,8]{2,1,0:T(1,128)S(1)}, s32[2,1,8]{2,1,0:T(1,128)}, u32[]{:S(2)}) copy-start(s32[2,1,8]{2,1,0:T(1,128)} %ancestors.7) | copy-start | bytes 196
  12.4 7.8 %copy-start.8 = (s32[2,1,8]{2,1,0:T(1,128)S(1)}, s32[2,1,8]{2,1,0:T(1,128)}, u32[]{:S(2)}) copy-start(s32[2,1,8]{2,1,0:T(1,128)} %migration.7) | copy-start | bytes 196
  12.4 7.8 %copy-start.9 = (f32[4]{0:T(128)S(1)}, f32[4]{0:T(128)}, u32[]{:S(2)}) copy-start(f32[4]{0:T(128)} %current.3) | copy-start | bytes 52
  37.3 1.9 %collective-permute-start.2 = (bf16[8,4,8192]{2,1,0:T(4,128)(2,1)S(1)}, bf16[8,4,8192]{2,1,0:T(4,128)(2,1)S(1)}, u32[]{:S(2)}, u32[]{:S(2)}) collective-permute-start(bf16[8,4,8192]{2,1,0:T(4,128)(2,1)S(1)} %get-tuple-element.9.local), channel_id=1, source_target_pairs={{0,1},{1,0},{2,3},{3,2},{4,5},{5,4},{6,7},{7,6},{8,9},{9,8},{10,11... | collective-permute-start | bytes 1572872 | tf_op jit(solution)/shard_map/ppermute | solution.py:35
  39.9 7.0 %collective-permute-start.3 = (bf16[1,4,8192]{2,1,0:T(4,128)(2,1)S(1)}, bf16[1,4,8192]{2,1,0:T(4,128)(2,1)S(1)}, u32[]{:S(2)}, u32[]{:S(2)}) collective-permute-start(bf16[1,4,8192]{2,1,0:T(4,128)(2,1)S(1)} %leaving.3), channel_id=1, source_target_pairs={{14,0},{15,1},{0,2},{1,3},{2,4},{3,5},{4,6},{5,7},{6,8},{7,9},{8,1... | collective-permute-start | bytes 196616 | tf_op jit(solution)/shard_map/ppermute | solution.py:41
  64.8 1.1 %collective-permute-start.4 = (f32[2,128]{1,0:T(2,128)S(1)}, f32[2,128]{1,0:T(2,128)S(1)}, u32[]{:S(2)}, u32[]{:S(2)}) collective-permute-start(f32[2,128]{1,0:T(2,128)S(1)} %get-tuple-element.12.own), channel_id=1, source_target_pairs={{0,1},{1,0},{2,3},{3,2},{4,5},{5,4},{6,7},{7,6},{8,9},{9,8},{10,11... | collective-permute-start | bytes 3080 | tf_op jit(solution)/shard_map/ppermute | solution.py:35
where the time goes:
time: 66.9 us; the launch traced here: 66.7 us
  Pallas kernels  44.8 us (67%)
  waiting for transfers between devices  10.2 us (15%)
  local copies, waits for them, and re-layouts  5.83 us (9%)
  starting transfers between devices  5.04 us (8%)
  between operations  0.82 us (1%)
    pallas_call x2, Pallas kernels, on_device(): pl.pallas_call(functools.partial(epoch_kernel, epoch), out_shape=(shape((...  35 us
    unnamed x23, local copies, waits for them, and re-layouts  5.83 us
    ppermute x2, waiting for transfers between devices, from_behind(): return lax.ppermute(block, 'island', route)  5.45 us
    ppermute x3, waiting for transfers between devices, from_partner(): return lax.ppermute(value, 'island', pairs)  4.78 us
    ppermute x2, starting transfers between devices, from_behind(): return lax.ppermute(block, 'island', route)  4.51 us
    pallas_call x1, Pallas kernels, on_device(): pl.pallas_call(noise_kernel, out_shape=shape((STEPS, PAIRS, STATES * ROWS...  4.17 us
    pallas_call x1, Pallas kernels, on_device(): pl.pallas_call(weights_kernel, out_shape=shape((BLOCKS, NEIGH * HALF, LAN...  3.54 us
    pallas_call x2, Pallas kernels, on_device(): pl.pallas_call(functools.partial(leaving_kernel, epoch), out_shape=shape(...  1.35 us
  transfers between devices with their start and end apart: 5, of which 4 were waited for; matrix products, arithmetic and copies ran while one was open for 1% of the time, Pallas kernels for 12%

commit v1 on v0

--- a/solution.py
+++ b/solution.py
@@ -17,6 +17,7 @@
 BLOCKS = 128
 ROWS = 8
 LANES = 128
+GROUP = 16
 PAIRS = CELLS // LANES
 HALF = BLOCK // 2
 NOISE_SCALE = 0.3 * 2.449489742783178 / 16777216.0
@@ -100,6 +101,29 @@
         copy = pltpu.make_async_copy(partner.at[pl.ds(slot, 1)], out, sem)
         copy.start()
         copy.wait()
+
+
+def members(g):
+    return [g * GROUP + i for i in range(GROUP)]
+
+
+def in_turn(*stages):
+    count = PAIRS // GROUP
+    depth = len(stages)
+
+    def one(at, low, high):
+        for s in reversed(range(low, high)):
+            stages[s](at - s)
+
+    def steady(at, carry):
+        one(at, 0, depth)
+        return carry
+
+    for at in range(depth - 1):
+        one(at, 0, at + 1)
+    lax.fori_loop(depth - 1, count, steady, 0)
+    for at in range(count, count + depth - 1):
+        one(at, at - count + 1, depth)
 
 
 def epoch_kernel(
@@ -120,9 +144,8 @@
     *rest,
 ):
     if epoch:
-        before, states, logliks, gather, natural, spread, unmix, total = rest
-    else:
-        states, logliks, gather, natural, spread, unmix, total = rest
+        before, *rest = rest
+    states, logliks, gather, natural, spread, spread_next, coupled, unmix, total = rest
     lane = lax.broadcasted_iota(jnp.int32, (1, LANES), 1)
 
     source = lax.broadcasted_iota(jnp.int32, (LANES, 4 * LANES), 0)
@@ -136,41 +159,38 @@
         chosen = ancestors[epoch, 0, j]
         picks.append((chosen % ROWS, chosen // ROWS == half[0], migration[epoch, 0, 0] == j))
 
-    def assemble(q, carry):
-        lanes = pl.ds(pl.multiple_of(q * LANES, LANES), LANES)
-        for j, (slot, is_local, is_new) in enumerate(picks):
-            kept = jnp.where(
-                is_local, local[slot, :, lanes].astype(jnp.float32), partner[slot, :, lanes].astype(jnp.float32)
-            )
-            gather[q, j * STATES : (j + 1) * STATES, :] = jnp.where(
-                is_new, arriving[0, :, lanes].astype(jnp.float32), kept
-            )
-        for c in range(0, STATES, 2):
-            two = [gather[q, pl.ds(c + d, ROWS, stride=STATES), :] for d in range(2)]
-            natural[q, c * ROWS : (c + 2) * ROWS, :] = jnp.concatenate(two, axis=0).astype(jnp.bfloat16)
-        return carry
-
-    lax.fori_loop(0, PAIRS, assemble, 0, unroll=4)
-
     rows = STATES * ROWS
-
-    def spread_out():
-        chunk = 8
-
-        def one(g, carry):
-            cells = natural[pl.ds(g * chunk, chunk)].reshape(chunk * rows, LANES)
-            placed = jnp.dot(cells, unmix[...], preferred_element_type=jnp.float32).astype(jnp.bfloat16)
-            for q in range(chunk):
-                for tile in range(4):
-                    spread[
-                        2 * (g * chunk + q) + tile // 2, (tile % 2) * rows : (tile % 2 + 1) * rows, :
-                    ] = placed[q * rows : (q + 1) * rows, tile * LANES : (tile + 1) * LANES]
-            return carry
-
-        lax.fori_loop(0, PAIRS // chunk, one, 0)
-
-    def product(b):
-        pieces = [spread[pattern[k, b]] for k in range(NEIGH)]
+    total[...] = jnp.zeros_like(total)
+
+    def assemble(g):
+        for q in members(g):
+            lanes = pl.ds(pl.multiple_of(q * LANES, LANES), LANES)
+            for j, (slot, is_local, is_new) in enumerate(picks):
+                kept = jnp.where(
+                    is_local,
+                    local[slot, :, lanes].astype(jnp.float32),
+                    partner[slot, :, lanes].astype(jnp.float32),
+                )
+                gather[q, j * STATES : (j + 1) * STATES, :] = jnp.where(
+                    is_new, arriving[0, :, lanes].astype(jnp.float32), kept
+                )
+            for c in range(0, STATES, 2):
+                two = [gather[q, pl.ds(c + d, ROWS, stride=STATES), :] for d in range(2)]
+                natural[q, c * ROWS : (c + 2) * ROWS, :] = jnp.concatenate(two, axis=0).astype(
+                    jnp.bfloat16
+                )
+
+    def spread_out(result, g):
+        cells = natural[pl.ds(g * GROUP, GROUP)].reshape(GROUP * rows, LANES)
+        placed = jnp.dot(cells, unmix[...], preferred_element_type=jnp.float32).astype(jnp.bfloat16)
+        for i, q in enumerate(members(g)):
+            for tile in range(4):
+                result[2 * q + tile // 2, (tile % 2) * rows : (tile % 2 + 1) * rows, :] = placed[
+                    i * rows : (i + 1) * rows, tile * LANES : (tile + 1) * LANES
+                ]
+
+    def product(held, b):
+        pieces = [held[pattern[k, b]] for k in range(NEIGH)]
         first = jnp.where(
             lane < HALF,
             pieces[0],
@@ -179,20 +199,19 @@
         both = jnp.concatenate([first, pieces[4][:, :HALF]], axis=1)
         return jnp.dot(both, weights[b], preferred_element_type=jnp.float32)
 
-    for inner in range(STEPS_EPOCH):
-        step = epoch * STEPS_EPOCH + inner
-        last = inner == STEPS_EPOCH - 1
-        now = current[step]
-        spread_out()
-        total[...] = jnp.zeros_like(total) if inner == 0 else total[...]
-
-        def one(q, carry):
-            left = product(2 * q)
-            right = product(2 * q + 1)
+    def couple(held, g):
+        for i, q in enumerate(members(g)):
+            left = product(held, 2 * q)
+            right = product(held, 2 * q + 1)
             inside = jnp.where(lane < BLOCK, left[:rows], right[rows:])
             across = jnp.where(lane < BLOCK, right[:rows], left[rows:])
-            coupled = inside + pltpu.roll(across, BLOCK, 1)
-            mixed = 0.6 * natural[q].astype(jnp.float32) + 0.8 * coupled
+            coupled[i] = inside + pltpu.roll(across, BLOCK, 1)
+
+    def propagate(step, g):
+        now = current[step]
+        gained = jnp.zeros((ROWS, LANES), jnp.float32)
+        for i, q in enumerate(members(g)):
+            mixed = 0.6 * natural[q].astype(jnp.float32) + 0.8 * coupled[i]
             drawn = noise[step, q]
             charge, over, heat, film = (mixed[c * ROWS : (c + 1) * ROWS] for c in range(STATES))
             rate = cell_rate[pl.ds(q, 1), :]
@@ -210,23 +229,29 @@
                 0.5 + 0.5 * jnp.tanh(0.5 * new_charge) - 0.4 * jnp.tanh(new_over) - (0.2 * now) * new_film
             )
             misfit = seen - predicted
+            gained += misfit * misfit
             fresh = (new_charge, new_over, new_heat, new_film)
-            if last:
+            if step % STEPS_EPOCH == STEPS_EPOCH - 1:
                 for c in range(STATES):
                     gather[q, pl.ds(c, ROWS, stride=STATES), :] = fresh[c]
             else:
                 natural[q] = jnp.concatenate(fresh, axis=0).astype(jnp.bfloat16)
-            return carry + misfit * misfit
-
-        total[...] += lax.fori_loop(0, PAIRS, one, jnp.zeros((ROWS, LANES), jnp.float32), unroll=4)
-
-    def finish(q, carry):
-        lanes = pl.ds(pl.multiple_of(q * LANES, LANES), LANES)
-        for j in range(ROWS):
-            states[j, :, lanes] = gather[q, j * STATES : (j + 1) * STATES, :].astype(jnp.bfloat16)
-        return carry
-
-    lax.fori_loop(0, PAIRS, finish, 0, unroll=4)
+        total[...] += gained
+
+    def finish(g):
+        for q in members(g):
+            lanes = pl.ds(pl.multiple_of(q * LANES, LANES), LANES)
+            for j in range(ROWS):
+                states[j, :, lanes] = gather[q, j * STATES : (j + 1) * STATES, :].astype(jnp.bfloat16)
+
+    step = epoch * STEPS_EPOCH
+    in_turn(assemble, functools.partial(spread_out, spread))
+    in_turn(
+        functools.partial(couple, spread),
+        functools.partial(propagate, step),
+        functools.partial(spread_out, spread_next),
+    )
+    in_turn(functools.partial(couple, spread_next), functools.partial(propagate, step + 1), finish)
 
     column = -0.5 * temper[0] * jnp.sum(total[...], axis=1, keepdims=True)
     slots = lax.broadcasted_iota(jnp.int32, (ROWS, LANES), 0)
@@ -304,6 +329,8 @@
                 pltpu.VMEM((PAIRS, STATES * ROWS, LANES), jnp.float32),
                 pltpu.VMEM((PAIRS, STATES * ROWS, LANES), jnp.bfloat16),
                 pltpu.VMEM((BLOCKS, 2 * STATES * ROWS, LANES), jnp.bfloat16),
+                pltpu.VMEM((BLOCKS, 2 * STATES * ROWS, LANES), jnp.bfloat16),
+                pltpu.VMEM((GROUP, STATES * ROWS, LANES), jnp.float32),
                 pltpu.VMEM((LANES, 4 * LANES), jnp.bfloat16),
                 pltpu.VMEM((ROWS, LANES), jnp.float32),
             ],

time: 66.9 us -> 48.9 us (0.73)
  Pallas kernels: 44.8 us -> 26.7 us
    pallas_call x2, Pallas kernels: 35 us -> 16.9 us  [on_device(): pl.pallas_call(functools.partial(epoch_kernel, epoch), out_shape=(shape((...]
  transfers between devices with their start and end apart: 5 -> 5, of which waited for: 4 -> 4; matrix products, arithmetic and copies ran while one was open for 1% -> 2% of each run, Pallas kernels for 12% -> 16%
where the time goes in v1:
time: 48.9 us; the launch traced here: 48.6 us
  Pallas kernels  26.7 us (55%)
  waiting for transfers between devices  10.2 us (21%)
  local copies, waits for them, and re-layouts  5.83 us (12%)
  starting transfers between devices  5.03 us (10%)
  between operations  0.82 us (2%)
    pallas_call x2, Pallas kernels, on_device(): pl.pallas_call(functools.partial(epoch_kernel, epoch), out_shape=(shape((...  16.9 us
    unnamed x23, local copies, waits for them, and re-layouts  5.83 us
    ppermute x2, waiting for transfers between devices, from_behind(): return lax.ppermute(block, 'island', route)  5.45 us
    ppermute x3, waiting for transfers between devices, from_partner(): return lax.ppermute(value, 'island', pairs)  4.79 us
    ppermute x2, starting transfers between devices, from_behind(): return lax.ppermute(block, 'island', route)  4.51 us
    pallas_call x1, Pallas kernels, on_device(): pl.pallas_call(noise_kernel, out_shape=shape((STEPS, PAIRS, STATES * ROWS...  4.17 us
    pallas_call x1, Pallas kernels, on_device(): pl.pallas_call(weights_kernel, out_shape=shape((BLOCKS, NEIGH * HALF, LAN...  3.54 us
    pallas_call x2, Pallas kernels, on_device(): pl.pallas_call(functools.partial(leaving_kernel, epoch), out_shape=shape(...  1.35 us
  transfers between devices with their start and end apart: 5, of which 4 were waited for; matrix products, arithmetic and copies ran while one was open for 2% of the time, Pallas kernels for 16%

profile of v1, /device:TPU:0, one launch (start us, length us, event | category | flops | bytes accessed | tf_op | source)
XLA Modules:
  0.0 48.6 jit_solution(13202544103424234729)
XLA Ops:
  0.6 0.5 %collective-permute-start = (bf16[8,4,8192]{2,1,0:T(4,128)(2,1)}, bf16[8,4,8192]{2,1,0:T(4,128)(2,1)S(1)}, u32[]{:S(2)}, u32[]{:S(2)}) collective-permute-start(bf16[8,4,8192]{2,1,0:T(4,128)(2,1)} %local.3), channel_id=1, source_target_pairs={{0,1},{1,0},{2,3},{3,2},{4,5},{5,4},{6,7},{7,6},{8,9},{9,8},{10,11... | collective-permute-start | bytes 1572872 | tf_op jit(solution)/shard_map/ppermute | solution.py:36
  1.1 1.7 %collective-permute-done.partner = bf16[8,4,8192]{2,1,0:T(4,128)(2,1)S(1)} collective-permute-done((bf16[8,4,8192]{2,1,0:T(4,128)(2,1)}, bf16[8,4,8192]{2,1,0:T(4,128)(2,1)S(1)}, u32[]{:S(2)}, u32[]{:S(2)}) %collective-permute-start) | collective-permute-done | bytes 524320 | tf_op jit(solution)/shard_map/ppermute | solution.py:36
  2.9 0.0 copy-start.1
  2.9 1.0 %copy-done.1 = bf16[8,4,8192]{2,1,0:T(4,128)(2,1)S(1)} copy-done((bf16[8,4,8192]{2,1,0:T(4,128)(2,1)S(1)}, bf16[8,4,8192]{2,1,0:T(4,128)(2,1)}, u32[]{:S(2)}) %copy-start.1) | copy-done | bytes 524312
  3.9 0.0 copy-start.5
  3.9 0.7 %copy-done.5 = s32[2,1,8]{2,1,0:T(1,128)S(1)} copy-done((s32[2,1,8]{2,1,0:T(1,128)S(1)}, s32[2,1,8]{2,1,0:T(1,128)}, u32[]{:S(2)}) %copy-start.5) | copy-done | bytes 88
  4.6 0.0 copy-start.7
  4.6 0.7 %copy-done.7 = s32[2,1,8]{2,1,0:T(1,128)S(1)} copy-done((s32[2,1,8]{2,1,0:T(1,128)S(1)}, s32[2,1,8]{2,1,0:T(1,128)}, u32[]{:S(2)}) %copy-start.7) | copy-done | bytes 88
  5.3 0.7 %leaving.2 = bf16[1,4,8192]{2,1,0:T(4,128)(2,1)S(1)} custom-call(s32[2,1,8]{2,1,0:T(1,128)S(1)} %copy-done.5, s32[2,1,8]{2,1,0:T(1,128)S(1)} %copy-done.7, s32[1]{0:T(128)} %bitcast.half, bf16[8,4,8192]{2,1,0:T(4,128)(2,1)S(1)} %copy-done.1, bf16[8,4,8192]{2,1,0:T(4,128)(2,1)S(1)} %collective-permute-done.partner), custom_call_target="tpu_custom_call" | custom-call | tf_op jit(solution)/shard_map/leaving/pallas_call | solution.py:310
  6.0 2.9 %collective-permute-start.1 = (bf16[1,4,8192]{2,1,0:T(4,128)(2,1)S(1)}, bf16[1,4,8192]{2,1,0:T(4,128)(2,1)S(1)}, u32[]{:S(2)}, u32[]{:S(2)}) collective-permute-start(bf16[1,4,8192]{2,1,0:T(4,128)(2,1)S(1)} %leaving.2), channel_id=1, source_target_pairs={{14,0},{15,1},{0,2},{1,3},{2,4},{3,5},{4,6},{5,7},{6,8},{7,9},{8,1... | collective-permute-start | bytes 196616 | tf_op jit(solution)/shard_map/ppermute | solution.py:42
  8.9 0.9 %copy.14 = f32[1,4,64,128]{3,2,1,0:T(8,128)S(1)} copy(f32[1,4,64,128]{3,1,2,0:T(4,128)} %bitcast.17) | data formatting | bytes 262144
  9.9 0.0 copy-start
  9.9 2.5 %copy-done = bf16[128,5,4096]{2,0,1:T(8,128)(2,1)S(1)} copy-done((bf16[128,5,4096]{2,0,1:T(8,128)(2,1)S(1)}, bf16[128,5,4096]{2,0,1:T(8,128)(2,1)}, u32[]{:S(2)}) %copy-start) | copy-done | bytes 5242904
  12.4 0.0 copy-start.10
  12.4 0.0 copy-start.2
  12.4 0.0 copy-start.3
  12.4 0.0 copy-start.4
  12.4 0.0 copy-start.6
  12.4 0.0 copy-start.8
  12.4 0.0 copy-start.9
  12.4 3.5 %weights.1 = bf16[128,160,128]{2,1,0:T(8,128)(2,1)S(1)} custom-call(bf16[5,128,4096]{2,1,0:T(8,128)(2,1)S(1)} %bitcast.10), custom_call_target="tpu_custom_call" | custom-call | flops 3000000 | bytes 10000000 | tf_op jit(solution)/shard_map/weights/pallas_call | solution.py:293
  16.0 0.0 copy-done.10
  16.0 4.2 %noise.1 = f32[4,64,32,128]{3,2,1,0:T(8,128)S(1)} custom-call(s32[1,4]{1,0:T(1,128)S(1)} %copy-done.10), custom_call_target="tpu_custom_call" | custom-call | flops 30000000 | bytes 12000000 | tf_op jit(solution)/shard_map/noise/pallas_call | solution.py:284
  20.1 0.0 collective-permute-done.1.arriving
  20.2 0.0 copy-done.2
  20.2 0.0 copy-done.3
  20.2 0.0 copy-done.4
  20.2 0.0 copy-done.6
  20.2 0.0 copy-done.8
  20.2 0.0 copy-done.9
  20.2 8.1 %epoch.2 = (bf16[8,4,8192]{2,1,0:T(4,128)(2,1)S(1)}, f32[2,128]{1,0:T(2,128)S(1)}) custom-call(s32[2,1,8]{2,1,0:T(1,128)S(1)} %copy-done.6, s32[2,1,8]{2,1,0:T(1,128)S(1)} %copy-done.8, s32[1]{0:T(128)} %bitcast.half, s32[5,128]{1,0:T(8,128)S(1)} %bitcast.15, f32[4]{0:T(128)S(1)} %copy-done.9, f32[1]{0:T(128)} %bitcast.2.temper, ...), custom_call_target="tpu_custom_call" | custom-call | tf_op jit(solution)/shard_map/epoch/pallas_call | solution.py:320
  28.3 0.0 collective-permute-start.2
  28.3 1.9 %collective-permute-done.2.partner = bf16[8,4,8192]{2,1,0:T(4,128)(2,1)S(1)} collective-permute-done((bf16[8,4,8192]{2,1,0:T(4,128)(2,1)S(1)}, bf16[8,4,8192]{2,1,0:T(4,128)(2,1)S(1)}, u32[]{:S(2)}, u32[]{:S(2)}) %collective-permute-start.2) | collective-permute-done | bytes 524320 | tf_op jit(solution)/shard_map/ppermute | solution.py:36
  30.2 0.7 %leaving.3 = bf16[1,4,8192]{2,1,0:T(4,128)(2,1)S(1)} custom-call(s32[2,1,8]{2,1,0:T(1,128)S(1)} %copy-done.6, s32[2,1,8]{2,1,0:T(1,128)S(1)} %copy-done.8, s32[1]{0:T(128)} %bitcast.half, bf16[8,4,8192]{2,1,0:T(4,128)(2,1)S(1)} %get-tuple-element.9.local, bf16[8,4,8192]{2,1,0:T(4,128)(2,1)S(1)} %collective-permute-done.2.partner), custom_call_target="tpu_custom_call" | custom-call | tf_op jit(solution)/shard_map/leaving/pallas_call | solution.py:310
  30.9 1.6 %collective-permute-start.3 = (bf16[1,4,8192]{2,1,0:T(4,128)(2,1)S(1)}, bf16[1,4,8192]{2,1,0:T(4,128)(2,1)S(1)}, u32[]{:S(2)}, u32[]{:S(2)}) collective-permute-start(bf16[1,4,8192]{2,1,0:T(4,128)(2,1)S(1)} %leaving.3), channel_id=1, source_target_pairs={{14,0},{15,1},{0,2},{1,3},{2,4},{3,5},{4,6},{5,7},{6,8},{7,9},{8,1... | collective-permute-start | bytes 196616 | tf_op jit(solution)/shard_map/ppermute | solution.py:42
  32.5 5.4 %collective-permute-done.3.arriving = bf16[1,4,8192]{2,1,0:T(4,128)(2,1)S(1)} collective-permute-done((bf16[1,4,8192]{2,1,0:T(4,128)(2,1)S(1)}, bf16[1,4,8192]{2,1,0:T(4,128)(2,1)S(1)}, u32[]{:S(2)}, u32[]{:S(2)}) %collective-permute-start.3) | collective-permute-done | bytes 65568 | tf_op jit(solution)/shard_map/ppermute | solution.py:42
  37.9 8.8 %epoch.3 = (bf16[8,4,8192]{2,1,0:T(4,128)(2,1)}, f32[2,128]{1,0:T(2,128)S(1)}) custom-call(s32[2,1,8]{2,1,0:T(1,128)S(1)} %copy-done.6, s32[2,1,8]{2,1,0:T(1,128)S(1)} %copy-done.8, s32[1]{0:T(128)} %bitcast.half, s32[5,128]{1,0:T(8,128)S(1)} %bitcast.16, f32[4]{0:T(128)S(1)} %copy-done.9, f32[1]{0:T(128)} %bitcast.2.temper, ...), custom_call_target="tpu_custom_call" | custom-call | tf_op jit(solution)/shard_map/epoch/pallas_call | solution.py:320
  46.8 0.0 collective-permute-start.4
  46.8 1.1 %collective-permute-done.4.other = f32[2,128]{1,0:T(2,128)S(1)} collective-permute-done((f32[2,128]{1,0:T(2,128)S(1)}, f32[2,128]{1,0:T(2,128)S(1)}, u32[]{:S(2)}, u32[]{:S(2)}) %collective-permute-start.4) | collective-permute-done | bytes 1056 | tf_op jit(solution)/shard_map/ppermute | solution.py:36
  47.9 0.7 %weigh.1 = (f32[2,8]{1,0:T(2,128)}, f32[1,1]{1,0:T(1,128)}) custom-call(f32[2,128]{1,0:T(2,128)S(1)} %get-tuple-element.12.own, f32[2,128]{1,0:T(2,128)S(1)} %collective-permute-done.4.other), custom_call_target="tpu_custom_call" | custom-call | tf_op jit(solution)/shard_map/weigh/pallas_call | solution.py:355
Async XLA Ops:
  0.6 2.3 %collective-permute-start = (bf16[8,4,8192]{2,1,0:T(4,128)(2,1)}, bf16[8,4,8192]{2,1,0:T(4,128)(2,1)S(1)}, u32[]{:S(2)}, u32[]{:S(2)}) collective-permute-start(bf16[8,4,8192]{2,1,0:T(4,128)(2,1)} %local.3), channel_id=1, source_target_pairs={{0,1},{1,0},{2,3},{3,2},{4,5},{5,4},{6,7},{7,6},{8,9},{9,8},{10,11... | collective-permute-start | bytes 1572872 | tf_op jit(solution)/shard_map/ppermute | solution.py:36
  2.9 1.0 %copy-start.1 = (bf16[8,4,8192]{2,1,0:T(4,128)(2,1)S(1)}, bf16[8,4,8192]{2,1,0:T(4,128)(2,1)}, u32[]{:S(2)}) copy-start(bf16[8,4,8192]{2,1,0:T(4,128)(2,1)} %local.3) | copy-start | bytes 1572868
  3.9 0.7 %copy-start.5 = (s32[2,1,8]{2,1,0:T(1,128)S(1)}, s32[2,1,8]{2,1,0:T(1,128)}, u32[]{:S(2)}) copy-start(s32[2,1,8]{2,1,0:T(1,128)} %ancestors.7) | copy-start | bytes 196
  4.6 0.7 %copy-start.7 = (s32[2,1,8]{2,1,0:T(1,128)S(1)}, s32[2,1,8]{2,1,0:T(1,128)}, u32[]{:S(2)}) copy-start(s32[2,1,8]{2,1,0:T(1,128)} %migration.7) | copy-start | bytes 196
  6.0 14.2 %collective-permute-start.1 = (bf16[1,4,8192]{2,1,0:T(4,128)(2,1)S(1)}, bf16[1,4,8192]{2,1,0:T(4,128)(2,1)S(1)}, u32[]{:S(2)}, u32[]{:S(2)}) collective-permute-start(bf16[1,4,8192]{2,1,0:T(4,128)(2,1)S(1)} %leaving.2), channel_id=1, source_target_pairs={{14,0},{15,1},{0,2},{1,3},{2,4},{3,5},{4,6},{5,7},{6,8},{7,9},{8,1... | collective-permute-start | bytes 196616 | tf_op jit(solution)/shard_map/ppermute | solution.py:42
  9.9 2.5 %copy-start = (bf16[128,5,4096]{2,0,1:T(8,128)(2,1)S(1)}, bf16[128,5,4096]{2,0,1:T(8,128)(2,1)}, u32[]{:S(2)}) copy-start(bf16[128,5,4096]{2,0,1:T(8,128)(2,1)} %param.13) | copy-start | bytes 15728644
  12.4 3.6 %copy-start.10 = (s32[1,4]{1,0:T(1,128)S(1)}, s32[1,4]{1,0:T(1,128)}, u32[]{:S(2)}) copy-start(s32[1,4]{1,0:T(1,128)} %seeds.1) | copy-start | bytes 52
  12.4 7.8 %copy-start.2 = (bf16[8,4,8192]{2,1,0:T(4,128)(2,1)S(1)}, bf16[8,4,8192]{2,1,0:T(4,128)(2,1)}, u32[]{:S(2)}) copy-start(bf16[8,4,8192]{2,1,0:T(4,128)(2,1)} %local.3) | copy-start | bytes 1572868
  12.4 7.8 %copy-start.3 = (f32[8192]{0:T(1024)S(1)}, f32[8192]{0:T(1024)}, u32[]{:S(2)}) copy-start(f32[8192]{0:T(1024)} %param.14) | copy-start | bytes 98308
  12.4 7.8 %copy-start.4 = (s32[128,5]{0,1:T(8,128)S(1)}, s32[128,5]{0,1:T(8,128)}, u32[]{:S(2)}) copy-start(s32[128,5]{0,1:T(8,128)} %param.12) | copy-start | bytes 7684
  12.4 7.8 %copy-start.6 = (s32[2,1,8]{2,1,0:T(1,128)S(1)}, s32[2,1,8]{2,1,0:T(1,128)}, u32[]{:S(2)}) copy-start(s32[2,1,8]{2,1,0:T(1,128)} %ancestors.7) | copy-start | bytes 196
  12.4 7.8 %copy-start.8 = (s32[2,1,8]{2,1,0:T(1,128)S(1)}, s32[2,1,8]{2,1,0:T(1,128)}, u32[]{:S(2)}) copy-start(s32[2,1,8]{2,1,0:T(1,128)} %migration.7) | copy-start | bytes 196
  12.4 7.8 %copy-start.9 = (f32[4]{0:T(128)S(1)}, f32[4]{0:T(128)}, u32[]{:S(2)}) copy-start(f32[4]{0:T(128)} %current.3) | copy-start | bytes 52
  28.3 1.9 %collective-permute-start.2 = (bf16[8,4,8192]{2,1,0:T(4,128)(2,1)S(1)}, bf16[8,4,8192]{2,1,0:T(4,128)(2,1)S(1)}, u32[]{:S(2)}, u32[]{:S(2)}) collective-permute-start(bf16[8,4,8192]{2,1,0:T(4,128)(2,1)S(1)} %get-tuple-element.9.local), channel_id=1, source_target_pairs={{0,1},{1,0},{2,3},{3,2},{4,5},{5,4},{6,7},{7,6},{8,9},{9,8},{10,11... | collective-permute-start | bytes 1572872 | tf_op jit(solution)/shard_map/ppermute | solution.py:36
  30.9 7.0 %collective-permute-start.3 = (bf16[1,4,8192]{2,1,0:T(4,128)(2,1)S(1)}, bf16[1,4,8192]{2,1,0:T(4,128)(2,1)S(1)}, u32[]{:S(2)}, u32[]{:S(2)}) collective-permute-start(bf16[1,4,8192]{2,1,0:T(4,128)(2,1)S(1)} %leaving.3), channel_id=1, source_target_pairs={{14,0},{15,1},{0,2},{1,3},{2,4},{3,5},{4,6},{5,7},{6,8},{7,9},{8,1... | collective-permute-start | bytes 196616 | tf_op jit(solution)/shard_map/ppermute | solution.py:42
  46.8 1.1 %collective-permute-start.4 = (f32[2,128]{1,0:T(2,128)S(1)}, f32[2,128]{1,0:T(2,128)S(1)}, u32[]{:S(2)}, u32[]{:S(2)}) collective-permute-start(f32[2,128]{1,0:T(2,128)S(1)} %get-tuple-element.12.own), channel_id=1, source_target_pairs={{0,1},{1,0},{2,3},{3,2},{4,5},{5,4},{6,7},{7,6},{8,9},{9,8},{10,11... | collective-permute-start | bytes 3080 | tf_op jit(solution)/shard_map/ppermute | solution.py:36

commit v2 on v1

--- a/solution.py
+++ b/solution.py
@@ -27,6 +27,10 @@
 HBM = pl.BlockSpec(memory_space=pl.ANY)
 
 
+def in_hbm(array):
+    return pltpu.with_memory_space_constraint(array, pltpu.HBM)
+
+
 def params(mib):
     return pltpu.CompilerParams(vmem_limit_bytes=mib << 20)
 
@@ -52,12 +56,12 @@
     return shifted(hashed) & 16777215
 
 
-def noise_kernel(seeds, out):
+def noise_kernel(epoch, seeds, out):
     row = lax.broadcasted_iota(jnp.int32, (STATES * ROWS, LANES), 0)
     lane = lax.broadcasted_iota(jnp.int32, (STATES * ROWS, LANES), 1)
     counter = 2 * (((row % ROWS) * STATES + row // ROWS) * CELLS + lane)
-    for step in range(STEPS):
-        start = counter + seeds[0, step] * 40503
+    for step in range(STEPS_EPOCH):
+        start = counter + seeds[0, epoch * STEPS_EPOCH + step] * 40503
 
         def one(q, carry):
             anchor = start + q * (2 * LANES)
@@ -68,13 +72,21 @@
         lax.fori_loop(0, PAIRS, one, 0, unroll=4)
 
 
-def weights_kernel(coupling, out, wide):
+def weights_kernel(coupling, out, held, wide, sems):
     group = 16
 
+    def fetch(g):
+        rows = pl.ds(pl.multiple_of(g * group, group), group)
+        return pltpu.make_async_copy(coupling.at[:, rows], held.at[:, rows], sems.at[g])
+
+    for g in range(BLOCKS // group):
+        fetch(g).start()
+
     def one(g, carry):
+        fetch(g).wait()
         for k in range(NEIGH):
             for r in range(HALF):
-                wide[k, r * group : (r + 1) * group, :] = coupling[
+                wide[k, r * group : (r + 1) * group, :] = held[
                     k, pl.ds(pl.multiple_of(g * group, group), group), r * LANES : (r + 1) * LANES
                 ].astype(jnp.float32)
             for b in range(group):
@@ -150,8 +162,7 @@
 
     source = lax.broadcasted_iota(jnp.int32, (LANES, 4 * LANES), 0)
     target = lax.broadcasted_iota(jnp.int32, (LANES, 4 * LANES), 1)
-    tile = target // LANES
-    wanted = (tile // 2) * BLOCK + (target % HALF) * 2 + tile % 2
+    wanted = (target >> 8) * BLOCK + (target & (HALF - 1)) * 2 + ((target >> 7) & 1)
     unmix[...] = jnp.where(source == wanted, 1.0, 0.0).astype(jnp.bfloat16)
 
     picks = []
@@ -212,10 +223,10 @@
         gained = jnp.zeros((ROWS, LANES), jnp.float32)
         for i, q in enumerate(members(g)):
             mixed = 0.6 * natural[q].astype(jnp.float32) + 0.8 * coupled[i]
-            drawn = noise[step, q]
+            drawn = noise[step % STEPS_EPOCH, q]
             charge, over, heat, film = (mixed[c * ROWS : (c + 1) * ROWS] for c in range(STATES))
             rate = cell_rate[pl.ds(q, 1), :]
-            seen = observed[step, pl.ds(q, 1), :]
+            seen = observed[step : step + 1, pl.ds(pl.multiple_of(q * LANES, LANES), LANES)]
             tanh_over = jnp.tanh(over)
             fade = jnp.exp(-0.5 * jnp.abs(charge))
             warm = 0.6 * jnp.tanh(heat)
@@ -281,32 +292,37 @@
     temper = (0.25 * jnp.power(2.0, (position // 2 % 4).astype(jnp.float32)))[None]
     shape = jax.ShapeDtypeStruct
 
-    noise = pl.pallas_call(
-        noise_kernel,
-        out_shape=shape((STEPS, PAIRS, STATES * ROWS, LANES), jnp.float32),
-        in_specs=[SMEM],
-        out_specs=VMEM,
-        compiler_params=params(2),
-        cost_estimate=pl.CostEstimate(flops=30000000, bytes_accessed=12000000, transcendentals=0),
-        name="noise",
-    )(noise_seeds)
     weights = pl.pallas_call(
         weights_kernel,
         out_shape=shape((BLOCKS, NEIGH * HALF, LANES), jnp.bfloat16),
-        in_specs=[VMEM],
+        in_specs=[HBM],
         out_specs=VMEM,
-        scratch_shapes=[pltpu.VMEM((NEIGH, HALF * 16, LANES), jnp.float32)],
-        compiler_params=params(4),
+        scratch_shapes=[
+            pltpu.VMEM((NEIGH, BLOCKS, BLOCK * BLOCK), jnp.bfloat16),
+            pltpu.VMEM((NEIGH, HALF * 16, LANES), jnp.float32),
+            pltpu.SemaphoreType.DMA((BLOCKS // 16,)),
+        ],
+        compiler_params=params(10),
         cost_estimate=pl.CostEstimate(flops=3000000, bytes_accessed=10000000, transcendentals=0),
         name="weights",
-    )(coupling.transpose(1, 0, 2))
-
+    )(in_hbm(coupling.transpose(1, 0, 2)))
+
+    ancestors, migration = in_hbm(ancestors), in_hbm(migration)
     states = particles
     logliks = ()
     rates = cell_rate.reshape(PAIRS, LANES)
-    seen = observed.reshape(STEPS, PAIRS, LANES)
     for epoch in range(EPOCHS):
         partner = from_partner(states)
+        noise = pl.pallas_call(
+            functools.partial(noise_kernel, epoch),
+            out_shape=shape((STEPS_EPOCH, PAIRS, STATES * ROWS, LANES), jnp.float32),
+            in_specs=[SMEM],
+            out_specs=VMEM,
+            compiler_params=params(2),
+            cost_estimate=pl.CostEstimate(flops=15000000, bytes_accessed=6000000, transcendentals=0),
+            name="noise",
+        )(in_hbm(noise_seeds))
+        partner, noise = lax.optimization_barrier((partner, noise))
         leaving = pl.pallas_call(
             functools.partial(leaving_kernel, epoch),
             out_shape=shape((1, STATES, CELLS), jnp.bfloat16),
@@ -315,7 +331,7 @@
             scratch_shapes=[pltpu.SemaphoreType.DMA],
             compiler_params=params(1),
             name="leaving",
-        )(ancestors, migration, half, states, partner)
+        )(ancestors, migration, half, states if epoch else in_hbm(states), partner)
         arriving = from_behind(leaving)
         states, logliks = pl.pallas_call(
             functools.partial(epoch_kernel, epoch),
@@ -340,8 +356,8 @@
             ancestors,
             migration,
             half,
-            pattern.T,
-            current,
+            in_hbm(pattern.T),
+            in_hbm(current),
             temper,
             states,
             partner,
@@ -349,7 +365,7 @@
             weights,
             noise,
             rates,
-            seen,
+            observed,
             *([logliks] if epoch else []),
         )
     log_weight, evidence = pl.pallas_call(

time: 48.9 us -> 43.7 us (0.89)
  local copies, waits for them, and re-layouts: 5.83 us -> 0.02 us
  Pallas kernels: 26.7 us -> 30.2 us
  waiting for transfers between devices: 10.2 us -> 8.41 us
  starting transfers between devices: 5.03 us -> 4.01 us
    unnamed x23 -> x6, local copies, waits for them, and re-layouts: 5.83 us -> 0.02 us
    ppermute x3, waiting for transfers between devices: 4.79 us -> 1.14 us  [from_partner(): return lax.ppermute(value, 'island', pairs)]
    ppermute x2, waiting for transfers between devices: 5.45 us -> 7.27 us  [from_behind(): return lax.ppermute(block, 'island', route)]
    pallas_call x1, Pallas kernels: 3.54 us -> 4.78 us  [on_device(): pl.pallas_call(weights_kernel, out_shape=shape((BLOCKS, NEIGH * HALF, LAN...]
    pallas_call x2, Pallas kernels: 1.35 us -> 2.39 us  [on_device(): pl.pallas_call(functools.partial(leaving_kernel, epoch), out_shape=shape(...]
    ppermute x2, starting transfers between devices: 4.51 us -> 3.48 us  [from_behind(): return lax.ppermute(block, 'island', route)]
    pallas_call x1 -> x2, Pallas kernels: 4.17 us -> 4.95 us  [on_device(): pl.pallas_call(functools.partial(noise_kernel, epoch), out_shape=shape((S...]
  transfers between devices with their start and end apart: 5 -> 5, of which waited for: 4 -> 3; matrix products, arithmetic and copies ran while one was open for 2% -> 0% of each run, Pallas kernels for 16% -> 22%
where the time goes in v2:
time: 43.7 us; the launch traced here: 43.4 us
  Pallas kernels  30.2 us (69%)
  waiting for transfers between devices  8.41 us (19%)
  starting transfers between devices  4.01 us (9%)
  between operations  0.76 us (2%)
    pallas_call x2, Pallas kernels, on_device(): pl.pallas_call(functools.partial(epoch_kernel, epoch), out_shape=(shape((...  17.4 us
    ppermute x2, waiting for transfers between devices, from_behind(): return lax.ppermute(block, 'island', route)  7.27 us
    pallas_call x2, Pallas kernels, on_device(): pl.pallas_call(functools.partial(noise_kernel, epoch), out_shape=shape((S...  4.95 us
    pallas_call x1, Pallas kernels, on_device(): pl.pallas_call(weights_kernel, out_shape=shape((BLOCKS, NEIGH * HALF, LAN...  4.78 us
    ppermute x2, starting transfers between devices, from_behind(): return lax.ppermute(block, 'island', route)  3.48 us
    pallas_call x2, Pallas kernels, on_device(): pl.pallas_call(functools.partial(leaving_kernel, epoch), out_shape=shape(...  2.39 us
    ppermute x3, waiting for transfers between devices, from_partner(): return lax.ppermute(value, 'island', pairs)  1.14 us
  transfers between devices with their start and end apart: 5, of which 3 were waited for; matrix products, arithmetic and copies ran while one was open for 0% of the time, Pallas kernels for 22%

profile of v2, /device:TPU:0, one launch (start us, length us, event | category | flops | bytes accessed | tf_op | source)
XLA Modules:
  0.0 43.4 jit_solution(7398294916521578955)
XLA Ops:
  0.6 0.5 %collective-permute-start = (bf16[8,4,8192]{2,1,0:T(4,128)(2,1)}, bf16[8,4,8192]{2,1,0:T(4,128)(2,1)S(1)}, u32[]{:S(2)}, u32[]{:S(2)}) collective-permute-start(bf16[8,4,8192]{2,1,0:T(4,128)(2,1)} %local.3), channel_id=1, source_target_pairs={{0,1},{1,0},{2,3},{3,2},{4,5},{5,4},{6,7},{7,6},{8,9},{9,8},{10,11... | collective-permute-start | bytes 1572872 | tf_op jit(solution)/shard_map/ppermute | solution.py:40
  1.1 2.5 %noise.2 = f32[2,64,32,128]{3,2,1,0:T(8,128)S(1)} custom-call(s32[1,4]{1,0:T(1,128)} %seeds.3), custom_call_target="tpu_custom_call" | custom-call | flops 15000000 | bytes 6000000 | tf_op jit(solution)/shard_map/noise/pallas_call | solution.py:316
  3.6 0.0 collective-permute-done.partner
  3.6 1.6 %leaving.2 = bf16[1,4,8192]{2,1,0:T(4,128)(2,1)S(1)} custom-call(s32[2,1,8]{2,1,0:T(1,128)} %ancestors.7, s32[2,1,8]{2,1,0:T(1,128)} %migration.7, s32[1]{0:T(128)} %bitcast.half, bf16[8,4,8192]{2,1,0:T(4,128)(2,1)} %local.3, bf16[8,4,8192]{2,1,0:T(4,128)(2,1)S(1)} %collective-permute-done.partner), custom_call_target="tpu_custom_call" | custom-call | tf_op jit(solution)/shard_map/leaving/pallas_call | solution.py:326
  5.2 2.6 %collective-permute-start.1 = (bf16[1,4,8192]{2,1,0:T(4,128)(2,1)S(1)}, bf16[1,4,8192]{2,1,0:T(4,128)(2,1)S(1)}, u32[]{:S(2)}, u32[]{:S(2)}) collective-permute-start(bf16[1,4,8192]{2,1,0:T(4,128)(2,1)S(1)} %leaving.2), channel_id=1, source_target_pairs={{14,0},{15,1},{0,2},{1,3},{2,4},{3,5},{4,6},{5,7},{6,8},{7,9},{8,1... | collective-permute-start | bytes 196616 | tf_op jit(solution)/shard_map/ppermute | solution.py:46
  7.9 0.0 copy-start
  7.9 0.0 copy-start.1
  7.9 0.0 copy-start.2
  7.9 4.8 %weights.1 = bf16[128,160,128]{2,1,0:T(8,128)(2,1)S(1)} custom-call(bf16[5,128,4096]{2,1,0:T(8,128)(2,1)} %bitcast.8), custom_call_target="tpu_custom_call" | custom-call | flops 3000000 | bytes 10000000 | tf_op jit(solution)/shard_map/weights/pallas_call | solution.py:295
  12.7 0.9 %collective-permute-done.1.arriving = bf16[1,4,8192]{2,1,0:T(4,128)(2,1)S(1)} collective-permute-done((bf16[1,4,8192]{2,1,0:T(4,128)(2,1)S(1)}, bf16[1,4,8192]{2,1,0:T(4,128)(2,1)S(1)}, u32[]{:S(2)}, u32[]{:S(2)}) %collective-permute-start.1) | collective-permute-done | bytes 65568 | tf_op jit(solution)/shard_map/ppermute | solution.py:46
  13.6 0.0 copy-done
  13.6 0.0 copy-done.1
  13.6 0.0 copy-done.2
  13.6 8.3 %epoch.2 = (bf16[8,4,8192]{2,1,0:T(4,128)(2,1)S(1)}, f32[2,128]{1,0:T(2,128)S(1)}) custom-call(s32[2,1,8]{2,1,0:T(1,128)} %ancestors.7, s32[2,1,8]{2,1,0:T(1,128)} %migration.7, s32[1]{0:T(128)} %bitcast.half, s32[5,128]{1,0:T(8,128)} %bitcast.9, f32[4]{0:T(128)} %current.3, f32[1]{0:T(128)} %bitcast.2.temper, bf16[8,4,8192]{2,1,0:T(4,128)(2,1)S(1)} %copy-done, ...), custom_call_target="tpu_custom_call" | custom-call | tf_op jit(solution)/shard_map/epoch/pallas_call | solution.py:336
  21.9 0.0 collective-permute-start.2
  21.9 2.5 %noise.3 = f32[2,64,32,128]{3,2,1,0:T(8,128)S(1)} custom-call(s32[1,4]{1,0:T(1,128)} %seeds.3), custom_call_target="tpu_custom_call" | custom-call | flops 15000000 | bytes 6000000 | tf_op jit(solution)/shard_map/noise/pallas_call | solution.py:316
  24.3 0.0 collective-permute-done.2.partner
  24.4 0.8 %leaving.3 = bf16[1,4,8192]{2,1,0:T(4,128)(2,1)S(1)} custom-call(s32[2,1,8]{2,1,0:T(1,128)} %ancestors.7, s32[2,1,8]{2,1,0:T(1,128)} %migration.7, s32[1]{0:T(128)} %bitcast.half, bf16[8,4,8192]{2,1,0:T(4,128)(2,1)S(1)} %get-tuple-element.15.local, bf16[8,4,8192]{2,1,0:T(4,128)(2,1)S(1)} %collective-permute-done.2.partner), custom_call_target="tpu_custom_call" | custom-call | tf_op jit(solution)/shard_map/leaving/pallas_call | solution.py:326
  25.2 0.9 %collective-permute-start.3 = (bf16[1,4,8192]{2,1,0:T(4,128)(2,1)S(1)}, bf16[1,4,8192]{2,1,0:T(4,128)(2,1)S(1)}, u32[]{:S(2)}, u32[]{:S(2)}) collective-permute-start(bf16[1,4,8192]{2,1,0:T(4,128)(2,1)S(1)} %leaving.3), channel_id=1, source_target_pairs={{14,0},{15,1},{0,2},{1,3},{2,4},{3,5},{4,6},{5,7},{6,8},{7,9},{8,1... | collective-permute-start | bytes 196616 | tf_op jit(solution)/shard_map/ppermute | solution.py:46
  26.1 6.4 %collective-permute-done.3.arriving = bf16[1,4,8192]{2,1,0:T(4,128)(2,1)S(1)} collective-permute-done((bf16[1,4,8192]{2,1,0:T(4,128)(2,1)S(1)}, bf16[1,4,8192]{2,1,0:T(4,128)(2,1)S(1)}, u32[]{:S(2)}, u32[]{:S(2)}) %collective-permute-start.3) | collective-permute-done | bytes 65568 | tf_op jit(solution)/shard_map/ppermute | solution.py:46
  32.4 9.1 %epoch.3 = (bf16[8,4,8192]{2,1,0:T(4,128)(2,1)}, f32[2,128]{1,0:T(2,128)S(1)}) custom-call(s32[2,1,8]{2,1,0:T(1,128)} %ancestors.7, s32[2,1,8]{2,1,0:T(1,128)} %migration.7, s32[1]{0:T(128)} %bitcast.half, s32[5,128]{1,0:T(8,128)} %bitcast.10, f32[4]{0:T(128)} %current.3, f32[1]{0:T(128)} %bitcast.2.temper, bf16[8,4,8192]{2,1,0:T(4,128)(2,1)S(1)} %get-tuple-element.15.local, ...), custom_call_target="tpu_custom_call" | custom-call | tf_op jit(solution)/shard_map/epoch/pallas_call | solution.py:336
  41.5 0.0 collective-permute-start.4
  41.5 1.1 %collective-permute-done.4.other = f32[2,128]{1,0:T(2,128)S(1)} collective-permute-done((f32[2,128]{1,0:T(2,128)S(1)}, f32[2,128]{1,0:T(2,128)S(1)}, u32[]{:S(2)}, u32[]{:S(2)}) %collective-permute-start.4) | collective-permute-done | bytes 1056 | tf_op jit(solution)/shard_map/ppermute | solution.py:40
  42.7 0.7 %weigh.1 = (f32[2,8]{1,0:T(2,128)}, f32[1,1]{1,0:T(1,128)}) custom-call(f32[2,128]{1,0:T(2,128)S(1)} %get-tuple-element.20.own, f32[2,128]{1,0:T(2,128)S(1)} %collective-permute-done.4.other), custom_call_target="tpu_custom_call" | custom-call | tf_op jit(solution)/shard_map/weigh/pallas_call | solution.py:371
Async XLA Ops:
  0.6 3.0 %collective-permute-start = (bf16[8,4,8192]{2,1,0:T(4,128)(2,1)}, bf16[8,4,8192]{2,1,0:T(4,128)(2,1)S(1)}, u32[]{:S(2)}, u32[]{:S(2)}) collective-permute-start(bf16[8,4,8192]{2,1,0:T(4,128)(2,1)} %local.3), channel_id=1, source_target_pairs={{0,1},{1,0},{2,3},{3,2},{4,5},{5,4},{6,7},{7,6},{8,9},{9,8},{10,11... | collective-permute-start | bytes 1572872 | tf_op jit(solution)/shard_map/ppermute | solution.py:40
  5.2 8.4 %collective-permute-start.1 = (bf16[1,4,8192]{2,1,0:T(4,128)(2,1)S(1)}, bf16[1,4,8192]{2,1,0:T(4,128)(2,1)S(1)}, u32[]{:S(2)}, u32[]{:S(2)}) collective-permute-start(bf16[1,4,8192]{2,1,0:T(4,128)(2,1)S(1)} %leaving.2), channel_id=1, source_target_pairs={{14,0},{15,1},{0,2},{1,3},{2,4},{3,5},{4,6},{5,7},{6,8},{7,9},{8,1... | collective-permute-start | bytes 196616 | tf_op jit(solution)/shard_map/ppermute | solution.py:46
  7.9 5.7 %copy-start = (bf16[8,4,8192]{2,1,0:T(4,128)(2,1)S(1)}, bf16[8,4,8192]{2,1,0:T(4,128)(2,1)}, u32[]{:S(2)}) copy-start(bf16[8,4,8192]{2,1,0:T(4,128)(2,1)} %local.3) | copy-start | bytes 1572868
  7.9 5.7 %copy-start.1 = (f32[4,8192]{1,0:T(4,128)S(1)}, f32[4,8192]{1,0:T(4,128)}, u32[]{:S(2)}) copy-start(f32[4,8192]{1,0:T(4,128)} %observed.3) | copy-start | bytes 393220
  7.9 5.7 %copy-start.2 = (f32[8192]{0:T(1024)S(1)}, f32[8192]{0:T(1024)}, u32[]{:S(2)}) copy-start(f32[8192]{0:T(1024)} %param.14) | copy-start | bytes 98308
  21.9 2.5 %collective-permute-start.2 = (bf16[8,4,8192]{2,1,0:T(4,128)(2,1)S(1)}, bf16[8,4,8192]{2,1,0:T(4,128)(2,1)S(1)}, u32[]{:S(2)}, u32[]{:S(2)}) collective-permute-start(bf16[8,4,8192]{2,1,0:T(4,128)(2,1)S(1)} %get-tuple-element.15.local), channel_id=1, source_target_pairs={{0,1},{1,0},{2,3},{3,2},{4,5},{5,4},{6,7},{7,6},{8,9},{9,8},{10,11... | collective-permute-start | bytes 1572872 | tf_op jit(solution)/shard_map/ppermute | solution.py:40
  25.2 7.3 %collective-permute-start.3 = (bf16[1,4,8192]{2,1,0:T(4,128)(2,1)S(1)}, bf16[1,4,8192]{2,1,0:T(4,128)(2,1)S(1)}, u32[]{:S(2)}, u32[]{:S(2)}) collective-permute-start(bf16[1,4,8192]{2,1,0:T(4,128)(2,1)S(1)} %leaving.3), channel_id=1, source_target_pairs={{14,0},{15,1},{0,2},{1,3},{2,4},{3,5},{4,6},{5,7},{6,8},{7,9},{8,1... | collective-permute-start | bytes 196616 | tf_op jit(solution)/shard_map/ppermute | solution.py:46
  41.5 1.1 %collective-permute-start.4 = (f32[2,128]{1,0:T(2,128)S(1)}, f32[2,128]{1,0:T(2,128)S(1)}, u32[]{:S(2)}, u32[]{:S(2)}) collective-permute-start(f32[2,128]{1,0:T(2,128)S(1)} %get-tuple-element.20.own), channel_id=1, source_target_pairs={{0,1},{1,0},{2,3},{3,2},{4,5},{5,4},{6,7},{7,6},{8,9},{9,8},{10,11... | collective-permute-start | bytes 3080 | tf_op jit(solution)/shard_map/ppermute | solution.py:40

commit v3 on v2

--- a/solution.py
+++ b/solution.py
@@ -56,20 +56,40 @@
     return shifted(hashed) & 16777215
 
 
-def noise_kernel(epoch, seeds, out):
+def draw(step, seed, out):
     row = lax.broadcasted_iota(jnp.int32, (STATES * ROWS, LANES), 0)
     lane = lax.broadcasted_iota(jnp.int32, (STATES * ROWS, LANES), 1)
-    counter = 2 * (((row % ROWS) * STATES + row // ROWS) * CELLS + lane)
+    start = 2 * (((row % ROWS) * STATES + row // ROWS) * CELLS + lane) + seed * 40503
+
+    def one(q, carry):
+        anchor = start + q * (2 * LANES)
+        apart = scramble(anchor) - scramble(anchor + 1)
+        out[step, q] = apart.astype(jnp.float32) * NOISE_SCALE
+        return carry
+
+    lax.fori_loop(0, PAIRS, one, 0, unroll=4)
+
+
+def first_noise_kernel(*refs):
+    sources, out, targets, (half, temper, sems) = refs[:5], refs[5], refs[6:11], refs[11:]
+    copies = [
+        pltpu.make_async_copy(source, target, sems.at[i])
+        for i, (source, target) in enumerate(zip(sources, targets))
+    ]
+    for copy in copies:
+        copy.start()
+    position = lax.axis_index("island")
+    half[0] = position & 1
+    temper[0] = 0.25 * lax.shift_left(jnp.int32(1), (position >> 1) & 3).astype(jnp.float32)
+    for copy in copies:
+        copy.wait()
     for step in range(STEPS_EPOCH):
-        start = counter + seeds[0, epoch * STEPS_EPOCH + step] * 40503
-
-        def one(q, carry):
-            anchor = start + q * (2 * LANES)
-            apart = scramble(anchor) - scramble(anchor + 1)
-            out[step, q] = apart.astype(jnp.float32) * NOISE_SCALE
-            return carry
-
-        lax.fori_loop(0, PAIRS, one, 0, unroll=4)
+        draw(step, targets[0][0, step], out)
+
+
+def noise_kernel(seeds, out):
+    for step in range(STEPS_EPOCH):
+        draw(step, seeds[0, STEPS_EPOCH + step], out)
 
 
 def weights_kernel(coupling, out, held, wide, sems):
@@ -91,7 +111,11 @@
                 ].astype(jnp.float32)
             for b in range(group):
                 picked = wide[k, pl.ds(b, HALF, stride=group), :]
-                out[g * group + b, k * HALF : (k + 1) * HALF, :] = picked.astype(jnp.bfloat16)
+                out[
+                    g * (group // 2) + b // 2,
+                    k * HALF : (k + 1) * HALF,
+                    (b % 2) * LANES : (b % 2 + 1) * LANES,
+                ] = picked.astype(jnp.bfloat16)
         return carry
 
     lax.fori_loop(0, BLOCKS // group, one, 0)
@@ -133,7 +157,7 @@
 
     for at in range(depth - 1):
         one(at, 0, at + 1)
-    lax.fori_loop(depth - 1, count, steady, 0)
+    lax.fori_loop(depth - 1, count, steady, 0, unroll=2)
     for at in range(count, count + depth - 1):
         one(at, at - count + 1, depth)
 
@@ -200,20 +224,20 @@
                     i * rows : (i + 1) * rows, tile * LANES : (tile + 1) * LANES
                 ]
 
-    def product(held, b):
+    def inputs(held, b):
         pieces = [held[pattern[k, b]] for k in range(NEIGH)]
         first = jnp.where(
             lane < HALF,
             pieces[0],
             jnp.where(lane < 2 * HALF, pieces[1], jnp.where(lane < 3 * HALF, pieces[2], pieces[3])),
         )
-        both = jnp.concatenate([first, pieces[4][:, :HALF]], axis=1)
-        return jnp.dot(both, weights[b], preferred_element_type=jnp.float32)
+        return jnp.concatenate([first, pieces[4][:, :HALF]], axis=1)
 
     def couple(held, g):
         for i, q in enumerate(members(g)):
-            left = product(held, 2 * q)
-            right = product(held, 2 * q + 1)
+            both = jnp.concatenate([inputs(held, 2 * q), inputs(held, 2 * q + 1)], axis=0)
+            product = jnp.dot(both, weights[q], preferred_element_type=jnp.float32)
+            left, right = product[: 2 * rows, :LANES], product[2 * rows :, LANES:]
             inside = jnp.where(lane < BLOCK, left[:rows], right[rows:])
             across = jnp.where(lane < BLOCK, right[:rows], left[rows:])
             coupled[i] = inside + pltpu.roll(across, BLOCK, 1)
@@ -287,14 +311,30 @@
 def on_device(
     particles, ancestors, migration, pattern, coupling, cell_rate, current, observed, noise_seeds
 ):
-    position = lax.axis_index("island")
-    half = (position % 2).astype(jnp.int32)[None]
-    temper = (0.25 * jnp.power(2.0, (position // 2 % 4).astype(jnp.float32)))[None]
     shape = jax.ShapeDtypeStruct
-
+    vector = shape((STEPS_EPOCH, PAIRS, STATES * ROWS, LANES), jnp.float32)
+    cost = pl.CostEstimate(flops=15000000, bytes_accessed=6000000, transcendentals=0)
+    partner = from_partner(particles)
+    scalars = (noise_seeds, ancestors, migration, pattern.T, current)
+    noise, *scalars = pl.pallas_call(
+        first_noise_kernel,
+        out_shape=(
+            vector,
+            *(pltpu.SMEM(x.shape, x.dtype) for x in scalars),
+            pltpu.SMEM((1,), jnp.int32),
+            pltpu.SMEM((1,), jnp.float32),
+        ),
+        in_specs=[HBM] * 5,
+        out_specs=(VMEM, *[SMEM] * 7),
+        scratch_shapes=[pltpu.SemaphoreType.DMA((5,))],
+        compiler_params=params(2),
+        cost_estimate=cost,
+        name="noise",
+    )(*(in_hbm(x) for x in scalars))
+    seeds, ancestors, migration, pattern, current, half, temper = scalars
     weights = pl.pallas_call(
         weights_kernel,
-        out_shape=shape((BLOCKS, NEIGH * HALF, LANES), jnp.bfloat16),
+        out_shape=shape((PAIRS, NEIGH * HALF, 2 * LANES), jnp.bfloat16),
         in_specs=[HBM],
         out_specs=VMEM,
         scratch_shapes=[
@@ -307,21 +347,21 @@
         name="weights",
     )(in_hbm(coupling.transpose(1, 0, 2)))
 
-    ancestors, migration = in_hbm(ancestors), in_hbm(migration)
     states = particles
     logliks = ()
     rates = cell_rate.reshape(PAIRS, LANES)
     for epoch in range(EPOCHS):
-        partner = from_partner(states)
-        noise = pl.pallas_call(
-            functools.partial(noise_kernel, epoch),
-            out_shape=shape((STEPS_EPOCH, PAIRS, STATES * ROWS, LANES), jnp.float32),
-            in_specs=[SMEM],
-            out_specs=VMEM,
-            compiler_params=params(2),
-            cost_estimate=pl.CostEstimate(flops=15000000, bytes_accessed=6000000, transcendentals=0),
-            name="noise",
-        )(in_hbm(noise_seeds))
+        if epoch:
+            partner = from_partner(states)
+            noise = pl.pallas_call(
+                noise_kernel,
+                out_shape=vector,
+                in_specs=[SMEM],
+                out_specs=VMEM,
+                compiler_params=params(2),
+                cost_estimate=cost,
+                name="noise",
+            )(seeds)
         partner, noise = lax.optimization_barrier((partner, noise))
         leaving = pl.pallas_call(
             functools.partial(leaving_kernel, epoch),
@@ -356,8 +396,8 @@
             ancestors,
             migration,
             half,
-            in_hbm(pattern.T),
-            in_hbm(current),
+            pattern,
+            current,
             temper,
             states,
             partner,

time: 43.7 us -> 36.4 us (0.83)
  Pallas kernels: 30.2 us -> 23.5 us
  waiting for transfers between devices: 8.41 us -> 6.62 us
  starting transfers between devices: 4.01 us -> 5.08 us
    pallas_call x2, Pallas kernels: 17.4 us -> 12.2 us  [on_device(): pl.pallas_call(functools.partial(epoch_kernel, epoch), out_shape=(shape((...]
    ppermute x2, waiting for transfers between devices: 7.27 us -> 5.48 us  [from_behind(): return lax.ppermute(block, 'island', route)]
    pallas_call x2, Pallas kernels: 2.39 us -> 0.98 us  [on_device(): pl.pallas_call(functools.partial(leaving_kernel, epoch), out_shape=shape(...]
    ppermute x2, starting transfers between devices: 3.48 us -> 4.34 us  [from_behind(): return lax.ppermute(block, 'island', route)]
  transfers between devices with their start and end apart: 5 -> 5, of which waited for: 3 -> 2; matrix products, arithmetic and copies ran while one was open for 0% -> 0% of each run, Pallas kernels for 22% -> 27%
where the time goes in v3:
time: 36.4 us; the launch traced here: 35.9 us
  Pallas kernels  23.5 us (65%)
  waiting for transfers between devices  6.62 us (18%)
  starting transfers between devices  5.08 us (14%)
  between operations  0.72 us (2%)
    pallas_call x2, Pallas kernels, on_device(): pl.pallas_call(functools.partial(epoch_kernel, epoch), out_shape=(shape((...  12.2 us
    ppermute x2, waiting for transfers between devices, from_behind(): return lax.ppermute(block, 'island', route)  5.48 us
    pallas_call x1, Pallas kernels, on_device(): pl.pallas_call(weights_kernel, out_shape=shape((PAIRS, NEIGH * HALF, 2 *...  5.19 us
    ppermute x2, starting transfers between devices, from_behind(): return lax.ppermute(block, 'island', route)  4.34 us
    pallas_call x1, Pallas kernels, on_device(): pl.pallas_call(first_noise_kernel, out_shape=(vector, *(pltpu.SMEM(x.shap...  2.6 us
    pallas_call x1, Pallas kernels, on_device(): pl.pallas_call(noise_kernel, out_shape=vector, in_specs=[SMEM], out_specs...  1.81 us
    ppermute x3, waiting for transfers between devices, from_partner(): return lax.ppermute(value, 'island', pairs)  1.14 us
    pallas_call x2, Pallas kernels, on_device(): pl.pallas_call(functools.partial(leaving_kernel, epoch), out_shape=shape(...  0.98 us
  transfers between devices with their start and end apart: 5, of which 2 were waited for; matrix products, arithmetic and copies ran while one was open for 0% of the time, Pallas kernels for 27%

profile of v3, /device:TPU:0, one launch (start us, length us, event | category | flops | bytes accessed | tf_op | source)
XLA Modules:
  0.0 35.9 jit_solution(17864459275183895893)
XLA Ops:
  0.6 0.5 %collective-permute-start = (bf16[8,4,8192]{2,1,0:T(4,128)(2,1)}, bf16[8,4,8192]{2,1,0:T(4,128)(2,1)S(1)}, u32[]{:S(2)}, u32[]{:S(2)}) collective-permute-start(bf16[8,4,8192]{2,1,0:T(4,128)(2,1)} %local.3), channel_id=1, source_target_pairs={{0,1},{1,0},{2,3},{3,2},{4,5},{5,4},{6,7},{7,6},{8,9},{9,8},{10,11... | collective-permute-start | bytes 1572872 | tf_op jit(solution)/shard_map/ppermute | solution.py:40
  1.1 2.6 %noise.2 = (f32[2,64,32,128]{3,2,1,0:T(8,128)S(1)}, s32[1,4]{1,0:T(1,128)S(4)}, s32[2,1,8]{2,1,0:T(1,128)S(4)}, s32[2,1,8]{2,1,0:T(1,128)S(4)}, s32[5,128]{1,0:T...) custom-call(s32[1,4]{1,0:T(1,128)} %refs_0_.1, s32[2,1,8]{2,1,0:T(1,128)} %refs_1_.1, s32[2,1,8]{2,1,0:T(1,128)} %refs_2_.1, ...), custom_call_target="tpu_custom_call" | custom-call | flops 15000000 | bytes 6000000 | tf_op jit(solution)/shard_map/noise/pallas_call | solution.py:319
  3.8 0.0 collective-permute-done.partner
  3.8 0.9 %leaving.2 = bf16[1,4,8192]{2,1,0:T(4,128)(2,1)S(1)} custom-call(s32[2,1,8]{2,1,0:T(1,128)S(4)} %get-tuple-element.21.ancestors, s32[2,1,8]{2,1,0:T(1,128)S(4)} %get-tuple-element.22.migration, s32[1]{0:T(128)S(4)} %get-tuple-element.23.half, bf16[8,4,8192]{2,1,0:T(4,128)(2,1)} %local.3, bf16[8,4,8192]{2,1,0:T(4,128)(2,1)S(1)} %collective-permute-done.partner), custom_call_target="tpu_custom_call" | custom-call | tf_op jit(solution)/shard_map/leaving/pallas_call | solution.py:366
  4.6 2.6 %collective-permute-start.1 = (bf16[1,4,8192]{2,1,0:T(4,128)(2,1)S(1)}, bf16[1,4,8192]{2,1,0:T(4,128)(2,1)S(1)}, u32[]{:S(2)}, u32[]{:S(2)}) collective-permute-start(bf16[1,4,8192]{2,1,0:T(4,128)(2,1)S(1)} %leaving.2), channel_id=1, source_target_pairs={{14,0},{15,1},{0,2},{1,3},{2,4},{3,5},{4,6},{5,7},{6,8},{7,9},{8,1... | collective-permute-start | bytes 196616 | tf_op jit(solution)/shard_map/ppermute | solution.py:46
  7.2 0.0 copy-start
  7.2 0.0 copy-start.1
  7.2 0.0 copy-start.2
  7.2 5.2 %weights.1 = bf16[64,160,256]{2,1,0:T(8,128)(2,1)S(1)} custom-call(bf16[5,128,4096]{2,1,0:T(8,128)(2,1)} %bitcast.6), custom_call_target="tpu_custom_call" | custom-call | flops 3000000 | bytes 10000000 | tf_op jit(solution)/shard_map/weights/pallas_call | solution.py:335
  12.4 0.0 collective-permute-done.1.arriving
  12.4 0.0 copy-done
  12.5 0.0 copy-done.1
  12.5 0.0 copy-done.2
  12.5 5.7 %epoch.2 = (bf16[8,4,8192]{2,1,0:T(4,128)(2,1)S(1)}, f32[2,128]{1,0:T(2,128)S(1)}) custom-call(s32[2,1,8]{2,1,0:T(1,128)S(4)} %get-tuple-element.21.ancestors, s32[2,1,8]{2,1,0:T(1,128)S(4)} %get-tuple-element.22.migration, s32[1]{0:T(128)S(4)} %get-tuple-element.23.half, s32[5,128]{1,0:T(8,128)S(4)} %get-tuple-element.24.pattern, ...), custom_call_target="tpu_custom_call" | custom-call | tf_op jit(solution)/shard_map/epoch/pallas_call | solution.py:376
  18.2 0.2 collective-permute-start.2
  18.4 1.8 %noise.3 = f32[2,64,32,128]{3,2,1,0:T(8,128)S(1)} custom-call(s32[1,4]{1,0:T(1,128)S(4)} %get-tuple-element.31.seeds), custom_call_target="tpu_custom_call" | custom-call | flops 15000000 | bytes 6000000 | tf_op jit(solution)/shard_map/noise/pallas_call | solution.py:356
  20.2 0.0 collective-permute-done.2.partner
  20.2 0.1 leaving.3
  20.4 1.8 %collective-permute-start.3 = (bf16[1,4,8192]{2,1,0:T(4,128)(2,1)S(1)}, bf16[1,4,8192]{2,1,0:T(4,128)(2,1)S(1)}, u32[]{:S(2)}, u32[]{:S(2)}) collective-permute-start(bf16[1,4,8192]{2,1,0:T(4,128)(2,1)S(1)} %leaving.3), channel_id=1, source_target_pairs={{14,0},{15,1},{0,2},{1,3},{2,4},{3,5},{4,6},{5,7},{6,8},{7,9},{8,1... | collective-permute-start | bytes 196616 | tf_op jit(solution)/shard_map/ppermute | solution.py:46
  22.1 5.5 %collective-permute-done.3.arriving = bf16[1,4,8192]{2,1,0:T(4,128)(2,1)S(1)} collective-permute-done((bf16[1,4,8192]{2,1,0:T(4,128)(2,1)S(1)}, bf16[1,4,8192]{2,1,0:T(4,128)(2,1)S(1)}, u32[]{:S(2)}, u32[]{:S(2)}) %collective-permute-start.3) | collective-permute-done | bytes 65568 | tf_op jit(solution)/shard_map/ppermute | solution.py:46
  27.6 6.4 %epoch.3 = (bf16[8,4,8192]{2,1,0:T(4,128)(2,1)}, f32[2,128]{1,0:T(2,128)S(1)}) custom-call(s32[2,1,8]{2,1,0:T(1,128)S(4)} %get-tuple-element.21.ancestors, s32[2,1,8]{2,1,0:T(1,128)S(4)} %get-tuple-element.22.migration, s32[1]{0:T(128)S(4)} %get-tuple-element.23.half, s32[5,128]{1,0:T(8,128)S(4)} %get-tuple-element.24.pattern, ...), custom_call_target="tpu_custom_call" | custom-call | tf_op jit(solution)/shard_map/epoch/pallas_call | solution.py:376
  34.0 0.0 collective-permute-start.4
  34.0 1.1 %collective-permute-done.4.other = f32[2,128]{1,0:T(2,128)S(1)} collective-permute-done((f32[2,128]{1,0:T(2,128)S(1)}, f32[2,128]{1,0:T(2,128)S(1)}, u32[]{:S(2)}, u32[]{:S(2)}) %collective-permute-start.4) | collective-permute-done | bytes 1056 | tf_op jit(solution)/shard_map/ppermute | solution.py:40
  35.2 0.7 %weigh.1 = (f32[2,8]{1,0:T(2,128)}, f32[1,1]{1,0:T(1,128)}) custom-call(f32[2,128]{1,0:T(2,128)S(1)} %get-tuple-element.36.own, f32[2,128]{1,0:T(2,128)S(1)} %collective-permute-done.4.other), custom_call_target="tpu_custom_call" | custom-call | tf_op jit(solution)/shard_map/weigh/pallas_call | solution.py:411
Async XLA Ops:
  0.6 3.1 %collective-permute-start = (bf16[8,4,8192]{2,1,0:T(4,128)(2,1)}, bf16[8,4,8192]{2,1,0:T(4,128)(2,1)S(1)}, u32[]{:S(2)}, u32[]{:S(2)}) collective-permute-start(bf16[8,4,8192]{2,1,0:T(4,128)(2,1)} %local.3), channel_id=1, source_target_pairs={{0,1},{1,0},{2,3},{3,2},{4,5},{5,4},{6,7},{7,6},{8,9},{9,8},{10,11... | collective-permute-start | bytes 1572872 | tf_op jit(solution)/shard_map/ppermute | solution.py:40
  4.6 7.8 %collective-permute-start.1 = (bf16[1,4,8192]{2,1,0:T(4,128)(2,1)S(1)}, bf16[1,4,8192]{2,1,0:T(4,128)(2,1)S(1)}, u32[]{:S(2)}, u32[]{:S(2)}) collective-permute-start(bf16[1,4,8192]{2,1,0:T(4,128)(2,1)S(1)} %leaving.2), channel_id=1, source_target_pairs={{14,0},{15,1},{0,2},{1,3},{2,4},{3,5},{4,6},{5,7},{6,8},{7,9},{8,1... | collective-permute-start | bytes 196616 | tf_op jit(solution)/shard_map/ppermute | solution.py:46
  7.2 5.2 %copy-start = (bf16[8,4,8192]{2,1,0:T(4,128)(2,1)S(1)}, bf16[8,4,8192]{2,1,0:T(4,128)(2,1)}, u32[]{:S(2)}) copy-start(bf16[8,4,8192]{2,1,0:T(4,128)(2,1)} %local.3) | copy-start | bytes 1572868
  7.2 5.2 %copy-start.1 = (f32[4,8192]{1,0:T(4,128)S(1)}, f32[4,8192]{1,0:T(4,128)}, u32[]{:S(2)}) copy-start(f32[4,8192]{1,0:T(4,128)} %observed.3) | copy-start | bytes 393220
  7.2 5.2 %copy-start.2 = (f32[8192]{0:T(1024)S(1)}, f32[8192]{0:T(1024)}, u32[]{:S(2)}) copy-start(f32[8192]{0:T(1024)} %param.14) | copy-start | bytes 98308
  18.2 2.0 %collective-permute-start.2 = (bf16[8,4,8192]{2,1,0:T(4,128)(2,1)S(1)}, bf16[8,4,8192]{2,1,0:T(4,128)(2,1)S(1)}, u32[]{:S(2)}, u32[]{:S(2)}) collective-permute-start(bf16[8,4,8192]{2,1,0:T(4,128)(2,1)S(1)} %get-tuple-element.30.local), channel_id=1, source_target_pairs={{0,1},{1,0},{2,3},{3,2},{4,5},{5,4},{6,7},{7,6},{8,9},{9,8},{10,11... | collective-permute-start | bytes 1572872 | tf_op jit(solution)/shard_map/ppermute | solution.py:40
  20.4 7.2 %collective-permute-start.3 = (bf16[1,4,8192]{2,1,0:T(4,128)(2,1)S(1)}, bf16[1,4,8192]{2,1,0:T(4,128)(2,1)S(1)}, u32[]{:S(2)}, u32[]{:S(2)}) collective-permute-start(bf16[1,4,8192]{2,1,0:T(4,128)(2,1)S(1)} %leaving.3), channel_id=1, source_target_pairs={{14,0},{15,1},{0,2},{1,3},{2,4},{3,5},{4,6},{5,7},{6,8},{7,9},{8,1... | collective-permute-start | bytes 196616 | tf_op jit(solution)/shard_map/ppermute | solution.py:46
  34.0 1.1 %collective-permute-start.4 = (f32[2,128]{1,0:T(2,128)S(1)}, f32[2,128]{1,0:T(2,128)S(1)}, u32[]{:S(2)}, u32[]{:S(2)}) collective-permute-start(f32[2,128]{1,0:T(2,128)S(1)} %get-tuple-element.36.own), channel_id=1, source_target_pairs={{0,1},{1,0},{2,3},{3,2},{4,5},{5,4},{6,7},{7,6},{8,9},{9,8},{10,11... | collective-permute-start | bytes 3080 | tf_op jit(solution)/shard_map/ppermute | solution.py:40

commit v4 on v3

--- a/solution.py
+++ b/solution.py
@@ -94,6 +94,7 @@
 
 def weights_kernel(coupling, out, held, wide, sems):
     group = 16
+    lane = lax.broadcasted_iota(jnp.int32, (1, LANES), 1)
 
     def fetch(g):
         rows = pl.ds(pl.multiple_of(g * group, group), group)
@@ -109,13 +110,15 @@
                 wide[k, r * group : (r + 1) * group, :] = held[
                     k, pl.ds(pl.multiple_of(g * group, group), group), r * LANES : (r + 1) * LANES
                 ].astype(jnp.float32)
-            for b in range(group):
-                picked = wide[k, pl.ds(b, HALF, stride=group), :]
+            for b in range(0, group, 2):
+                left, right = (wide[k, pl.ds(b + d, HALF, stride=group), :] for d in range(2))
+                across = pltpu.roll(jnp.where(lane < BLOCK, right, left), BLOCK, 1)
+                even, odd = jnp.where(lane < BLOCK, left, across), jnp.where(lane < BLOCK, across, right)
                 out[
-                    g * (group // 2) + b // 2,
-                    k * HALF : (k + 1) * HALF,
-                    (b % 2) * LANES : (b % 2 + 1) * LANES,
-                ] = picked.astype(jnp.bfloat16)
+                    g * (group // 4) + b // 4,
+                    k * BLOCK : (k + 1) * BLOCK,
+                    (b // 2 % 2) * LANES : (b // 2 % 2 + 1) * LANES,
+                ] = jnp.concatenate([even, odd], axis=0).astype(jnp.bfloat16)
         return carry
 
     lax.fori_loop(0, BLOCKS // group, one, 0)
@@ -184,9 +187,9 @@
     states, logliks, gather, natural, spread, spread_next, coupled, unmix, total = rest
     lane = lax.broadcasted_iota(jnp.int32, (1, LANES), 1)
 
-    source = lax.broadcasted_iota(jnp.int32, (LANES, 4 * LANES), 0)
-    target = lax.broadcasted_iota(jnp.int32, (LANES, 4 * LANES), 1)
-    wanted = (target >> 8) * BLOCK + (target & (HALF - 1)) * 2 + ((target >> 7) & 1)
+    source = lax.broadcasted_iota(jnp.int32, (LANES, 2 * LANES), 0)
+    target = lax.broadcasted_iota(jnp.int32, (LANES, 2 * LANES), 1)
+    wanted = (target >> 7) * BLOCK + (target & (HALF - 1)) * 2 + ((target >> 5) & 1)
     unmix[...] = jnp.where(source == wanted, 1.0, 0.0).astype(jnp.bfloat16)
 
     picks = []
@@ -219,28 +222,30 @@
         cells = natural[pl.ds(g * GROUP, GROUP)].reshape(GROUP * rows, LANES)
         placed = jnp.dot(cells, unmix[...], preferred_element_type=jnp.float32).astype(jnp.bfloat16)
         for i, q in enumerate(members(g)):
-            for tile in range(4):
-                result[2 * q + tile // 2, (tile % 2) * rows : (tile % 2 + 1) * rows, :] = placed[
-                    i * rows : (i + 1) * rows, tile * LANES : (tile + 1) * LANES
+            for side in range(2):
+                result[2 * q + side] = placed[
+                    i * rows : (i + 1) * rows, side * LANES : (side + 1) * LANES
                 ]
 
     def inputs(held, b):
         pieces = [held[pattern[k, b]] for k in range(NEIGH)]
-        first = jnp.where(
-            lane < HALF,
-            pieces[0],
-            jnp.where(lane < 2 * HALF, pieces[1], jnp.where(lane < 3 * HALF, pieces[2], pieces[3])),
+        return jnp.concatenate(
+            [
+                jnp.where(lane < BLOCK, pieces[0], pieces[1]),
+                jnp.where(lane < BLOCK, pieces[2], pieces[3]),
+                pieces[4][:, :BLOCK],
+            ],
+            axis=1,
         )
-        return jnp.concatenate([first, pieces[4][:, :HALF]], axis=1)
 
     def couple(held, g):
-        for i, q in enumerate(members(g)):
-            both = jnp.concatenate([inputs(held, 2 * q), inputs(held, 2 * q + 1)], axis=0)
-            product = jnp.dot(both, weights[q], preferred_element_type=jnp.float32)
-            left, right = product[: 2 * rows, :LANES], product[2 * rows :, LANES:]
-            inside = jnp.where(lane < BLOCK, left[:rows], right[rows:])
-            across = jnp.where(lane < BLOCK, right[:rows], left[rows:])
-            coupled[i] = inside + pltpu.roll(across, BLOCK, 1)
+        for i in range(0, GROUP, 2):
+            quad = g * (GROUP // 2) + i // 2
+            four = jnp.concatenate([inputs(held, 4 * quad + d) for d in range(4)], axis=0)
+            product = jnp.dot(four, weights[quad], preferred_element_type=jnp.float32)
+            for side in range(2):
+                part = product[2 * side * rows : 2 * (side + 1) * rows, side * LANES : (side + 1) * LANES]
+                coupled[i + side] = jnp.where(lane < BLOCK, part[:rows], part[rows:])
 
     def propagate(step, g):
         now = current[step]
@@ -334,7 +339,7 @@
     seeds, ancestors, migration, pattern, current, half, temper = scalars
     weights = pl.pallas_call(
         weights_kernel,
-        out_shape=shape((PAIRS, NEIGH * HALF, 2 * LANES), jnp.bfloat16),
+        out_shape=shape((BLOCKS // 4, NEIGH * BLOCK, 4 * BLOCK), jnp.bfloat16),
         in_specs=[HBM],
         out_specs=VMEM,
         scratch_shapes=[
@@ -384,10 +389,10 @@
             scratch_shapes=[
                 pltpu.VMEM((PAIRS, STATES * ROWS, LANES), jnp.float32),
                 pltpu.VMEM((PAIRS, STATES * ROWS, LANES), jnp.bfloat16),
-                pltpu.VMEM((BLOCKS, 2 * STATES * ROWS, LANES), jnp.bfloat16),
-                pltpu.VMEM((BLOCKS, 2 * STATES * ROWS, LANES), jnp.bfloat16),
+                pltpu.VMEM((BLOCKS, STATES * ROWS, LANES), jnp.bfloat16),
+                pltpu.VMEM((BLOCKS, STATES * ROWS, LANES), jnp.bfloat16),
                 pltpu.VMEM((GROUP, STATES * ROWS, LANES), jnp.float32),
-                pltpu.VMEM((LANES, 4 * LANES), jnp.bfloat16),
+                pltpu.VMEM((LANES, 2 * LANES), jnp.bfloat16),
                 pltpu.VMEM((ROWS, LANES), jnp.float32),
             ],
             compiler_params=params(12),

time: 36.4 us -> 33.9 us (0.931)
  Pallas kernels: 23.5 us -> 21.5 us
    pallas_call x2, Pallas kernels: 12.2 us -> 9.48 us  [on_device(): pl.pallas_call(functools.partial(epoch_kernel, epoch), out_shape=(shape((...]
    pallas_call x1, Pallas kernels: 5.19 us -> 5.92 us  [on_device(): pl.pallas_call(weights_kernel, out_shape=shape((BLOCKS // 4, NEIGH * BLOC...]
  transfers between devices with their start and end apart: 5 -> 5, of which waited for: 2 -> 2; matrix products, arithmetic and copies ran while one was open for 0% -> 0% of each run, Pallas kernels for 27% -> 31%
where the time goes in v4:
time: 33.9 us; the launch traced here: 33.8 us
  Pallas kernels  21.5 us (63%)
  waiting for transfers between devices  6.63 us (20%)
  starting transfers between devices  4.88 us (14%)
  between operations  0.72 us (2%)
    pallas_call x2, Pallas kernels, on_device(): pl.pallas_call(functools.partial(epoch_kernel, epoch), out_shape=(shape((...  9.48 us
    pallas_call x1, Pallas kernels, on_device(): pl.pallas_call(weights_kernel, out_shape=shape((BLOCKS // 4, NEIGH * BLOC...  5.92 us
    ppermute x2, waiting for transfers between devices, from_behind(): return lax.ppermute(block, 'island', route)  5.49 us
    ppermute x2, starting transfers between devices, from_behind(): return lax.ppermute(block, 'island', route)  4.16 us
    pallas_call x1, Pallas kernels, on_device(): pl.pallas_call(first_noise_kernel, out_shape=(vector, *(pltpu.SMEM(x.shap...  2.6 us
    pallas_call x1, Pallas kernels, on_device(): pl.pallas_call(noise_kernel, out_shape=vector, in_specs=[SMEM], out_specs...  1.81 us
    ppermute x3, waiting for transfers between devices, from_partner(): return lax.ppermute(value, 'island', pairs)  1.14 us
    pallas_call x2, Pallas kernels, on_device(): pl.pallas_call(functools.partial(leaving_kernel, epoch), out_shape=shape(...  0.98 us
  transfers between devices with their start and end apart: 5, of which 2 were waited for; matrix products, arithmetic and copies ran while one was open for 0% of the time, Pallas kernels for 31%

profile of v4, /device:TPU:0, one launch (start us, length us, event | category | flops | bytes accessed | tf_op | source)
XLA Modules:
  0.0 33.8 jit_solution(4823812219470939995)
XLA Ops:
  0.6 0.5 %collective-permute-start = (bf16[8,4,8192]{2,1,0:T(4,128)(2,1)}, bf16[8,4,8192]{2,1,0:T(4,128)(2,1)S(1)}, u32[]{:S(2)}, u32[]{:S(2)}) collective-permute-start(bf16[8,4,8192]{2,1,0:T(4,128)(2,1)} %local.3), channel_id=1, source_target_pairs={{0,1},{1,0},{2,3},{3,2},{4,5},{5,4},{6,7},{7,6},{8,9},{9,8},{10,11... | collective-permute-start | bytes 1572872 | tf_op jit(solution)/shard_map/ppermute | solution.py:40
  1.1 2.6 %noise.2 = (f32[2,64,32,128]{3,2,1,0:T(8,128)S(1)}, s32[1,4]{1,0:T(1,128)S(4)}, s32[2,1,8]{2,1,0:T(1,128)S(4)}, s32[2,1,8]{2,1,0:T(1,128)S(4)}, s32[5,128]{1,0:T...) custom-call(s32[1,4]{1,0:T(1,128)} %refs_0_.1, s32[2,1,8]{2,1,0:T(1,128)} %refs_1_.1, s32[2,1,8]{2,1,0:T(1,128)} %refs_2_.1, ...), custom_call_target="tpu_custom_call" | custom-call | flops 15000000 | bytes 6000000 | tf_op jit(solution)/shard_map/noise/pallas_call | solution.py:324
  3.8 0.0 collective-permute-done.partner
  3.8 0.9 %leaving.2 = bf16[1,4,8192]{2,1,0:T(4,128)(2,1)S(1)} custom-call(s32[2,1,8]{2,1,0:T(1,128)S(4)} %get-tuple-element.21.ancestors, s32[2,1,8]{2,1,0:T(1,128)S(4)} %get-tuple-element.22.migration, s32[1]{0:T(128)S(4)} %get-tuple-element.23.half, bf16[8,4,8192]{2,1,0:T(4,128)(2,1)} %local.3, bf16[8,4,8192]{2,1,0:T(4,128)(2,1)S(1)} %collective-permute-done.partner), custom_call_target="tpu_custom_call" | custom-call | tf_op jit(solution)/shard_map/leaving/pallas_call | solution.py:371
  4.6 2.6 %collective-permute-start.1 = (bf16[1,4,8192]{2,1,0:T(4,128)(2,1)S(1)}, bf16[1,4,8192]{2,1,0:T(4,128)(2,1)S(1)}, u32[]{:S(2)}, u32[]{:S(2)}) collective-permute-start(bf16[1,4,8192]{2,1,0:T(4,128)(2,1)S(1)} %leaving.2), channel_id=1, source_target_pairs={{14,0},{15,1},{0,2},{1,3},{2,4},{3,5},{4,6},{5,7},{6,8},{7,9},{8,1... | collective-permute-start | bytes 196616 | tf_op jit(solution)/shard_map/ppermute | solution.py:46
  7.2 0.0 copy-start
  7.2 0.0 copy-start.1
  7.2 0.0 copy-start.2
  7.2 5.9 %weights.1 = bf16[32,320,256]{2,1,0:T(8,128)(2,1)S(1)} custom-call(bf16[5,128,4096]{2,1,0:T(8,128)(2,1)} %bitcast.6), custom_call_target="tpu_custom_call" | custom-call | flops 3000000 | bytes 10000000 | tf_op jit(solution)/shard_map/weights/pallas_call | solution.py:340
  13.2 0.0 collective-permute-done.1.arriving
  13.2 0.0 copy-done
  13.2 0.0 copy-done.1
  13.2 0.0 copy-done.2
  13.2 4.4 %epoch.2 = (bf16[8,4,8192]{2,1,0:T(4,128)(2,1)S(1)}, f32[2,128]{1,0:T(2,128)S(1)}) custom-call(s32[2,1,8]{2,1,0:T(1,128)S(4)} %get-tuple-element.21.ancestors, s32[2,1,8]{2,1,0:T(1,128)S(4)} %get-tuple-element.22.migration, s32[1]{0:T(128)S(4)} %get-tuple-element.23.half, s32[5,128]{1,0:T(8,128)S(4)} %get-tuple-element.24.pattern, ...), custom_call_target="tpu_custom_call" | custom-call | tf_op jit(solution)/shard_map/epoch/pallas_call | solution.py:381
  17.6 0.2 collective-permute-start.2
  17.8 1.8 %noise.3 = f32[2,64,32,128]{3,2,1,0:T(8,128)S(1)} custom-call(s32[1,4]{1,0:T(1,128)S(4)} %get-tuple-element.31.seeds), custom_call_target="tpu_custom_call" | custom-call | flops 15000000 | bytes 6000000 | tf_op jit(solution)/shard_map/noise/pallas_call | solution.py:361
  19.6 0.0 collective-permute-done.2.partner
  19.7 0.1 leaving.3
  19.8 1.6 %collective-permute-start.3 = (bf16[1,4,8192]{2,1,0:T(4,128)(2,1)S(1)}, bf16[1,4,8192]{2,1,0:T(4,128)(2,1)S(1)}, u32[]{:S(2)}, u32[]{:S(2)}) collective-permute-start(bf16[1,4,8192]{2,1,0:T(4,128)(2,1)S(1)} %leaving.3), channel_id=1, source_target_pairs={{14,0},{15,1},{0,2},{1,3},{2,4},{3,5},{4,6},{5,7},{6,8},{7,9},{8,1... | collective-permute-start | bytes 196616 | tf_op jit(solution)/shard_map/ppermute | solution.py:46
  21.4 5.5 %collective-permute-done.3.arriving = bf16[1,4,8192]{2,1,0:T(4,128)(2,1)S(1)} collective-permute-done((bf16[1,4,8192]{2,1,0:T(4,128)(2,1)S(1)}, bf16[1,4,8192]{2,1,0:T(4,128)(2,1)S(1)}, u32[]{:S(2)}, u32[]{:S(2)}) %collective-permute-start.3) | collective-permute-done | bytes 65568 | tf_op jit(solution)/shard_map/ppermute | solution.py:46
  26.8 5.1 %epoch.3 = (bf16[8,4,8192]{2,1,0:T(4,128)(2,1)}, f32[2,128]{1,0:T(2,128)S(1)}) custom-call(s32[2,1,8]{2,1,0:T(1,128)S(4)} %get-tuple-element.21.ancestors, s32[2,1,8]{2,1,0:T(1,128)S(4)} %get-tuple-element.22.migration, s32[1]{0:T(128)S(4)} %get-tuple-element.23.half, s32[5,128]{1,0:T(8,128)S(4)} %get-tuple-element.24.pattern, ...), custom_call_target="tpu_custom_call" | custom-call | tf_op jit(solution)/shard_map/epoch/pallas_call | solution.py:381
  31.9 0.0 collective-permute-start.4
  31.9 1.1 %collective-permute-done.4.other = f32[2,128]{1,0:T(2,128)S(1)} collective-permute-done((f32[2,128]{1,0:T(2,128)S(1)}, f32[2,128]{1,0:T(2,128)S(1)}, u32[]{:S(2)}, u32[]{:S(2)}) %collective-permute-start.4) | collective-permute-done | bytes 1056 | tf_op jit(solution)/shard_map/ppermute | solution.py:40
  33.0 0.7 %weigh.1 = (f32[2,8]{1,0:T(2,128)}, f32[1,1]{1,0:T(1,128)}) custom-call(f32[2,128]{1,0:T(2,128)S(1)} %get-tuple-element.36.own, f32[2,128]{1,0:T(2,128)S(1)} %collective-permute-done.4.other), custom_call_target="tpu_custom_call" | custom-call | tf_op jit(solution)/shard_map/weigh/pallas_call | solution.py:416
Async XLA Ops:
  0.6 3.1 %collective-permute-start = (bf16[8,4,8192]{2,1,0:T(4,128)(2,1)}, bf16[8,4,8192]{2,1,0:T(4,128)(2,1)S(1)}, u32[]{:S(2)}, u32[]{:S(2)}) collective-permute-start(bf16[8,4,8192]{2,1,0:T(4,128)(2,1)} %local.3), channel_id=1, source_target_pairs={{0,1},{1,0},{2,3},{3,2},{4,5},{5,4},{6,7},{7,6},{8,9},{9,8},{10,11... | collective-permute-start | bytes 1572872 | tf_op jit(solution)/shard_map/ppermute | solution.py:40
  4.6 8.5 %collective-permute-start.1 = (bf16[1,4,8192]{2,1,0:T(4,128)(2,1)S(1)}, bf16[1,4,8192]{2,1,0:T(4,128)(2,1)S(1)}, u32[]{:S(2)}, u32[]{:S(2)}) collective-permute-start(bf16[1,4,8192]{2,1,0:T(4,128)(2,1)S(1)} %leaving.2), channel_id=1, source_target_pairs={{14,0},{15,1},{0,2},{1,3},{2,4},{3,5},{4,6},{5,7},{6,8},{7,9},{8,1... | collective-permute-start | bytes 196616 | tf_op jit(solution)/shard_map/ppermute | solution.py:46
  7.2 5.9 %copy-start = (bf16[8,4,8192]{2,1,0:T(4,128)(2,1)S(1)}, bf16[8,4,8192]{2,1,0:T(4,128)(2,1)}, u32[]{:S(2)}) copy-start(bf16[8,4,8192]{2,1,0:T(4,128)(2,1)} %local.3) | copy-start | bytes 1572868
  7.2 6.0 %copy-start.1 = (f32[4,8192]{1,0:T(4,128)S(1)}, f32[4,8192]{1,0:T(4,128)}, u32[]{:S(2)}) copy-start(f32[4,8192]{1,0:T(4,128)} %observed.3) | copy-start | bytes 393220
  7.2 6.0 %copy-start.2 = (f32[8192]{0:T(1024)S(1)}, f32[8192]{0:T(1024)}, u32[]{:S(2)}) copy-start(f32[8192]{0:T(1024)} %param.14) | copy-start | bytes 98308
  17.6 2.0 %collective-permute-start.2 = (bf16[8,4,8192]{2,1,0:T(4,128)(2,1)S(1)}, bf16[8,4,8192]{2,1,0:T(4,128)(2,1)S(1)}, u32[]{:S(2)}, u32[]{:S(2)}) collective-permute-start(bf16[8,4,8192]{2,1,0:T(4,128)(2,1)S(1)} %get-tuple-element.30.local), channel_id=1, source_target_pairs={{0,1},{1,0},{2,3},{3,2},{4,5},{5,4},{6,7},{7,6},{8,9},{9,8},{10,11... | collective-permute-start | bytes 1572872 | tf_op jit(solution)/shard_map/ppermute | solution.py:40
  19.8 7.1 %collective-permute-start.3 = (bf16[1,4,8192]{2,1,0:T(4,128)(2,1)S(1)}, bf16[1,4,8192]{2,1,0:T(4,128)(2,1)S(1)}, u32[]{:S(2)}, u32[]{:S(2)}) collective-permute-start(bf16[1,4,8192]{2,1,0:T(4,128)(2,1)S(1)} %leaving.3), channel_id=1, source_target_pairs={{14,0},{15,1},{0,2},{1,3},{2,4},{3,5},{4,6},{5,7},{6,8},{7,9},{8,1... | collective-permute-start | bytes 196616 | tf_op jit(solution)/shard_map/ppermute | solution.py:46
  31.9 1.1 %collective-permute-start.4 = (f32[2,128]{1,0:T(2,128)S(1)}, f32[2,128]{1,0:T(2,128)S(1)}, u32[]{:S(2)}, u32[]{:S(2)}) collective-permute-start(f32[2,128]{1,0:T(2,128)S(1)} %get-tuple-element.36.own), channel_id=1, source_target_pairs={{0,1},{1,0},{2,3},{3,2},{4,5},{5,4},{6,7},{7,6},{8,9},{9,8},{10,11... | collective-permute-start | bytes 3080 | tf_op jit(solution)/shard_map/ppermute | solution.py:40

commit v5 on v4

--- a/solution.py
+++ b/solution.py
@@ -17,6 +17,7 @@
 BLOCKS = 128
 ROWS = 8
 LANES = 128
+TURNS = 2
 GROUP = 16
 PAIRS = CELLS // LANES
 HALF = BLOCK // 2
@@ -70,8 +71,8 @@
     lax.fori_loop(0, PAIRS, one, 0, unroll=4)
 
 
-def first_noise_kernel(*refs):
-    sources, out, targets, (half, temper, sems) = refs[:5], refs[5], refs[6:11], refs[11:]
+def first_kernel(*refs):
+    sources, out, targets, (half, temper, sems) = refs[:7], refs[7], refs[8:15], refs[15:]
     copies = [
         pltpu.make_async_copy(source, target, sems.at[i])
         for i, (source, target) in enumerate(zip(sources, targets))
@@ -81,10 +82,12 @@
     position = lax.axis_index("island")
     half[0] = position & 1
     temper[0] = 0.25 * lax.shift_left(jnp.int32(1), (position >> 1) & 3).astype(jnp.float32)
-    for copy in copies:
+    for copy in copies[:5]:
         copy.wait()
     for step in range(STEPS_EPOCH):
         draw(step, targets[0][0, step], out)
+    for copy in copies[5:]:
+        copy.wait()
 
 
 def noise_kernel(seeds, out):
@@ -92,36 +95,32 @@
         draw(step, seeds[0, STEPS_EPOCH + step], out)
 
 
-def weights_kernel(coupling, out, held, wide, sems):
+def weights_kernel(coupling, out, wide):
     group = 16
     lane = lax.broadcasted_iota(jnp.int32, (1, LANES), 1)
 
-    def fetch(g):
-        rows = pl.ds(pl.multiple_of(g * group, group), group)
-        return pltpu.make_async_copy(coupling.at[:, rows], held.at[:, rows], sems.at[g])
-
-    for g in range(BLOCKS // group):
-        fetch(g).start()
-
-    def one(g, carry):
-        fetch(g).wait()
-        for k in range(NEIGH):
-            for r in range(HALF):
-                wide[k, r * group : (r + 1) * group, :] = held[
-                    k, pl.ds(pl.multiple_of(g * group, group), group), r * LANES : (r + 1) * LANES
-                ].astype(jnp.float32)
-            for b in range(0, group, 2):
-                left, right = (wide[k, pl.ds(b + d, HALF, stride=group), :] for d in range(2))
-                across = pltpu.roll(jnp.where(lane < BLOCK, right, left), BLOCK, 1)
-                even, odd = jnp.where(lane < BLOCK, left, across), jnp.where(lane < BLOCK, across, right)
-                out[
-                    g * (group // 4) + b // 4,
-                    k * BLOCK : (k + 1) * BLOCK,
-                    (b // 2 % 2) * LANES : (b // 2 % 2 + 1) * LANES,
-                ] = jnp.concatenate([even, odd], axis=0).astype(jnp.bfloat16)
+    def move(g, k, held):
+        for r in range(HALF):
+            wide[held, r * group : (r + 1) * group, :] = coupling[
+                k, pl.ds(pl.multiple_of(g * group, group), group), r * LANES : (r + 1) * LANES
+            ].astype(jnp.float32)
+        for b in range(0, group, 2):
+            left, right = (wide[held, pl.ds(b + d, HALF, stride=group), :] for d in range(2))
+            across = pltpu.roll(jnp.where(lane < BLOCK, right, left), BLOCK, 1)
+            even, odd = jnp.where(lane < BLOCK, left, across), jnp.where(lane < BLOCK, across, right)
+            out[
+                g * (group // 4) + b // 4,
+                k * BLOCK : (k + 1) * BLOCK,
+                (b // 2 % 2) * LANES : (b // 2 % 2 + 1) * LANES,
+            ] = jnp.concatenate([even, odd], axis=0).astype(jnp.bfloat16)
+
+    def one(at, carry):
+        for d in range(TURNS):
+            for k in range(NEIGH):
+                move(TURNS * at + d, k, d * NEIGH + k)
         return carry
 
-    lax.fori_loop(0, BLOCKS // group, one, 0)
+    lax.fori_loop(0, BLOCKS // group // TURNS, one, 0)
 
 
 def leaving_kernel(epoch, ancestors, migration, half, local, partner, out, sem):
@@ -320,39 +319,34 @@
     vector = shape((STEPS_EPOCH, PAIRS, STATES * ROWS, LANES), jnp.float32)
     cost = pl.CostEstimate(flops=15000000, bytes_accessed=6000000, transcendentals=0)
     partner = from_partner(particles)
-    scalars = (noise_seeds, ancestors, migration, pattern.T, current)
-    noise, *scalars = pl.pallas_call(
-        first_noise_kernel,
+    sources = (noise_seeds, ancestors, migration, pattern.T, current, particles, coupling.transpose(1, 0, 2))
+    noise, seeds, ancestors, migration, pattern, current, states, coupling, half, temper = pl.pallas_call(
+        first_kernel,
         out_shape=(
             vector,
-            *(pltpu.SMEM(x.shape, x.dtype) for x in scalars),
+            *(pltpu.SMEM(x.shape, x.dtype) for x in sources[:5]),
+            *(shape(x.shape, x.dtype) for x in sources[5:]),
             pltpu.SMEM((1,), jnp.int32),
             pltpu.SMEM((1,), jnp.float32),
         ),
-        in_specs=[HBM] * 5,
-        out_specs=(VMEM, *[SMEM] * 7),
-        scratch_shapes=[pltpu.SemaphoreType.DMA((5,))],
+        in_specs=[HBM] * 7,
+        out_specs=(VMEM, *[SMEM] * 5, VMEM, VMEM, SMEM, SMEM),
+        scratch_shapes=[pltpu.SemaphoreType.DMA((7,))],
         compiler_params=params(2),
         cost_estimate=cost,
-        name="noise",
-    )(*(in_hbm(x) for x in scalars))
-    seeds, ancestors, migration, pattern, current, half, temper = scalars
+        name="first",
+    )(*(in_hbm(x) for x in sources))
     weights = pl.pallas_call(
         weights_kernel,
         out_shape=shape((BLOCKS // 4, NEIGH * BLOCK, 4 * BLOCK), jnp.bfloat16),
-        in_specs=[HBM],
+        in_specs=[VMEM],
         out_specs=VMEM,
-        scratch_shapes=[
-            pltpu.VMEM((NEIGH, BLOCKS, BLOCK * BLOCK), jnp.bfloat16),
-            pltpu.VMEM((NEIGH, HALF * 16, LANES), jnp.float32),
-            pltpu.SemaphoreType.DMA((BLOCKS // 16,)),
-        ],
-        compiler_params=params(10),
+        scratch_shapes=[pltpu.VMEM((TURNS * NEIGH, HALF * 16, LANES), jnp.float32)],
+        compiler_params=params(6),
         cost_estimate=pl.CostEstimate(flops=3000000, bytes_accessed=10000000, transcendentals=0),
         name="weights",
-    )(in_hbm(coupling.transpose(1, 0, 2)))
-
-    states = particles
+    )(coupling)
+
     logliks = ()
     rates = cell_rate.reshape(PAIRS, LANES)
     for epoch in range(EPOCHS):
@@ -376,7 +370,7 @@
             scratch_shapes=[pltpu.SemaphoreType.DMA],
             compiler_params=params(1),
             name="leaving",
-        )(ancestors, migration, half, states if epoch else in_hbm(states), partner)
+        )(ancestors, migration, half, states, partner)
         arriving = from_behind(leaving)
         states, logliks = pl.pallas_call(
             functools.partial(epoch_kernel, epoch),

time: 33.9 us -> 33.1 us (0.976)
  waiting for transfers between devices: 6.63 us -> 9.2 us
  Pallas kernels: 21.5 us -> 19.4 us
  starting transfers between devices: 4.88 us -> 3.63 us
    ppermute x2, waiting for transfers between devices: 5.49 us -> 7.97 us  [from_behind(): return lax.ppermute(block, 'island', route)]
    pallas_call x1, Pallas kernels: 5.92 us -> 4.51 us  [on_device(): pl.pallas_call(weights_kernel, out_shape=shape((BLOCKS // 4, NEIGH * BLOC...]
    ppermute x2, starting transfers between devices: 4.16 us -> 3.1 us  [from_behind(): return lax.ppermute(block, 'island', route)]
    pallas_call x2, Pallas kernels: 0.98 us -> 0.19 us  [on_device(): pl.pallas_call(functools.partial(leaving_kernel, epoch), out_shape=shape(...]
  transfers between devices with their start and end apart: 5 -> 5, of which waited for: 2 -> 4; matrix products, arithmetic and copies ran while one was open for 0% -> 0% of each run, Pallas kernels for 31% -> 27%
where the time goes in v5:
time: 33.1 us; the launch traced here: 33 us
  Pallas kernels  19.4 us (59%)
  waiting for transfers between devices  9.2 us (28%)
  starting transfers between devices  3.63 us (11%)
  between operations  0.68 us (2%)
    pallas_call x2, Pallas kernels, on_device(): pl.pallas_call(functools.partial(epoch_kernel, epoch), out_shape=(shape((...  9.46 us
    ppermute x2, waiting for transfers between devices, from_behind(): return lax.ppermute(block, 'island', route)  7.97 us
    pallas_call x1, Pallas kernels, on_device(): pl.pallas_call(weights_kernel, out_shape=shape((BLOCKS // 4, NEIGH * BLOC...  4.51 us
    ppermute x2, starting transfers between devices, from_behind(): return lax.ppermute(block, 'island', route)  3.1 us
    pallas_call x1, Pallas kernels, on_device(): pl.pallas_call(first_kernel, out_shape=(vector, *(pltpu.SMEM(x.shape, x.d...  2.72 us
    pallas_call x1, Pallas kernels, on_device(): pl.pallas_call(noise_kernel, out_shape=vector, in_specs=[SMEM], out_specs...  1.81 us
    ppermute x3, waiting for transfers between devices, from_partner(): return lax.ppermute(value, 'island', pairs)  1.23 us
    pallas_call x1, Pallas kernels, on_device(): pl.pallas_call(weigh_kernel, out_shape=(shape((EPOCHS, ROWS), jnp.float32...  0.74 us
  transfers between devices with their start and end apart: 5, of which 4 were waited for; matrix products, arithmetic and copies ran while one was open for 0% of the time, Pallas kernels for 27%

profile of v5, /device:TPU:0, one launch (start us, length us, event | category | flops | bytes accessed | tf_op | source)
XLA Modules:
  0.0 33.0 jit_solution(15819938421051730307)
XLA Ops:
  0.6 0.5 %collective-permute-start = (bf16[8,4,8192]{2,1,0:T(4,128)(2,1)}, bf16[8,4,8192]{2,1,0:T(4,128)(2,1)S(1)}, u32[]{:S(2)}, u32[]{:S(2)}) collective-permute-start(bf16[8,4,8192]{2,1,0:T(4,128)(2,1)} %refs_5_.1), channel_id=1, source_target_pairs={{0,1},{1,0},{2,3},{3,2},{4,5},{5,4},{6,7},{7,6},{8,9},{9,8},{10,11... | collective-permute-start | bytes 1572872 | tf_op jit(solution)/shard_map/ppermute | solution.py:41
  1.2 2.7 %first.1 = (f32[2,64,32,128]{3,2,1,0:T(8,128)S(1)}, s32[1,4]{1,0:T(1,128)S(4)}, s32[2,1,8]{2,1,0:T(1,128)S(4)}, s32[2,1,8]{2,1,0:T(1,128)S(4)}, s32[5,128]{1,0:T...) custom-call(s32[1,4]{1,0:T(1,128)} %refs_0_.1, ...), custom_call_target="tpu_custom_call" | custom-call | flops 15000000 | bytes 6000000 | tf_op jit(solution)/shard_map/first/pallas_call | solution.py:323
  3.9 0.0 collective-permute-done.partner
  3.9 0.1 leaving.2
  4.0 2.6 %collective-permute-start.1 = (bf16[1,4,8192]{2,1,0:T(4,128)(2,1)S(1)}, bf16[1,4,8192]{2,1,0:T(4,128)(2,1)S(1)}, u32[]{:S(2)}, u32[]{:S(2)}) collective-permute-start(bf16[1,4,8192]{2,1,0:T(4,128)(2,1)S(1)} %leaving.2), channel_id=1, source_target_pairs={{14,0},{15,1},{0,2},{1,3},{2,4},{3,5},{4,6},{5,7},{6,8},{7,9},{8,1... | collective-permute-start | bytes 196616 | tf_op jit(solution)/shard_map/ppermute | solution.py:47
  6.6 0.0 copy-start
  6.6 0.0 copy-start.1
  6.6 4.5 %weights.1 = bf16[32,320,256]{2,1,0:T(8,128)(2,1)S(1)} custom-call(bf16[5,128,4096]{2,1,0:T(8,128)(2,1)S(1)} %get-tuple-element.32.coupling), custom_call_target="tpu_custom_call" | custom-call | flops 3000000 | bytes 10000000 | tf_op jit(solution)/shard_map/weights/pallas_call | solution.py:339
  11.1 1.3 %collective-permute-done.1.arriving = bf16[1,4,8192]{2,1,0:T(4,128)(2,1)S(1)} collective-permute-done((bf16[1,4,8192]{2,1,0:T(4,128)(2,1)S(1)}, bf16[1,4,8192]{2,1,0:T(4,128)(2,1)S(1)}, u32[]{:S(2)}, u32[]{:S(2)}) %collective-permute-start.1) | collective-permute-done | bytes 65568 | tf_op jit(solution)/shard_map/ppermute | solution.py:47
  12.4 0.0 copy-done
  12.4 0.0 copy-done.1
  12.4 4.4 %epoch.2 = (bf16[8,4,8192]{2,1,0:T(4,128)(2,1)S(1)}, f32[2,128]{1,0:T(2,128)S(1)}) custom-call(s32[2,1,8]{2,1,0:T(1,128)S(4)} %get-tuple-element.23.ancestors, s32[2,1,8]{2,1,0:T(1,128)S(4)} %get-tuple-element.24.migration, s32[1]{0:T(128)S(4)} %get-tuple-element.25.half, s32[5,128]{1,0:T(8,128)S(4)} %get-tuple-element.26.pattern, ...), custom_call_target="tpu_custom_call" | custom-call | tf_op jit(solution)/shard_map/epoch/pallas_call | solution.py:375
  16.8 0.0 collective-permute-start.2
  16.8 1.8 %noise.1 = f32[2,64,32,128]{3,2,1,0:T(8,128)S(1)} custom-call(s32[1,4]{1,0:T(1,128)S(4)} %get-tuple-element.35.seeds), custom_call_target="tpu_custom_call" | custom-call | flops 15000000 | bytes 6000000 | tf_op jit(solution)/shard_map/noise/pallas_call | solution.py:355
  18.6 0.1 collective-permute-done.2.partner
  18.7 0.1 leaving.3
  18.8 0.5 %collective-permute-start.3 = (bf16[1,4,8192]{2,1,0:T(4,128)(2,1)S(1)}, bf16[1,4,8192]{2,1,0:T(4,128)(2,1)S(1)}, u32[]{:S(2)}, u32[]{:S(2)}) collective-permute-start(bf16[1,4,8192]{2,1,0:T(4,128)(2,1)S(1)} %leaving.3), channel_id=1, source_target_pairs={{14,0},{15,1},{0,2},{1,3},{2,4},{3,5},{4,6},{5,7},{6,8},{7,9},{8,1... | collective-permute-start | bytes 196616 | tf_op jit(solution)/shard_map/ppermute | solution.py:47
  19.3 6.7 %collective-permute-done.3.arriving = bf16[1,4,8192]{2,1,0:T(4,128)(2,1)S(1)} collective-permute-done((bf16[1,4,8192]{2,1,0:T(4,128)(2,1)S(1)}, bf16[1,4,8192]{2,1,0:T(4,128)(2,1)S(1)}, u32[]{:S(2)}, u32[]{:S(2)}) %collective-permute-start.3) | collective-permute-done | bytes 65568 | tf_op jit(solution)/shard_map/ppermute | solution.py:47
  26.0 5.1 %epoch.3 = (bf16[8,4,8192]{2,1,0:T(4,128)(2,1)}, f32[2,128]{1,0:T(2,128)S(1)}) custom-call(s32[2,1,8]{2,1,0:T(1,128)S(4)} %get-tuple-element.23.ancestors, s32[2,1,8]{2,1,0:T(1,128)S(4)} %get-tuple-element.24.migration, s32[1]{0:T(128)S(4)} %get-tuple-element.25.half, s32[5,128]{1,0:T(8,128)S(4)} %get-tuple-element.26.pattern, ...), custom_call_target="tpu_custom_call" | custom-call | tf_op jit(solution)/shard_map/epoch/pallas_call | solution.py:375
  31.1 0.0 collective-permute-start.4
  31.1 1.1 %collective-permute-done.4.other = f32[2,128]{1,0:T(2,128)S(1)} collective-permute-done((f32[2,128]{1,0:T(2,128)S(1)}, f32[2,128]{1,0:T(2,128)S(1)}, u32[]{:S(2)}, u32[]{:S(2)}) %collective-permute-start.4) | collective-permute-done | bytes 1056 | tf_op jit(solution)/shard_map/ppermute | solution.py:41
  32.2 0.7 %weigh.1 = (f32[2,8]{1,0:T(2,128)}, f32[1,1]{1,0:T(1,128)}) custom-call(f32[2,128]{1,0:T(2,128)S(1)} %get-tuple-element.40.own, f32[2,128]{1,0:T(2,128)S(1)} %collective-permute-done.4.other), custom_call_target="tpu_custom_call" | custom-call | tf_op jit(solution)/shard_map/weigh/pallas_call | solution.py:410
Async XLA Ops:
  0.6 3.3 %collective-permute-start = (bf16[8,4,8192]{2,1,0:T(4,128)(2,1)}, bf16[8,4,8192]{2,1,0:T(4,128)(2,1)S(1)}, u32[]{:S(2)}, u32[]{:S(2)}) collective-permute-start(bf16[8,4,8192]{2,1,0:T(4,128)(2,1)} %refs_5_.1), channel_id=1, source_target_pairs={{0,1},{1,0},{2,3},{3,2},{4,5},{5,4},{6,7},{7,6},{8,9},{9,8},{10,11... | collective-permute-start | bytes 1572872 | tf_op jit(solution)/shard_map/ppermute | solution.py:41
  4.0 8.4 %collective-permute-start.1 = (bf16[1,4,8192]{2,1,0:T(4,128)(2,1)S(1)}, bf16[1,4,8192]{2,1,0:T(4,128)(2,1)S(1)}, u32[]{:S(2)}, u32[]{:S(2)}) collective-permute-start(bf16[1,4,8192]{2,1,0:T(4,128)(2,1)S(1)} %leaving.2), channel_id=1, source_target_pairs={{14,0},{15,1},{0,2},{1,3},{2,4},{3,5},{4,6},{5,7},{6,8},{7,9},{8,1... | collective-permute-start | bytes 196616 | tf_op jit(solution)/shard_map/ppermute | solution.py:47
  6.6 5.8 %copy-start = (f32[4,8192]{1,0:T(4,128)S(1)}, f32[4,8192]{1,0:T(4,128)}, u32[]{:S(2)}) copy-start(f32[4,8192]{1,0:T(4,128)} %observed.3) | copy-start | bytes 393220
  6.6 5.8 %copy-start.1 = (f32[8192]{0:T(1024)S(1)}, f32[8192]{0:T(1024)}, u32[]{:S(2)}) copy-start(f32[8192]{0:T(1024)} %param.14) | copy-start | bytes 98308
  16.8 1.9 %collective-permute-start.2 = (bf16[8,4,8192]{2,1,0:T(4,128)(2,1)S(1)}, bf16[8,4,8192]{2,1,0:T(4,128)(2,1)S(1)}, u32[]{:S(2)}, u32[]{:S(2)}) collective-permute-start(bf16[8,4,8192]{2,1,0:T(4,128)(2,1)S(1)} %get-tuple-element.34.local), channel_id=1, source_target_pairs={{0,1},{1,0},{2,3},{3,2},{4,5},{5,4},{6,7},{7,6},{8,9},{9,8},{10,11... | collective-permute-start | bytes 1572872 | tf_op jit(solution)/shard_map/ppermute | solution.py:41
  18.8 7.2 %collective-permute-start.3 = (bf16[1,4,8192]{2,1,0:T(4,128)(2,1)S(1)}, bf16[1,4,8192]{2,1,0:T(4,128)(2,1)S(1)}, u32[]{:S(2)}, u32[]{:S(2)}) collective-permute-start(bf16[1,4,8192]{2,1,0:T(4,128)(2,1)S(1)} %leaving.3), channel_id=1, source_target_pairs={{14,0},{15,1},{0,2},{1,3},{2,4},{3,5},{4,6},{5,7},{6,8},{7,9},{8,1... | collective-permute-start | bytes 196616 | tf_op jit(solution)/shard_map/ppermute | solution.py:47
  31.1 1.1 %collective-permute-start.4 = (f32[2,128]{1,0:T(2,128)S(1)}, f32[2,128]{1,0:T(2,128)S(1)}, u32[]{:S(2)}, u32[]{:S(2)}) collective-permute-start(f32[2,128]{1,0:T(2,128)S(1)} %get-tuple-element.40.own), channel_id=1, source_target_pairs={{0,1},{1,0},{2,3},{3,2},{4,5},{5,4},{6,7},{7,6},{8,9},{9,8},{10,11... | collective-permute-start | bytes 3080 | tf_op jit(solution)/shard_map/ppermute | solution.py:41

commit v6 on v5

--- a/solution.py
+++ b/solution.py
@@ -57,7 +57,7 @@
     return shifted(hashed) & 16777215
 
 
-def draw(step, seed, out):
+def draw(seed, out):
     row = lax.broadcasted_iota(jnp.int32, (STATES * ROWS, LANES), 0)
     lane = lax.broadcasted_iota(jnp.int32, (STATES * ROWS, LANES), 1)
     start = 2 * (((row % ROWS) * STATES + row // ROWS) * CELLS + lane) + seed * 40503
@@ -65,7 +65,7 @@
     def one(q, carry):
         anchor = start + q * (2 * LANES)
         apart = scramble(anchor) - scramble(anchor + 1)
-        out[step, q] = apart.astype(jnp.float32) * NOISE_SCALE
+        out[q] = apart.astype(jnp.float32) * NOISE_SCALE
         return carry
 
     lax.fori_loop(0, PAIRS, one, 0, unroll=4)
@@ -73,6 +73,7 @@
 
 def first_kernel(*refs):
     sources, out, targets, (half, temper, sems) = refs[:7], refs[7], refs[8:15], refs[15:]
+    sources = (*sources[:6], sources[6].at[:, : BLOCKS // 2])
     copies = [
         pltpu.make_async_copy(source, target, sems.at[i])
         for i, (source, target) in enumerate(zip(sources, targets))
@@ -84,25 +85,31 @@
     temper[0] = 0.25 * lax.shift_left(jnp.int32(1), (position >> 1) & 3).astype(jnp.float32)
     for copy in copies[:5]:
         copy.wait()
-    for step in range(STEPS_EPOCH):
-        draw(step, targets[0][0, step], out)
+    draw(targets[0][0, 0], out)
     for copy in copies[5:]:
         copy.wait()
 
 
-def noise_kernel(seeds, out):
-    for step in range(STEPS_EPOCH):
-        draw(step, seeds[0, STEPS_EPOCH + step], out)
-
-
-def weights_kernel(coupling, out, wide):
+def second_kernel(seeds, coupling, out, target, sem):
+    copy = pltpu.make_async_copy(coupling.at[:, BLOCKS // 2 :], target, sem)
+    copy.start()
+    draw(seeds[0, 1], out)
+    copy.wait()
+
+
+def noise_kernel(seeds, *outs):
+    for step, out in enumerate(outs):
+        draw(seeds[0, STEPS_EPOCH + step], out)
+
+
+def weights_kernel(front, back, out, wide):
     group = 16
     lane = lax.broadcasted_iota(jnp.int32, (1, LANES), 1)
 
-    def move(g, k, held):
+    def move(coupling, g, local_g, k, held):
         for r in range(HALF):
             wide[held, r * group : (r + 1) * group, :] = coupling[
-                k, pl.ds(pl.multiple_of(g * group, group), group), r * LANES : (r + 1) * LANES
+                k, pl.ds(pl.multiple_of(local_g * group, group), group), r * LANES : (r + 1) * LANES
             ].astype(jnp.float32)
         for b in range(0, group, 2):
             left, right = (wide[held, pl.ds(b + d, HALF, stride=group), :] for d in range(2))
@@ -114,13 +121,17 @@
                 (b // 2 % 2) * LANES : (b // 2 % 2 + 1) * LANES,
             ] = jnp.concatenate([even, odd], axis=0).astype(jnp.bfloat16)
 
-    def one(at, carry):
-        for d in range(TURNS):
-            for k in range(NEIGH):
-                move(TURNS * at + d, k, d * NEIGH + k)
-        return carry
-
-    lax.fori_loop(0, BLOCKS // group // TURNS, one, 0)
+    groups = BLOCKS // 2 // group
+    for part, coupling in enumerate((front, back)):
+
+        def one(at, carry, part=part, coupling=coupling):
+            for d in range(TURNS):
+                g = TURNS * at + d
+                for k in range(NEIGH):
+                    move(coupling, part * groups + g, g, k, d * NEIGH + k)
+            return carry
+
+        lax.fori_loop(0, groups // TURNS, one, 0)
 
 
 def leaving_kernel(epoch, ancestors, migration, half, local, partner, out, sem):
@@ -176,7 +187,8 @@
     partner,
     arriving,
     weights,
-    noise,
+    noise_first,
+    noise_second,
     cell_rate,
     observed,
     *rest,
@@ -251,7 +263,7 @@
         gained = jnp.zeros((ROWS, LANES), jnp.float32)
         for i, q in enumerate(members(g)):
             mixed = 0.6 * natural[q].astype(jnp.float32) + 0.8 * coupled[i]
-            drawn = noise[step % STEPS_EPOCH, q]
+            drawn = (noise_first, noise_second)[step % STEPS_EPOCH][q]
             charge, over, heat, film = (mixed[c * ROWS : (c + 1) * ROWS] for c in range(STATES))
             rate = cell_rate[pl.ds(q, 1), :]
             seen = observed[step : step + 1, pl.ds(pl.multiple_of(q * LANES, LANES), LANES)]
@@ -316,16 +328,19 @@
     particles, ancestors, migration, pattern, coupling, cell_rate, current, observed, noise_seeds
 ):
     shape = jax.ShapeDtypeStruct
-    vector = shape((STEPS_EPOCH, PAIRS, STATES * ROWS, LANES), jnp.float32)
+    vector = shape((PAIRS, STATES * ROWS, LANES), jnp.float32)
     cost = pl.CostEstimate(flops=15000000, bytes_accessed=6000000, transcendentals=0)
     partner = from_partner(particles)
     sources = (noise_seeds, ancestors, migration, pattern.T, current, particles, coupling.transpose(1, 0, 2))
-    noise, seeds, ancestors, migration, pattern, current, states, coupling, half, temper = pl.pallas_call(
+    halves = shape((NEIGH, BLOCKS // 2, BLOCK * BLOCK), jnp.bfloat16)
+    sources = [in_hbm(x) for x in sources]
+    noise, seeds, ancestors, migration, pattern, current, states, front, half, temper = pl.pallas_call(
         first_kernel,
         out_shape=(
             vector,
             *(pltpu.SMEM(x.shape, x.dtype) for x in sources[:5]),
-            *(shape(x.shape, x.dtype) for x in sources[5:]),
+            shape(particles.shape, particles.dtype),
+            halves,
             pltpu.SMEM((1,), jnp.int32),
             pltpu.SMEM((1,), jnp.float32),
         ),
@@ -335,17 +350,7 @@
         compiler_params=params(2),
         cost_estimate=cost,
         name="first",
-    )(*(in_hbm(x) for x in sources))
-    weights = pl.pallas_call(
-        weights_kernel,
-        out_shape=shape((BLOCKS // 4, NEIGH * BLOCK, 4 * BLOCK), jnp.bfloat16),
-        in_specs=[VMEM],
-        out_specs=VMEM,
-        scratch_shapes=[pltpu.VMEM((TURNS * NEIGH, HALF * 16, LANES), jnp.float32)],
-        compiler_params=params(6),
-        cost_estimate=pl.CostEstimate(flops=3000000, bytes_accessed=10000000, transcendentals=0),
-        name="weights",
-    )(coupling)
+    )(*sources)
 
     logliks = ()
     rates = cell_rate.reshape(PAIRS, LANES)
@@ -354,9 +359,9 @@
             partner = from_partner(states)
             noise = pl.pallas_call(
                 noise_kernel,
-                out_shape=vector,
+                out_shape=(vector, vector),
                 in_specs=[SMEM],
-                out_specs=VMEM,
+                out_specs=(VMEM, VMEM),
                 compiler_params=params(2),
                 cost_estimate=cost,
                 name="noise",
@@ -372,13 +377,36 @@
             name="leaving",
         )(ancestors, migration, half, states, partner)
         arriving = from_behind(leaving)
+        if not epoch:
+            leaving, seeds = lax.optimization_barrier((leaving, seeds))
+            later, back = pl.pallas_call(
+                second_kernel,
+                out_shape=(vector, halves),
+                in_specs=[SMEM, HBM],
+                out_specs=(VMEM, VMEM),
+                scratch_shapes=[pltpu.SemaphoreType.DMA],
+                compiler_params=params(2),
+                cost_estimate=cost,
+                name="second",
+            )(seeds, sources[6])
+            noise = (noise, later)
+            weights = pl.pallas_call(
+                weights_kernel,
+                out_shape=shape((BLOCKS // 4, NEIGH * BLOCK, 4 * BLOCK), jnp.bfloat16),
+                in_specs=[VMEM, VMEM],
+                out_specs=VMEM,
+                scratch_shapes=[pltpu.VMEM((TURNS * NEIGH, HALF * 16, LANES), jnp.float32)],
+                compiler_params=params(6),
+                cost_estimate=pl.CostEstimate(flops=3000000, bytes_accessed=10000000, transcendentals=0),
+                name="weights",
+            )(front, back)
         states, logliks = pl.pallas_call(
             functools.partial(epoch_kernel, epoch),
             out_shape=(
                 shape((ROWS, STATES, CELLS), jnp.bfloat16),
                 shape((EPOCHS, LANES), jnp.float32),
             ),
-            in_specs=[SMEM] * 6 + [VMEM] * (8 if epoch else 7),
+            in_specs=[SMEM] * 6 + [VMEM] * (9 if epoch else 8),
             out_specs=(VMEM, VMEM),
             scratch_shapes=[
                 pltpu.VMEM((PAIRS, STATES * ROWS, LANES), jnp.float32),
@@ -402,7 +430,7 @@
             partner,
             arriving,
             weights,
-            noise,
+            *noise,
             rates,
             observed,
             *([logliks] if epoch else []),

time: 33.1 us -> 33 us (level)
  waiting for transfers between devices: 9.2 us -> 6.67 us
  starting transfers between devices: 3.63 us -> 4.9 us
  Pallas kernels: 19.4 us -> 20.5 us
    ppermute x2, waiting for transfers between devices: 7.97 us -> 5.52 us  [from_behind(): return lax.ppermute(block, 'island', route)]
    pallas_call x1 -> x2, Pallas kernels: 1.81 us -> 3.56 us  [the longest x1 1.81 us: on_device(): pl.pallas_call(noise_kernel, out_shape=(vector, vector), in_specs=[SMEM],...]
    ppermute x2, starting transfers between devices: 3.1 us -> 4.21 us  [from_behind(): return lax.ppermute(block, 'island', route)]
    pallas_call x1, Pallas kernels: 2.72 us -> 1.98 us  [on_device(): pl.pallas_call(first_kernel, out_shape=(vector, *(pltpu.SMEM(x.shape, x.d...]
  transfers between devices with their start and end apart: 5 -> 5, of which waited for: 4 -> 2; matrix products, arithmetic and copies ran while one was open for 0% -> 0% of each run, Pallas kernels for 27% -> 31%
where the time goes in v6:
time: 33 us; the launch traced here: 32.8 us
  Pallas kernels  20.5 us (62%)
  waiting for transfers between devices  6.67 us (20%)
  starting transfers between devices  4.9 us (15%)
  between operations  0.73 us (2%)
    pallas_call x2, Pallas kernels, on_device(): pl.pallas_call(functools.partial(epoch_kernel, epoch), out_shape=(shape((...  9.47 us
    ppermute x2, waiting for transfers between devices, from_behind(): return lax.ppermute(block, 'island', route)  5.52 us
    pallas_call x1, Pallas kernels, on_device(): pl.pallas_call(weights_kernel, out_shape=shape((BLOCKS // 4, NEIGH * BLOC...  4.51 us
    ppermute x2, starting transfers between devices, from_behind(): return lax.ppermute(block, 'island', route)  4.21 us
    pallas_call x1, Pallas kernels, on_device(): pl.pallas_call(first_kernel, out_shape=(vector, *(pltpu.SMEM(x.shape, x.d...  1.98 us
    pallas_call x1, Pallas kernels, on_device(): pl.pallas_call(noise_kernel, out_shape=(vector, vector), in_specs=[SMEM],...  1.81 us
    pallas_call x1, Pallas kernels, on_device(): pl.pallas_call(second_kernel, out_shape=(vector, halves), in_specs=[SMEM,...  1.75 us
    ppermute x3, waiting for transfers between devices, from_partner(): return lax.ppermute(value, 'island', pairs)  1.14 us
  transfers between devices with their start and end apart: 5, of which 2 were waited for; matrix products, arithmetic and copies ran while one was open for 0% of the time, Pallas kernels for 31%

profile of v6, /device:TPU:0, one launch (start us, length us, event | category | flops | bytes accessed | tf_op | source)
XLA Modules:
  0.0 32.8 jit_solution(13752041370105941642)
XLA Ops:
  0.6 0.5 %collective-permute-start = (bf16[8,4,8192]{2,1,0:T(4,128)(2,1)}, bf16[8,4,8192]{2,1,0:T(4,128)(2,1)S(1)}, u32[]{:S(2)}, u32[]{:S(2)}) collective-permute-start(bf16[8,4,8192]{2,1,0:T(4,128)(2,1)} %refs_5_.1), channel_id=1, source_target_pairs={{0,1},{1,0},{2,3},{3,2},{4,5},{5,4},{6,7},{7,6},{8,9},{9,8},{10,11... | collective-permute-start | bytes 1572872 | tf_op jit(solution)/shard_map/ppermute | solution.py:41
  1.1 2.0 %first.1 = (f32[64,32,128]{2,1,0:T(8,128)S(1)}, s32[1,4]{1,0:T(1,128)S(4)}, s32[2,1,8]{2,1,0:T(1,128)S(4)}, s32[2,1,8]{2,1,0:T(1,128)S(4)}, s32[5,128]{1,0:T(8,1...) custom-call(s32[1,4]{1,0:T(1,128)} %refs_0_.1, ...), custom_call_target="tpu_custom_call" | custom-call | flops 15000000 | bytes 6000000 | tf_op jit(solution)/shard_map/first/pallas_call | solution.py:337
  3.1 0.0 collective-permute-done.partner
  3.1 0.1 leaving.2
  3.3 2.6 %collective-permute-start.1 = (bf16[1,4,8192]{2,1,0:T(4,128)(2,1)S(1)}, bf16[1,4,8192]{2,1,0:T(4,128)(2,1)S(1)}, u32[]{:S(2)}, u32[]{:S(2)}) collective-permute-start(bf16[1,4,8192]{2,1,0:T(4,128)(2,1)S(1)} %leaving.2), channel_id=1, source_target_pairs={{14,0},{15,1},{0,2},{1,3},{2,4},{3,5},{4,6},{5,7},{6,8},{7,9},{8,1... | collective-permute-start | bytes 196616 | tf_op jit(solution)/shard_map/ppermute | solution.py:47
  5.9 1.7 %second.1 = (f32[64,32,128]{2,1,0:T(8,128)S(1)}, bf16[5,64,4096]{2,1,0:T(8,128)(2,1)S(1)}) custom-call(s32[1,4]{1,0:T(1,128)S(4)} %get-tuple-element.40.seeds, bf16[5,128,4096]{2,1,0:T(8,128)(2,1)} %bitcast.7), custom_call_target="tpu_custom_call" | custom-call | flops 15000000 | bytes 6000000 | tf_op jit(solution)/shard_map/second/pallas_call | solution.py:382
  7.7 0.0 copy-start
  7.7 0.0 copy-start.1
  7.7 4.5 %weights.1 = bf16[32,320,256]{2,1,0:T(8,128)(2,1)S(1)} custom-call(bf16[5,64,4096]{2,1,0:T(8,128)(2,1)S(1)} %get-tuple-element.38.front, bf16[5,64,4096]{2,1,0:T(8,128)(2,1)S(1)} %get-tuple-element.41.back), custom_call_target="tpu_custom_call" | custom-call | flops 3000000 | bytes 10000000 | tf_op jit(solution)/shard_map/weights/pallas_call | solution.py:393
  12.2 0.0 collective-permute-done.1.arriving
  12.2 0.0 copy-done
  12.2 0.0 copy-done.1
  12.2 4.4 %epoch.2 = (bf16[8,4,8192]{2,1,0:T(4,128)(2,1)S(1)}, f32[2,128]{1,0:T(2,128)S(1)}) custom-call(s32[2,1,8]{2,1,0:T(1,128)S(4)} %get-tuple-element.29.ancestors, s32[2,1,8]{2,1,0:T(1,128)S(4)} %get-tuple-element.30.migration, s32[1]{0:T(128)S(4)} %get-tuple-element.31.half, s32[5,128]{1,0:T(8,128)S(4)} %get-tuple-element.32.pattern, ...), custom_call_target="tpu_custom_call" | custom-call | tf_op jit(solution)/shard_map/epoch/pallas_call | solution.py:403
  16.7 0.2 collective-permute-start.2
  16.8 1.8 %noise.1 = (f32[64,32,128]{2,1,0:T(8,128)S(1)}, f32[64,32,128]{2,1,0:T(8,128)S(1)}) custom-call(s32[1,4]{1,0:T(1,128)S(4)} %get-tuple-element.40.seeds), custom_call_target="tpu_custom_call" | custom-call | flops 15000000 | bytes 6000000 | tf_op jit(solution)/shard_map/noise/pallas_call | solution.py:360
  18.6 0.0 collective-permute-done.2.partner
  18.7 0.1 leaving.3
  18.8 1.6 %collective-permute-start.3 = (bf16[1,4,8192]{2,1,0:T(4,128)(2,1)S(1)}, bf16[1,4,8192]{2,1,0:T(4,128)(2,1)S(1)}, u32[]{:S(2)}, u32[]{:S(2)}) collective-permute-start(bf16[1,4,8192]{2,1,0:T(4,128)(2,1)S(1)} %leaving.3), channel_id=1, source_target_pairs={{14,0},{15,1},{0,2},{1,3},{2,4},{3,5},{4,6},{5,7},{6,8},{7,9},{8,1... | collective-permute-start | bytes 196616 | tf_op jit(solution)/shard_map/ppermute | solution.py:47
  20.4 5.5 %collective-permute-done.3.arriving = bf16[1,4,8192]{2,1,0:T(4,128)(2,1)S(1)} collective-permute-done((bf16[1,4,8192]{2,1,0:T(4,128)(2,1)S(1)}, bf16[1,4,8192]{2,1,0:T(4,128)(2,1)S(1)}, u32[]{:S(2)}, u32[]{:S(2)}) %collective-permute-start.3) | collective-permute-done | bytes 65568 | tf_op jit(solution)/shard_map/ppermute | solution.py:47
  25.9 5.1 %epoch.3 = (bf16[8,4,8192]{2,1,0:T(4,128)(2,1)}, f32[2,128]{1,0:T(2,128)S(1)}) custom-call(s32[2,1,8]{2,1,0:T(1,128)S(4)} %get-tuple-element.29.ancestors, s32[2,1,8]{2,1,0:T(1,128)S(4)} %get-tuple-element.30.migration, s32[1]{0:T(128)S(4)} %get-tuple-element.31.half, s32[5,128]{1,0:T(8,128)S(4)} %get-tuple-element.32.pattern, ...), custom_call_target="tpu_custom_call" | custom-call | tf_op jit(solution)/shard_map/epoch/pallas_call | solution.py:403
  30.9 0.0 collective-permute-start.4
  30.9 1.1 %collective-permute-done.4.other = f32[2,128]{1,0:T(2,128)S(1)} collective-permute-done((f32[2,128]{1,0:T(2,128)S(1)}, f32[2,128]{1,0:T(2,128)S(1)}, u32[]{:S(2)}, u32[]{:S(2)}) %collective-permute-start.4) | collective-permute-done | bytes 1056 | tf_op jit(solution)/shard_map/ppermute | solution.py:41
  32.1 0.7 %weigh.1 = (f32[2,8]{1,0:T(2,128)}, f32[1,1]{1,0:T(1,128)}) custom-call(f32[2,128]{1,0:T(2,128)S(1)} %get-tuple-element.52.own, f32[2,128]{1,0:T(2,128)S(1)} %collective-permute-done.4.other), custom_call_target="tpu_custom_call" | custom-call | tf_op jit(solution)/shard_map/weigh/pallas_call | solution.py:438
Async XLA Ops:
  0.6 2.5 %collective-permute-start = (bf16[8,4,8192]{2,1,0:T(4,128)(2,1)}, bf16[8,4,8192]{2,1,0:T(4,128)(2,1)S(1)}, u32[]{:S(2)}, u32[]{:S(2)}) collective-permute-start(bf16[8,4,8192]{2,1,0:T(4,128)(2,1)} %refs_5_.1), channel_id=1, source_target_pairs={{0,1},{1,0},{2,3},{3,2},{4,5},{5,4},{6,7},{7,6},{8,9},{9,8},{10,11... | collective-permute-start | bytes 1572872 | tf_op jit(solution)/shard_map/ppermute | solution.py:41
  3.3 8.9 %collective-permute-start.1 = (bf16[1,4,8192]{2,1,0:T(4,128)(2,1)S(1)}, bf16[1,4,8192]{2,1,0:T(4,128)(2,1)S(1)}, u32[]{:S(2)}, u32[]{:S(2)}) collective-permute-start(bf16[1,4,8192]{2,1,0:T(4,128)(2,1)S(1)} %leaving.2), channel_id=1, source_target_pairs={{14,0},{15,1},{0,2},{1,3},{2,4},{3,5},{4,6},{5,7},{6,8},{7,9},{8,1... | collective-permute-start | bytes 196616 | tf_op jit(solution)/shard_map/ppermute | solution.py:47
  7.7 4.5 %copy-start = (f32[4,8192]{1,0:T(4,128)S(1)}, f32[4,8192]{1,0:T(4,128)}, u32[]{:S(2)}) copy-start(f32[4,8192]{1,0:T(4,128)} %observed.3) | copy-start | bytes 393220
  7.7 4.5 %copy-start.1 = (f32[8192]{0:T(1024)S(1)}, f32[8192]{0:T(1024)}, u32[]{:S(2)}) copy-start(f32[8192]{0:T(1024)} %param.14) | copy-start | bytes 98308
  16.7 2.0 %collective-permute-start.2 = (bf16[8,4,8192]{2,1,0:T(4,128)(2,1)S(1)}, bf16[8,4,8192]{2,1,0:T(4,128)(2,1)S(1)}, u32[]{:S(2)}, u32[]{:S(2)}) collective-permute-start(bf16[8,4,8192]{2,1,0:T(4,128)(2,1)S(1)} %get-tuple-element.44.local), channel_id=1, source_target_pairs={{0,1},{1,0},{2,3},{3,2},{4,5},{5,4},{6,7},{7,6},{8,9},{9,8},{10,11... | collective-permute-start | bytes 1572872 | tf_op jit(solution)/shard_map/ppermute | solution.py:41
  18.8 7.1 %collective-permute-start.3 = (bf16[1,4,8192]{2,1,0:T(4,128)(2,1)S(1)}, bf16[1,4,8192]{2,1,0:T(4,128)(2,1)S(1)}, u32[]{:S(2)}, u32[]{:S(2)}) collective-permute-start(bf16[1,4,8192]{2,1,0:T(4,128)(2,1)S(1)} %leaving.3), channel_id=1, source_target_pairs={{14,0},{15,1},{0,2},{1,3},{2,4},{3,5},{4,6},{5,7},{6,8},{7,9},{8,1... | collective-permute-start | bytes 196616 | tf_op jit(solution)/shard_map/ppermute | solution.py:47
  30.9 1.1 %collective-permute-start.4 = (f32[2,128]{1,0:T(2,128)S(1)}, f32[2,128]{1,0:T(2,128)S(1)}, u32[]{:S(2)}, u32[]{:S(2)}) collective-permute-start(f32[2,128]{1,0:T(2,128)S(1)} %get-tuple-element.52.own), channel_id=1, source_target_pairs={{0,1},{1,0},{2,3},{3,2},{4,5},{5,4},{6,7},{7,6},{8,9},{9,8},{10,11... | collective-permute-start | bytes 3080 | tf_op jit(solution)/shard_map/ppermute | solution.py:41

commit v7 on v6

--- a/solution.py
+++ b/solution.py
@@ -65,7 +65,8 @@
     def one(q, carry):
         anchor = start + q * (2 * LANES)
         apart = scramble(anchor) - scramble(anchor + 1)
-        out[q] = apart.astype(jnp.float32) * NOISE_SCALE
+        rows = STATES * ROWS
+        out[pl.ds(pl.multiple_of(q * rows, rows), rows), :] = apart.astype(jnp.float32) * NOISE_SCALE
         return carry
 
     lax.fori_loop(0, PAIRS, one, 0, unroll=4)
@@ -152,6 +153,40 @@
         copy.wait()
 
 
+def advance(mixed, drawn, rate, seen, now):
+    charge, over, heat, film = mixed
+    tanh_over = jnp.tanh(over)
+    fade = jnp.exp(-0.5 * jnp.abs(charge))
+    warm = 0.6 * jnp.tanh(heat)
+    rise = jnp.exp(warm + 2.0 * tanh_over) - jnp.exp(warm - 2.0 * tanh_over)
+    reaction = (0.5 * rate) * rise * fade / (1.0 + fade * fade)
+    new_charge = charge - 0.25 * reaction + drawn[0]
+    new_over = 0.7 * over + 0.5 * (now - reaction) + drawn[1]
+    new_heat = 0.9 * heat + 0.2 * reaction * tanh_over + drawn[2]
+    new_film = 0.95 * film + 0.02 * reaction * reaction + drawn[3]
+    predicted = 0.5 + 0.5 * jnp.tanh(0.5 * new_charge) - 0.4 * jnp.tanh(new_over) - (0.2 * now) * new_film
+    return (new_charge, new_over, new_heat, new_film), seen - predicted
+
+
+def fill_unmix(unmix):
+    source = lax.broadcasted_iota(jnp.int32, (LANES, 2 * LANES), 0)
+    target = lax.broadcasted_iota(jnp.int32, (LANES, 2 * LANES), 1)
+    wanted = (target >> 7) * BLOCK + (target & (HALF - 1)) * 2 + ((target >> 5) & 1)
+    unmix[...] = jnp.where(source == wanted, 1.0, 0.0).astype(jnp.bfloat16)
+
+
+def inputs(load, pattern, b, lane):
+    pieces = [load(pattern[k, b]) for k in range(NEIGH)]
+    return jnp.concatenate(
+        [
+            jnp.where(lane < BLOCK, pieces[0], pieces[1]),
+            jnp.where(lane < BLOCK, pieces[2], pieces[3]),
+            pieces[4][:, :BLOCK],
+        ],
+        axis=1,
+    )
+
+
 def members(g):
     return [g * GROUP + i for i in range(GROUP)]
 
@@ -185,7 +220,6 @@
     temper,
     local,
     partner,
-    arriving,
     weights,
     noise_first,
     noise_second,
@@ -194,15 +228,13 @@
     *rest,
 ):
     if epoch:
-        before, *rest = rest
+        before, *rest, seen_rows = rest[:3] + rest[4:] + rest[3:4]
+    else:
+        arriving, *rest = rest
     states, logliks, gather, natural, spread, spread_next, coupled, unmix, total = rest
     lane = lax.broadcasted_iota(jnp.int32, (1, LANES), 1)
 
-    source = lax.broadcasted_iota(jnp.int32, (LANES, 2 * LANES), 0)
-    target = lax.broadcasted_iota(jnp.int32, (LANES, 2 * LANES), 1)
-    wanted = (target >> 7) * BLOCK + (target & (HALF - 1)) * 2 + ((target >> 5) & 1)
-    unmix[...] = jnp.where(source == wanted, 1.0, 0.0).astype(jnp.bfloat16)
-
+    fill_unmix(unmix)
     picks = []
     for j in range(ROWS):
         chosen = ancestors[epoch, 0, j]
@@ -220,9 +252,9 @@
                     local[slot, :, lanes].astype(jnp.float32),
                     partner[slot, :, lanes].astype(jnp.float32),
                 )
-                gather[q, j * STATES : (j + 1) * STATES, :] = jnp.where(
-                    is_new, arriving[0, :, lanes].astype(jnp.float32), kept
-                )
+                if not epoch:
+                    kept = jnp.where(is_new, arriving[0, :, lanes].astype(jnp.float32), kept)
+                gather[q, j * STATES : (j + 1) * STATES, :] = kept
             for c in range(0, STATES, 2):
                 two = [gather[q, pl.ds(c + d, ROWS, stride=STATES), :] for d in range(2)]
                 natural[q, c * ROWS : (c + 2) * ROWS, :] = jnp.concatenate(two, axis=0).astype(
@@ -238,21 +270,10 @@
                     i * rows : (i + 1) * rows, side * LANES : (side + 1) * LANES
                 ]
 
-    def inputs(held, b):
-        pieces = [held[pattern[k, b]] for k in range(NEIGH)]
-        return jnp.concatenate(
-            [
-                jnp.where(lane < BLOCK, pieces[0], pieces[1]),
-                jnp.where(lane < BLOCK, pieces[2], pieces[3]),
-                pieces[4][:, :BLOCK],
-            ],
-            axis=1,
-        )
-
     def couple(held, g):
         for i in range(0, GROUP, 2):
             quad = g * (GROUP // 2) + i // 2
-            four = jnp.concatenate([inputs(held, 4 * quad + d) for d in range(4)], axis=0)
+            four = jnp.concatenate([inputs(lambda n: held[n], pattern, 4 * quad + d, lane) for d in range(4)], axis=0)
             product = jnp.dot(four, weights[quad], preferred_element_type=jnp.float32)
             for side in range(2):
                 part = product[2 * side * rows : 2 * (side + 1) * rows, side * LANES : (side + 1) * LANES]
@@ -263,25 +284,15 @@
         gained = jnp.zeros((ROWS, LANES), jnp.float32)
         for i, q in enumerate(members(g)):
             mixed = 0.6 * natural[q].astype(jnp.float32) + 0.8 * coupled[i]
-            drawn = (noise_first, noise_second)[step % STEPS_EPOCH][q]
-            charge, over, heat, film = (mixed[c * ROWS : (c + 1) * ROWS] for c in range(STATES))
-            rate = cell_rate[pl.ds(q, 1), :]
+            drawn = (noise_first, noise_second)[step % STEPS_EPOCH][
+                pl.ds(pl.multiple_of(q * rows, rows), rows), :
+            ]
             seen = observed[step : step + 1, pl.ds(pl.multiple_of(q * LANES, LANES), LANES)]
-            tanh_over = jnp.tanh(over)
-            fade = jnp.exp(-0.5 * jnp.abs(charge))
-            warm = 0.6 * jnp.tanh(heat)
-            rise = jnp.exp(warm + 2.0 * tanh_over) - jnp.exp(warm - 2.0 * tanh_over)
-            reaction = (0.5 * rate) * rise * fade / (1.0 + fade * fade)
-            new_charge = charge - 0.25 * reaction + drawn[:ROWS]
-            new_over = 0.7 * over + 0.5 * (now - reaction) + drawn[ROWS : 2 * ROWS]
-            new_heat = 0.9 * heat + 0.2 * reaction * tanh_over + drawn[2 * ROWS : 3 * ROWS]
-            new_film = 0.95 * film + 0.02 * reaction * reaction + drawn[3 * ROWS :]
-            predicted = (
-                0.5 + 0.5 * jnp.tanh(0.5 * new_charge) - 0.4 * jnp.tanh(new_over) - (0.2 * now) * new_film
-            )
-            misfit = seen - predicted
+            if epoch:
+                seen_rows[step % STEPS_EPOCH, pl.ds(q, 1), :] = seen
+            parts = ([x[c * ROWS : (c + 1) * ROWS] for c in range(STATES)] for x in (mixed, drawn))
+            fresh, misfit = advance(*parts, cell_rate[pl.ds(q, 1), :], seen, now)
             gained += misfit * misfit
-            fresh = (new_charge, new_over, new_heat, new_film)
             if step % STEPS_EPOCH == STEPS_EPOCH - 1:
                 for c in range(STATES):
                     gather[q, pl.ds(c, ROWS, stride=STATES), :] = fresh[c]
@@ -310,6 +321,75 @@
     if epoch:
         logliks[0:1, :] = before[0:1, :]
     logliks[epoch : epoch + 1, :] = across_lanes
+
+
+def migrant_kernel(
+    migration,
+    pattern,
+    current,
+    temper,
+    arriving,
+    weights,
+    noise_first,
+    noise_second,
+    cell_rate,
+    seen,
+    before,
+    _,
+    logliks,
+    states,
+    rows,
+    spread,
+    unmix,
+    result,
+    sem,
+):
+    slot = migration[1, 0, 0]
+    lane = lax.broadcasted_iota(jnp.int32, (1, LANES), 1)
+    fill_unmix(unmix)
+    for q in range(PAIRS):
+        rows[ROWS * q : ROWS * q + STATES, :] = arriving[0, :, q * LANES : (q + 1) * LANES].astype(jnp.float32)
+    channels = [pl.ds(c, PAIRS, stride=ROWS) for c in range(STATES)]
+    held = [rows[channel, :] for channel in channels]
+    total = jnp.zeros((PAIRS, LANES), jnp.float32)
+    for inner in range(STEPS_EPOCH):
+        placed = jnp.dot(
+            jnp.concatenate(held, axis=0).astype(jnp.bfloat16), unmix[...], preferred_element_type=jnp.float32
+        )
+        for c in range(STATES):
+            for side in range(2):
+                spread[pl.ds(ROWS * side + c, PAIRS, stride=2 * ROWS), :] = placed[
+                    c * PAIRS : (c + 1) * PAIRS, side * LANES : (side + 1) * LANES
+                ]
+
+        def block(n):
+            return spread[pl.ds(pl.multiple_of(n * ROWS, ROWS), ROWS), :]
+
+        for quad in range(BLOCKS // 4):
+            four = jnp.concatenate([inputs(block, pattern, 4 * quad + d, lane) for d in range(4)], axis=0)
+            product = jnp.dot(
+                four.astype(jnp.bfloat16), weights[quad], preferred_element_type=jnp.float32
+            )
+            for side in range(2):
+                part = product[2 * side * ROWS : 2 * (side + 1) * ROWS, side * LANES : (side + 1) * LANES]
+                at = (2 * quad + side) * ROWS
+                rows[at : at + ROWS, :] = jnp.where(lane < BLOCK, part[:ROWS], part[ROWS:])
+        noise = (noise_first, noise_second)[inner]
+        mixed = [0.6 * held[c] + 0.8 * rows[channels[c], :] for c in range(STATES)]
+        drawn = [noise[pl.ds(c * ROWS + slot, PAIRS, stride=STATES * ROWS), :] for c in range(STATES)]
+        fresh, misfit = advance(mixed, drawn, cell_rate[...], seen[inner], current[STEPS_EPOCH + inner])
+        total += misfit * misfit
+        held = [x.astype(jnp.bfloat16).astype(jnp.float32) for x in fresh]
+    for c in range(STATES):
+        rows[channels[c], :] = held[c]
+    for q in range(PAIRS):
+        result[0, :, q * LANES : (q + 1) * LANES] = rows[ROWS * q : ROWS * q + STATES, :].astype(jnp.bfloat16)
+    copy = pltpu.make_async_copy(result, states.at[pl.ds(slot, 1)], sem)
+    copy.start()
+    gained = -0.5 * temper[0] * jnp.sum(jnp.sum(total, axis=0, keepdims=True), axis=1, keepdims=True)
+    epochs = lax.broadcasted_iota(jnp.int32, (EPOCHS, LANES), 0)
+    logliks[...] = jnp.where((epochs == 1) & (lane == slot), gained, before[...])
+    copy.wait()
 
 
 def weigh_kernel(own, other, log_weight, evidence):
@@ -328,7 +408,7 @@
     particles, ancestors, migration, pattern, coupling, cell_rate, current, observed, noise_seeds
 ):
     shape = jax.ShapeDtypeStruct
-    vector = shape((PAIRS, STATES * ROWS, LANES), jnp.float32)
+    vector = shape((PAIRS * STATES * ROWS, LANES), jnp.float32)
     cost = pl.CostEstimate(flops=15000000, bytes_accessed=6000000, transcendentals=0)
     partner = from_partner(particles)
     sources = (noise_seeds, ancestors, migration, pattern.T, current, particles, coupling.transpose(1, 0, 2))
@@ -400,14 +480,15 @@
                 cost_estimate=pl.CostEstimate(flops=3000000, bytes_accessed=10000000, transcendentals=0),
                 name="weights",
             )(front, back)
-        states, logliks = pl.pallas_call(
+        states, logliks, *seen = pl.pallas_call(
             functools.partial(epoch_kernel, epoch),
             out_shape=(
                 shape((ROWS, STATES, CELLS), jnp.bfloat16),
                 shape((EPOCHS, LANES), jnp.float32),
+                *([shape((STEPS_EPOCH, PAIRS, LANES), jnp.float32)] if epoch else []),
             ),
-            in_specs=[SMEM] * 6 + [VMEM] * (9 if epoch else 8),
-            out_specs=(VMEM, VMEM),
+            in_specs=[SMEM] * 6 + [VMEM] * 8,
+            out_specs=(VMEM, VMEM, *([VMEM] if epoch else [])),
             scratch_shapes=[
                 pltpu.VMEM((PAIRS, STATES * ROWS, LANES), jnp.float32),
                 pltpu.VMEM((PAIRS, STATES * ROWS, LANES), jnp.bfloat16),
@@ -418,6 +499,7 @@
                 pltpu.VMEM((ROWS, LANES), jnp.float32),
             ],
             compiler_params=params(12),
+            cost_estimate=pl.CostEstimate(flops=400000000, bytes_accessed=20000000, transcendentals=1000000),
             name="epoch",
         )(
             ancestors,
@@ -428,13 +510,40 @@
             temper,
             states,
             partner,
-            arriving,
             weights,
             *noise,
             rates,
             observed,
-            *([logliks] if epoch else []),
+            logliks if epoch else arriving,
         )
+    logliks, states = pl.pallas_call(
+        migrant_kernel,
+        out_shape=(shape((EPOCHS, LANES), jnp.float32), shape((ROWS, STATES, CELLS), jnp.bfloat16)),
+        in_specs=[SMEM] * 4 + [VMEM] * 7 + [HBM],
+        out_specs=(VMEM, HBM),
+        input_output_aliases={11: 1},
+        scratch_shapes=[
+            pltpu.VMEM((PAIRS * ROWS, LANES), jnp.float32),
+            pltpu.VMEM((BLOCKS * ROWS, LANES), jnp.float32),
+            pltpu.VMEM((LANES, 2 * LANES), jnp.bfloat16),
+            pltpu.VMEM((1, STATES, CELLS), jnp.bfloat16),
+            pltpu.SemaphoreType.DMA,
+        ],
+        compiler_params=params(6),
+        name="migrant",
+    )(
+        migration,
+        pattern,
+        current,
+        temper,
+        arriving,
+        weights,
+        *noise,
+        rates,
+        *seen,
+        logliks,
+        states,
+    )
     log_weight, evidence = pl.pallas_call(
         weigh_kernel,
         out_shape=(shape((EPOCHS, ROWS), jnp.float32), shape((1, 1), jnp.float32)),

time: 33 us -> 31.5 us (0.955)
  waiting for transfers between devices: 6.67 us -> 1.55 us
  Pallas kernels: 20.5 us -> 23.9 us
    ppermute x2, waiting for transfers between devices: 5.52 us -> 0.41 us  [from_behind(): return lax.ppermute(block, 'island', route)]
    pallas_call x0 -> x1, Pallas kernels: none -> 3.34 us  [on_device(): pl.pallas_call(migrant_kernel, out_shape=(shape((EPOCHS, LANES), jnp.floa...]
  transfers between devices with their start and end apart: 5 -> 5, of which waited for: 2 -> 2; matrix products, arithmetic and copies ran while one was open for 0% -> 0% of each run, Pallas kernels for 31% -> 48%
where the time goes in v7:
time: 31.5 us; the launch traced here: 31.3 us
  Pallas kernels  23.9 us (76%)
  starting transfers between devices  5.15 us (16%)
  waiting for transfers between devices  1.55 us (5%)
  between operations  0.74 us (2%)
    pallas_call x2, Pallas kernels, on_device(): pl.pallas_call(functools.partial(epoch_kernel, epoch), out_shape=(shape((...  9.51 us
    pallas_call x1, Pallas kernels, on_device(): pl.pallas_call(weights_kernel, out_shape=shape((BLOCKS // 4, NEIGH * BLOC...  4.51 us
    ppermute x2, starting transfers between devices, from_behind(): return lax.ppermute(block, 'island', route)  4.38 us
    pallas_call x1, Pallas kernels, on_device(): pl.pallas_call(migrant_kernel, out_shape=(shape((EPOCHS, LANES), jnp.floa...  3.34 us
    pallas_call x1, Pallas kernels, on_device(): pl.pallas_call(first_kernel, out_shape=(vector, *(pltpu.SMEM(x.shape, x.d...  1.98 us
    pallas_call x1, Pallas kernels, on_device(): pl.pallas_call(noise_kernel, out_shape=(vector, vector), in_specs=[SMEM],...  1.81 us
    pallas_call x1, Pallas kernels, on_device(): pl.pallas_call(second_kernel, out_shape=(vector, halves), in_specs=[SMEM,...  1.75 us
    ppermute x3, waiting for transfers between devices, from_partner(): return lax.ppermute(value, 'island', pairs)  1.13 us
  transfers between devices with their start and end apart: 5, of which 2 were waited for; matrix products, arithmetic and copies ran while one was open for 0% of the time, Pallas kernels for 48%

profile of v7, /device:TPU:0, one launch (start us, length us, event | category | flops | bytes accessed | tf_op | source)
XLA Modules:
  0.0 31.3 jit_solution(15009221872964451254)
XLA Ops:
  0.6 0.5 %collective-permute-start = (bf16[8,4,8192]{2,1,0:T(4,128)(2,1)}, bf16[8,4,8192]{2,1,0:T(4,128)(2,1)S(1)}, u32[]{:S(2)}, u32[]{:S(2)}) collective-permute-start(bf16[8,4,8192]{2,1,0:T(4,128)(2,1)} %refs_5_.1), channel_id=1, source_target_pairs={{0,1},{1,0},{2,3},{3,2},{4,5},{5,4},{6,7},{7,6},{8,9},{9,8},{10,11... | collective-permute-start | bytes 1572872 | tf_op jit(solution)/shard_map/ppermute | solution.py:41
  1.1 2.0 %first.1 = (f32[2048,128]{1,0:T(8,128)S(1)}, s32[1,4]{1,0:T(1,128)S(4)}, s32[2,1,8]{2,1,0:T(1,128)S(4)}, s32[2,1,8]{2,1,0:T(1,128)S(4)}, s32[5,128]{1,0:T(8,128)...) custom-call(s32[1,4]{1,0:T(1,128)} %refs_0_.1, ...), custom_call_target="tpu_custom_call" | custom-call | flops 15000000 | bytes 6000000 | tf_op jit(solution)/shard_map/first/pallas_call | solution.py:417
  3.1 0.0 collective-permute-done.partner
  3.1 0.1 leaving.2
  3.3 2.6 %collective-permute-start.1 = (bf16[1,4,8192]{2,1,0:T(4,128)(2,1)S(1)}, bf16[1,4,8192]{2,1,0:T(4,128)(2,1)S(1)}, u32[]{:S(2)}, u32[]{:S(2)}) collective-permute-start(bf16[1,4,8192]{2,1,0:T(4,128)(2,1)S(1)} %leaving.2), channel_id=1, source_target_pairs={{14,0},{15,1},{0,2},{1,3},{2,4},{3,5},{4,6},{5,7},{6,8},{7,9},{8,1... | collective-permute-start | bytes 196616 | tf_op jit(solution)/shard_map/ppermute | solution.py:47
  5.9 1.7 %second.1 = (f32[2048,128]{1,0:T(8,128)S(1)}, bf16[5,64,4096]{2,1,0:T(8,128)(2,1)S(1)}) custom-call(s32[1,4]{1,0:T(1,128)S(4)} %get-tuple-element.43.seeds, bf16[5,128,4096]{2,1,0:T(8,128)(2,1)} %bitcast.8), custom_call_target="tpu_custom_call" | custom-call | flops 15000000 | bytes 6000000 | tf_op jit(solution)/shard_map/second/pallas_call | solution.py:462
  7.7 0.0 copy-start
  7.7 0.0 copy-start.1
  7.7 4.5 %weights.1 = bf16[32,320,256]{2,1,0:T(8,128)(2,1)S(1)} custom-call(bf16[5,64,4096]{2,1,0:T(8,128)(2,1)S(1)} %get-tuple-element.41.front, bf16[5,64,4096]{2,1,0:T(8,128)(2,1)S(1)} %get-tuple-element.44.back), custom_call_target="tpu_custom_call" | custom-call | flops 3000000 | bytes 10000000 | tf_op jit(solution)/shard_map/weights/pallas_call | solution.py:473
  12.2 0.0 collective-permute-done.1.rest_0_
  12.2 0.0 copy-done
  12.2 0.0 copy-done.1
  12.2 4.4 %epoch.2 = (bf16[8,4,8192]{2,1,0:T(4,128)(2,1)S(1)}, f32[2,128]{1,0:T(2,128)S(1)}) custom-call(s32[2,1,8]{2,1,0:T(1,128)S(4)} %get-tuple-element.36.ancestors, s32[2,1,8]{2,1,0:T(1,128)S(4)} %get-tuple-element.32.migration, s32[1]{0:T(128)S(4)} %get-tuple-element.37.half, s32[5,128]{1,0:T(8,128)S(4)} %get-tuple-element.33.pattern, ...), custom_call_target="tpu_custom_call" | custom-call | flops 400000000 | bytes 20000000 | tf_op jit(solution)/shard_map/epoch/pallas_call | solution.py:483
  16.6 0.2 collective-permute-start.2
  16.8 1.8 %noise.1 = (f32[2048,128]{1,0:T(8,128)S(1)}, f32[2048,128]{1,0:T(8,128)S(1)}) custom-call(s32[1,4]{1,0:T(1,128)S(4)} %get-tuple-element.43.seeds), custom_call_target="tpu_custom_call" | custom-call | flops 15000000 | bytes 6000000 | tf_op jit(solution)/shard_map/noise/pallas_call | solution.py:440
  18.6 0.0 collective-permute-done.2.partner
  18.7 0.1 leaving.3
  18.8 1.7 %collective-permute-start.3 = (bf16[1,4,8192]{2,1,0:T(4,128)(2,1)S(1)}, bf16[1,4,8192]{2,1,0:T(4,128)(2,1)S(1)}, u32[]{:S(2)}, u32[]{:S(2)}) collective-permute-start(bf16[1,4,8192]{2,1,0:T(4,128)(2,1)S(1)} %leaving.3), channel_id=1, source_target_pairs={{14,0},{15,1},{0,2},{1,3},{2,4},{3,5},{4,6},{5,7},{6,8},{7,9},{8,1... | collective-permute-start | bytes 196616 | tf_op jit(solution)/shard_map/ppermute | solution.py:47
  20.5 5.1 %epoch.3 = (bf16[8,4,8192]{2,1,0:T(4,128)(2,1)}, f32[2,128]{1,0:T(2,128)S(1)}, f32[2,64,128]{2,1,0:T(8,128)S(1)}) custom-call(s32[2,1,8]{2,1,0:T(1,128)S(4)} %get-tuple-element.36.ancestors, s32[2,1,8]{2,1,0:T(1,128)S(4)} %get-tuple-element.32.migration, s32[1]{0:T(128)S(4)} %get-tuple-element.37.half, s32[5,128]{1,0:T(8,128)S(4)} %get-tuple-element.33.pattern, ...), custom_call_target="tpu_custom_call" | custom-call | flops 400000000 | bytes 20000000 | tf_op jit(solution)/shard_map/epoch/pallas_call | solution.py:483
  25.6 0.4 %collective-permute-done.3.arriving = bf16[1,4,8192]{2,1,0:T(4,128)(2,1)S(1)} collective-permute-done((bf16[1,4,8192]{2,1,0:T(4,128)(2,1)S(1)}, bf16[1,4,8192]{2,1,0:T(4,128)(2,1)S(1)}, u32[]{:S(2)}, u32[]{:S(2)}) %collective-permute-start.3) | collective-permute-done | bytes 65568 | tf_op jit(solution)/shard_map/ppermute | solution.py:47
  26.0 3.3 %migrant.1 = (f32[2,128]{1,0:T(2,128)S(1)}, bf16[8,4,8192]{2,1,0:T(4,128)(2,1)}) custom-call(s32[2,1,8]{2,1,0:T(1,128)S(4)} %get-tuple-element.32.migration, s32[5,128]{1,0:T(8,128)S(4)} %get-tuple-element.33.pattern, f32[4]{0:T(128)S(4)} %get-tuple-element.34.current, f32[1]{0:T(128)S(4)} %get-tuple-element.35.temper, ...), custom_call_target="tpu_custom_call", output_to_operand_aliasing={{1}: (11, {})} | custom-call | tf_op jit(solution)/shard_map/migrant/pallas_call | solution.py:519
  29.4 0.1 collective-permute-start.4
  29.5 1.1 %collective-permute-done.4.other = f32[2,128]{1,0:T(2,128)S(1)} collective-permute-done((f32[2,128]{1,0:T(2,128)S(1)}, f32[2,128]{1,0:T(2,128)S(1)}, u32[]{:S(2)}, u32[]{:S(2)}) %collective-permute-start.4) | collective-permute-done | bytes 1056 | tf_op jit(solution)/shard_map/ppermute | solution.py:41
  30.6 0.7 %weigh.1 = (f32[2,8]{1,0:T(2,128)}, f32[1,1]{1,0:T(1,128)}) custom-call(f32[2,128]{1,0:T(2,128)S(1)} %get-tuple-element.58.own, f32[2,128]{1,0:T(2,128)S(1)} %collective-permute-done.4.other), custom_call_target="tpu_custom_call" | custom-call | tf_op jit(solution)/shard_map/weigh/pallas_call | solution.py:547
Async XLA Ops:
  0.6 2.5 %collective-permute-start = (bf16[8,4,8192]{2,1,0:T(4,128)(2,1)}, bf16[8,4,8192]{2,1,0:T(4,128)(2,1)S(1)}, u32[]{:S(2)}, u32[]{:S(2)}) collective-permute-start(bf16[8,4,8192]{2,1,0:T(4,128)(2,1)} %refs_5_.1), channel_id=1, source_target_pairs={{0,1},{1,0},{2,3},{3,2},{4,5},{5,4},{6,7},{7,6},{8,9},{9,8},{10,11... | collective-permute-start | bytes 1572872 | tf_op jit(solution)/shard_map/ppermute | solution.py:41
  3.3 8.9 %collective-permute-start.1 = (bf16[1,4,8192]{2,1,0:T(4,128)(2,1)S(1)}, bf16[1,4,8192]{2,1,0:T(4,128)(2,1)S(1)}, u32[]{:S(2)}, u32[]{:S(2)}) collective-permute-start(bf16[1,4,8192]{2,1,0:T(4,128)(2,1)S(1)} %leaving.2), channel_id=1, source_target_pairs={{14,0},{15,1},{0,2},{1,3},{2,4},{3,5},{4,6},{5,7},{6,8},{7,9},{8,1... | collective-permute-start | bytes 196616 | tf_op jit(solution)/shard_map/ppermute | solution.py:47
  7.7 4.5 %copy-start = (f32[4,8192]{1,0:T(4,128)S(1)}, f32[4,8192]{1,0:T(4,128)}, u32[]{:S(2)}) copy-start(f32[4,8192]{1,0:T(4,128)} %observed.3) | copy-start | bytes 393220
  7.7 4.5 %copy-start.1 = (f32[8192]{0:T(1024)S(1)}, f32[8192]{0:T(1024)}, u32[]{:S(2)}) copy-start(f32[8192]{0:T(1024)} %param.14) | copy-start | bytes 98308
  16.6 2.0 %collective-permute-start.2 = (bf16[8,4,8192]{2,1,0:T(4,128)(2,1)S(1)}, bf16[8,4,8192]{2,1,0:T(4,128)(2,1)S(1)}, u32[]{:S(2)}, u32[]{:S(2)}) collective-permute-start(bf16[8,4,8192]{2,1,0:T(4,128)(2,1)S(1)} %get-tuple-element.47.local), channel_id=1, source_target_pairs={{0,1},{1,0},{2,3},{3,2},{4,5},{5,4},{6,7},{7,6},{8,9},{9,8},{10,11... | collective-permute-start | bytes 1572872 | tf_op jit(solution)/shard_map/ppermute | solution.py:41
  18.8 7.3 %collective-permute-start.3 = (bf16[1,4,8192]{2,1,0:T(4,128)(2,1)S(1)}, bf16[1,4,8192]{2,1,0:T(4,128)(2,1)S(1)}, u32[]{:S(2)}, u32[]{:S(2)}) collective-permute-start(bf16[1,4,8192]{2,1,0:T(4,128)(2,1)S(1)} %leaving.3), channel_id=1, source_target_pairs={{14,0},{15,1},{0,2},{1,3},{2,4},{3,5},{4,6},{5,7},{6,8},{7,9},{8,1... | collective-permute-start | bytes 196616 | tf_op jit(solution)/shard_map/ppermute | solution.py:47
  29.4 1.2 %collective-permute-start.4 = (f32[2,128]{1,0:T(2,128)S(1)}, f32[2,128]{1,0:T(2,128)S(1)}, u32[]{:S(2)}, u32[]{:S(2)}) collective-permute-start(f32[2,128]{1,0:T(2,128)S(1)} %get-tuple-element.58.own), channel_id=1, source_target_pairs={{0,1},{1,0},{2,3},{3,2},{4,5},{5,4},{6,7},{7,6},{8,9},{9,8},{10,11... | collective-permute-start | bytes 3080 | tf_op jit(solution)/shard_map/ppermute | solution.py:41

commit v8 on v7

--- a/solution.py
+++ b/solution.py
@@ -91,25 +91,20 @@
         copy.wait()
 
 
-def second_kernel(seeds, coupling, out, target, sem):
-    copy = pltpu.make_async_copy(coupling.at[:, BLOCKS // 2 :], target, sem)
-    copy.start()
-    draw(seeds[0, 1], out)
-    copy.wait()
-
-
 def noise_kernel(seeds, *outs):
     for step, out in enumerate(outs):
         draw(seeds[0, STEPS_EPOCH + step], out)
 
 
-def weights_kernel(front, back, out, wide):
+def weights_kernel(seeds, front, coupling, out, noise, back, wide, sem):
+    copy = pltpu.make_async_copy(coupling.at[:, BLOCKS // 2 :], back, sem)
+    copy.start()
     group = 16
     lane = lax.broadcasted_iota(jnp.int32, (1, LANES), 1)
 
-    def move(coupling, g, local_g, k, held):
+    def move(blocks, g, local_g, k, held):
         for r in range(HALF):
-            wide[held, r * group : (r + 1) * group, :] = coupling[
+            wide[held, r * group : (r + 1) * group, :] = blocks[
                 k, pl.ds(pl.multiple_of(local_g * group, group), group), r * LANES : (r + 1) * LANES
             ].astype(jnp.float32)
         for b in range(0, group, 2):
@@ -123,13 +118,16 @@
             ] = jnp.concatenate([even, odd], axis=0).astype(jnp.bfloat16)
 
     groups = BLOCKS // 2 // group
-    for part, coupling in enumerate((front, back)):
-
-        def one(at, carry, part=part, coupling=coupling):
+    for part, blocks in enumerate((front, back)):
+        if part:
+            draw(seeds[0, 1], noise)
+            copy.wait()
+
+        def one(at, carry, part=part, blocks=blocks):
             for d in range(TURNS):
                 g = TURNS * at + d
                 for k in range(NEIGH):
-                    move(coupling, part * groups + g, g, k, d * NEIGH + k)
+                    move(blocks, part * groups + g, g, k, d * NEIGH + k)
             return carry
 
         lax.fori_loop(0, groups // TURNS, one, 0)
@@ -335,14 +333,10 @@
     cell_rate,
     seen,
     before,
-    _,
     logliks,
-    states,
     rows,
     spread,
     unmix,
-    result,
-    sem,
 ):
     slot = migration[1, 0, 0]
     lane = lax.broadcasted_iota(jnp.int32, (1, LANES), 1)
@@ -382,13 +376,16 @@
         held = [x.astype(jnp.bfloat16).astype(jnp.float32) for x in fresh]
     for c in range(STATES):
         rows[channels[c], :] = held[c]
-    for q in range(PAIRS):
-        result[0, :, q * LANES : (q + 1) * LANES] = rows[ROWS * q : ROWS * q + STATES, :].astype(jnp.bfloat16)
-    copy = pltpu.make_async_copy(result, states.at[pl.ds(slot, 1)], sem)
-    copy.start()
     gained = -0.5 * temper[0] * jnp.sum(jnp.sum(total, axis=0, keepdims=True), axis=1, keepdims=True)
     epochs = lax.broadcasted_iota(jnp.int32, (EPOCHS, LANES), 0)
     logliks[...] = jnp.where((epochs == 1) & (lane == slot), gained, before[...])
+
+
+def place_kernel(migration, rows, _, states, result, sem):
+    for q in range(PAIRS):
+        result[0, :, q * LANES : (q + 1) * LANES] = rows[ROWS * q : ROWS * q + STATES, :].astype(jnp.bfloat16)
+    copy = pltpu.make_async_copy(result, states.at[pl.ds(migration[1, 0, 0], 1)], sem)
+    copy.start()
     copy.wait()
 
 
@@ -459,27 +456,21 @@
         arriving = from_behind(leaving)
         if not epoch:
             leaving, seeds = lax.optimization_barrier((leaving, seeds))
-            later, back = pl.pallas_call(
-                second_kernel,
-                out_shape=(vector, halves),
-                in_specs=[SMEM, HBM],
+            weights, later = pl.pallas_call(
+                weights_kernel,
+                out_shape=(shape((BLOCKS // 4, NEIGH * BLOCK, 4 * BLOCK), jnp.bfloat16), vector),
+                in_specs=[SMEM, VMEM, HBM],
                 out_specs=(VMEM, VMEM),
-                scratch_shapes=[pltpu.SemaphoreType.DMA],
-                compiler_params=params(2),
-                cost_estimate=cost,
-                name="second",
-            )(seeds, sources[6])
+                scratch_shapes=[
+                    pltpu.VMEM(halves.shape, halves.dtype),
+                    pltpu.VMEM((TURNS * NEIGH, HALF * 16, LANES), jnp.float32),
+                    pltpu.SemaphoreType.DMA,
+                ],
+                compiler_params=params(8),
+                cost_estimate=pl.CostEstimate(flops=18000000, bytes_accessed=16000000, transcendentals=0),
+                name="weights",
+            )(seeds, front, sources[6])
             noise = (noise, later)
-            weights = pl.pallas_call(
-                weights_kernel,
-                out_shape=shape((BLOCKS // 4, NEIGH * BLOCK, 4 * BLOCK), jnp.bfloat16),
-                in_specs=[VMEM, VMEM],
-                out_specs=VMEM,
-                scratch_shapes=[pltpu.VMEM((TURNS * NEIGH, HALF * 16, LANES), jnp.float32)],
-                compiler_params=params(6),
-                cost_estimate=pl.CostEstimate(flops=3000000, bytes_accessed=10000000, transcendentals=0),
-                name="weights",
-            )(front, back)
         states, logliks, *seen = pl.pallas_call(
             functools.partial(epoch_kernel, epoch),
             out_shape=(
@@ -516,34 +507,30 @@
             observed,
             logliks if epoch else arriving,
         )
-    logliks, states = pl.pallas_call(
+    logliks, rows = pl.pallas_call(
         migrant_kernel,
-        out_shape=(shape((EPOCHS, LANES), jnp.float32), shape((ROWS, STATES, CELLS), jnp.bfloat16)),
-        in_specs=[SMEM] * 4 + [VMEM] * 7 + [HBM],
-        out_specs=(VMEM, HBM),
-        input_output_aliases={11: 1},
+        out_shape=(shape((EPOCHS, LANES), jnp.float32), shape((PAIRS * ROWS, LANES), jnp.float32)),
+        in_specs=[SMEM] * 4 + [VMEM] * 7,
+        out_specs=(VMEM, VMEM),
         scratch_shapes=[
-            pltpu.VMEM((PAIRS * ROWS, LANES), jnp.float32),
             pltpu.VMEM((BLOCKS * ROWS, LANES), jnp.float32),
             pltpu.VMEM((LANES, 2 * LANES), jnp.bfloat16),
-            pltpu.VMEM((1, STATES, CELLS), jnp.bfloat16),
-            pltpu.SemaphoreType.DMA,
         ],
-        compiler_params=params(6),
+        compiler_params=params(4),
         name="migrant",
-    )(
-        migration,
-        pattern,
-        current,
-        temper,
-        arriving,
-        weights,
-        *noise,
-        rates,
-        *seen,
-        logliks,
-        states,
-    )
+    )(migration, pattern, current, temper, arriving, weights, *noise, rates, *seen, logliks)
+    other = from_partner(logliks)
+    states = pl.pallas_call(
+        place_kernel,
+        out_shape=shape((ROWS, STATES, CELLS), jnp.bfloat16),
+        in_specs=[SMEM, VMEM, HBM],
+        out_specs=HBM,
+        input_output_aliases={2: 0},
+        scratch_shapes=[pltpu.VMEM((1, STATES, CELLS), jnp.bfloat16), pltpu.SemaphoreType.DMA],
+        compiler_params=params(1),
+        cost_estimate=pl.CostEstimate(flops=1000000, bytes_accessed=2000000, transcendentals=0),
+        name="place",
+    )(migration, rows, states)
     log_weight, evidence = pl.pallas_call(
         weigh_kernel,
         out_shape=(shape((EPOCHS, ROWS), jnp.float32), shape((1, 1), jnp.float32)),
@@ -551,7 +538,7 @@
         out_specs=(VMEM, VMEM),
         compiler_params=params(1),
         name="weigh",
-    )(logliks, from_partner(logliks))
+    )(logliks, other)
     return (states, evidence.reshape(1), log_weight)
 
 

time: 31.5 us -> 30.3 us (0.962)
  Pallas kernels: 23.9 us -> 23.1 us
  starting transfers between devices: 5.15 us -> 4.78 us
    ppermute x3, waiting for transfers between devices: 1.13 us -> 0.56 us  [from_partner(): return lax.ppermute(value, 'island', pairs)]
    pallas_call x1, Pallas kernels: 3.34 us -> 2.77 us  [on_device(): pl.pallas_call(migrant_kernel, out_shape=(shape((EPOCHS, LANES), jnp.floa...]
    ppermute x2, waiting for transfers between devices: 0.41 us -> 0.98 us  [from_behind(): return lax.ppermute(block, 'island', route)]
  transfers between devices with their start and end apart: 5 -> 5, of which waited for: 2 -> 4; matrix products, arithmetic and copies ran while one was open for 0% -> 0% of each run, Pallas kernels for 48% -> 50%
where the time goes in v8:
time: 30.3 us; the launch traced here: 30.1 us
  Pallas kernels  23.1 us (76%)
  starting transfers between devices  4.78 us (16%)
  waiting for transfers between devices  1.54 us (5%)
  between operations  0.72 us (2%)
    pallas_call x2, Pallas kernels, on_device(): pl.pallas_call(functools.partial(epoch_kernel, epoch), out_shape=(shape((...  9.49 us
    pallas_call x1, Pallas kernels, on_device(): pl.pallas_call(weights_kernel, out_shape=(shape((BLOCKS // 4, NEIGH * BLO...  5.44 us
    ppermute x2, starting transfers between devices, from_behind(): return lax.ppermute(block, 'island', route)  4.25 us
    pallas_call x1, Pallas kernels, on_device(): pl.pallas_call(migrant_kernel, out_shape=(shape((EPOCHS, LANES), jnp.floa...  2.77 us
    pallas_call x1, Pallas kernels, on_device(): pl.pallas_call(first_kernel, out_shape=(vector, *(pltpu.SMEM(x.shape, x.d...  1.98 us
    pallas_call x1, Pallas kernels, on_device(): pl.pallas_call(noise_kernel, out_shape=(vector, vector), in_specs=[SMEM],...  1.82 us
    ppermute x2, waiting for transfers between devices, from_behind(): return lax.ppermute(block, 'island', route)  0.98 us
    pallas_call x1, Pallas kernels, on_device(): pl.pallas_call(weigh_kernel, out_shape=(shape((EPOCHS, ROWS), jnp.float32...  0.74 us
  transfers between devices with their start and end apart: 5, of which 4 were waited for; matrix products, arithmetic and copies ran while one was open for 0% of the time, Pallas kernels for 50%

profile of v8, /device:TPU:0, one launch (start us, length us, event | category | flops | bytes accessed | tf_op | source)
XLA Modules:
  0.0 30.1 jit_solution(11282241867766003249)
XLA Ops:
  0.6 0.5 %collective-permute-start = (bf16[8,4,8192]{2,1,0:T(4,128)(2,1)}, bf16[8,4,8192]{2,1,0:T(4,128)(2,1)S(1)}, u32[]{:S(2)}, u32[]{:S(2)}) collective-permute-start(bf16[8,4,8192]{2,1,0:T(4,128)(2,1)} %refs_5_.1), channel_id=1, source_target_pairs={{0,1},{1,0},{2,3},{3,2},{4,5},{5,4},{6,7},{7,6},{8,9},{9,8},{10,11... | collective-permute-start | bytes 1572872 | tf_op jit(solution)/shard_map/ppermute | solution.py:41
  1.1 2.0 %first.1 = (f32[2048,128]{1,0:T(8,128)S(1)}, s32[1,4]{1,0:T(1,128)S(4)}, s32[2,1,8]{2,1,0:T(1,128)S(4)}, s32[2,1,8]{2,1,0:T(1,128)S(4)}, s32[5,128]{1,0:T(8,128)...) custom-call(s32[1,4]{1,0:T(1,128)} %refs_0_.1, ...), custom_call_target="tpu_custom_call" | custom-call | flops 15000000 | bytes 6000000 | tf_op jit(solution)/shard_map/first/pallas_call | solution.py:414
  3.1 0.0 copy-start
  3.1 0.0 copy-start.1
  3.2 0.0 collective-permute-done.partner
  3.2 0.1 leaving.2
  3.3 2.6 %collective-permute-start.1 = (bf16[1,4,8192]{2,1,0:T(4,128)(2,1)S(1)}, bf16[1,4,8192]{2,1,0:T(4,128)(2,1)S(1)}, u32[]{:S(2)}, u32[]{:S(2)}) collective-permute-start(bf16[1,4,8192]{2,1,0:T(4,128)(2,1)S(1)} %leaving.2), channel_id=1, source_target_pairs={{14,0},{15,1},{0,2},{1,3},{2,4},{3,5},{4,6},{5,7},{6,8},{7,9},{8,1... | collective-permute-start | bytes 196616 | tf_op jit(solution)/shard_map/ppermute | solution.py:47
  5.9 5.4 %weights.1 = (bf16[32,320,256]{2,1,0:T(8,128)(2,1)S(1)}, f32[2048,128]{1,0:T(8,128)S(1)}) custom-call(s32[1,4]{1,0:T(1,128)S(4)} %get-tuple-element.42.seeds, bf16[5,64,4096]{2,1,0:T(8,128)(2,1)S(1)} %get-tuple-element.43.front, bf16[5,128,4096]{2,1,0:T(8,128)(2,1)} %bitcast.8), custom_call_target="tpu_custom_call" | custom-call | flops 18000000 | bytes 16000000 | tf_op jit(solution)/shard_map/weights/pallas_call | solution.py:459
  11.4 0.3 %collective-permute-done.1.rest_0_ = bf16[1,4,8192]{2,1,0:T(4,128)(2,1)S(1)} collective-permute-done((bf16[1,4,8192]{2,1,0:T(4,128)(2,1)S(1)}, bf16[1,4,8192]{2,1,0:T(4,128)(2,1)S(1)}, u32[]{:S(2)}, u32[]{:S(2)}) %collective-permute-start.1) | collective-permute-done | bytes 65568 | tf_op jit(solution)/shard_map/ppermute | solution.py:47
  11.7 0.0 copy-done
  11.7 0.0 copy-done.1
  11.7 4.4 %epoch.2 = (bf16[8,4,8192]{2,1,0:T(4,128)(2,1)S(1)}, f32[2,128]{1,0:T(2,128)S(1)}) custom-call(s32[2,1,8]{2,1,0:T(1,128)S(4)} %get-tuple-element.36.ancestors, s32[2,1,8]{2,1,0:T(1,128)S(4)} %get-tuple-element.32.migration, s32[1]{0:T(128)S(4)} %get-tuple-element.37.half, s32[5,128]{1,0:T(8,128)S(4)} %get-tuple-element.33.pattern, ...), custom_call_target="tpu_custom_call" | custom-call | flops 400000000 | bytes 20000000 | tf_op jit(solution)/shard_map/epoch/pallas_call | solution.py:474
  16.1 0.0 collective-permute-start.2
  16.1 1.8 %noise.1 = (f32[2048,128]{1,0:T(8,128)S(1)}, f32[2048,128]{1,0:T(8,128)S(1)}) custom-call(s32[1,4]{1,0:T(1,128)S(4)} %get-tuple-element.42.seeds), custom_call_target="tpu_custom_call" | custom-call | flops 15000000 | bytes 6000000 | tf_op jit(solution)/shard_map/noise/pallas_call | solution.py:437
  17.9 0.1 collective-permute-done.2.partner
  18.0 0.1 leaving.3
  18.1 1.6 %collective-permute-start.3 = (bf16[1,4,8192]{2,1,0:T(4,128)(2,1)S(1)}, bf16[1,4,8192]{2,1,0:T(4,128)(2,1)S(1)}, u32[]{:S(2)}, u32[]{:S(2)}) collective-permute-start(bf16[1,4,8192]{2,1,0:T(4,128)(2,1)S(1)} %leaving.3), channel_id=1, source_target_pairs={{14,0},{15,1},{0,2},{1,3},{2,4},{3,5},{4,6},{5,7},{6,8},{7,9},{8,1... | collective-permute-start | bytes 196616 | tf_op jit(solution)/shard_map/ppermute | solution.py:47
  19.7 5.1 %epoch.3 = (bf16[8,4,8192]{2,1,0:T(4,128)(2,1)}, f32[2,128]{1,0:T(2,128)S(1)}, f32[2,64,128]{2,1,0:T(8,128)S(1)}) custom-call(s32[2,1,8]{2,1,0:T(1,128)S(4)} %get-tuple-element.36.ancestors, s32[2,1,8]{2,1,0:T(1,128)S(4)} %get-tuple-element.32.migration, s32[1]{0:T(128)S(4)} %get-tuple-element.37.half, s32[5,128]{1,0:T(8,128)S(4)} %get-tuple-element.33.pattern, ...), custom_call_target="tpu_custom_call" | custom-call | flops 400000000 | bytes 20000000 | tf_op jit(solution)/shard_map/epoch/pallas_call | solution.py:474
  24.8 0.7 %collective-permute-done.3.arriving = bf16[1,4,8192]{2,1,0:T(4,128)(2,1)S(1)} collective-permute-done((bf16[1,4,8192]{2,1,0:T(4,128)(2,1)S(1)}, bf16[1,4,8192]{2,1,0:T(4,128)(2,1)S(1)}, u32[]{:S(2)}, u32[]{:S(2)}) %collective-permute-start.3) | collective-permute-done | bytes 65568 | tf_op jit(solution)/shard_map/ppermute | solution.py:47
  25.5 2.8 %migrant.1 = (f32[2,128]{1,0:T(2,128)S(1)}, f32[512,128]{1,0:T(8,128)S(1)}) custom-call(s32[2,1,8]{2,1,0:T(1,128)S(4)} %get-tuple-element.32.migration, s32[5,128]{1,0:T(8,128)S(4)} %get-tuple-element.33.pattern, f32[4]{0:T(128)S(4)} %get-tuple-element.34.current, f32[1]{0:T(128)S(4)} %get-tuple-element.35.temper, ...), custom_call_target="tpu_custom_call" | custom-call | tf_op jit(solution)/shard_map/migrant/pallas_call | solution.py:510
  28.2 0.0 collective-permute-start.4
  28.3 0.7 %place.1 = bf16[8,4,8192]{2,1,0:T(4,128)(2,1)} custom-call(s32[2,1,8]{2,1,0:T(1,128)S(4)} %get-tuple-element.32.migration, f32[512,128]{1,0:T(8,128)S(1)} %get-tuple-element.56.rows, bf16[8,4,8192]{2,1,0:T(4,128)(2,1)} %get-tuple-element.57._), custom_call_target="tpu_custom_call", output_to_operand_aliasing={{}: (2, {})} | custom-call | flops 1000000 | bytes 2000000 | tf_op jit(solution)/shard_map/place/pallas_call | solution.py:523
  28.9 0.5 %collective-permute-done.4.other = f32[2,128]{1,0:T(2,128)S(1)} collective-permute-done((f32[2,128]{1,0:T(2,128)S(1)}, f32[2,128]{1,0:T(2,128)S(1)}, u32[]{:S(2)}, u32[]{:S(2)}) %collective-permute-start.4) | collective-permute-done | bytes 1056 | tf_op jit(solution)/shard_map/ppermute | solution.py:41
  29.4 0.7 %weigh.1 = (f32[2,8]{1,0:T(2,128)}, f32[1,1]{1,0:T(1,128)}) custom-call(f32[2,128]{1,0:T(2,128)S(1)} %get-tuple-element.58.own, f32[2,128]{1,0:T(2,128)S(1)} %collective-permute-done.4.other), custom_call_target="tpu_custom_call" | custom-call | tf_op jit(solution)/shard_map/weigh/pallas_call | solution.py:534
Async XLA Ops:
  0.6 2.5 %collective-permute-start = (bf16[8,4,8192]{2,1,0:T(4,128)(2,1)}, bf16[8,4,8192]{2,1,0:T(4,128)(2,1)S(1)}, u32[]{:S(2)}, u32[]{:S(2)}) collective-permute-start(bf16[8,4,8192]{2,1,0:T(4,128)(2,1)} %refs_5_.1), channel_id=1, source_target_pairs={{0,1},{1,0},{2,3},{3,2},{4,5},{5,4},{6,7},{7,6},{8,9},{9,8},{10,11... | collective-permute-start | bytes 1572872 | tf_op jit(solution)/shard_map/ppermute | solution.py:41
  3.1 8.5 %copy-start = (f32[4,8192]{1,0:T(4,128)S(1)}, f32[4,8192]{1,0:T(4,128)}, u32[]{:S(2)}) copy-start(f32[4,8192]{1,0:T(4,128)} %observed.3) | copy-start | bytes 393220
  3.1 8.5 %copy-start.1 = (f32[8192]{0:T(1024)S(1)}, f32[8192]{0:T(1024)}, u32[]{:S(2)}) copy-start(f32[8192]{0:T(1024)} %param.14) | copy-start | bytes 98308
  3.3 8.4 %collective-permute-start.1 = (bf16[1,4,8192]{2,1,0:T(4,128)(2,1)S(1)}, bf16[1,4,8192]{2,1,0:T(4,128)(2,1)S(1)}, u32[]{:S(2)}, u32[]{:S(2)}) collective-permute-start(bf16[1,4,8192]{2,1,0:T(4,128)(2,1)S(1)} %leaving.2), channel_id=1, source_target_pairs={{14,0},{15,1},{0,2},{1,3},{2,4},{3,5},{4,6},{5,7},{6,8},{7,9},{8,1... | collective-permute-start | bytes 196616 | tf_op jit(solution)/shard_map/ppermute | solution.py:47
  16.1 1.9 %collective-permute-start.2 = (bf16[8,4,8192]{2,1,0:T(4,128)(2,1)S(1)}, bf16[8,4,8192]{2,1,0:T(4,128)(2,1)S(1)}, u32[]{:S(2)}, u32[]{:S(2)}) collective-permute-start(bf16[8,4,8192]{2,1,0:T(4,128)(2,1)S(1)} %get-tuple-element.47.local), channel_id=1, source_target_pairs={{0,1},{1,0},{2,3},{3,2},{4,5},{5,4},{6,7},{7,6},{8,9},{9,8},{10,11... | collective-permute-start | bytes 1572872 | tf_op jit(solution)/shard_map/ppermute | solution.py:41
  18.1 7.4 %collective-permute-start.3 = (bf16[1,4,8192]{2,1,0:T(4,128)(2,1)S(1)}, bf16[1,4,8192]{2,1,0:T(4,128)(2,1)S(1)}, u32[]{:S(2)}, u32[]{:S(2)}) collective-permute-start(bf16[1,4,8192]{2,1,0:T(4,128)(2,1)S(1)} %leaving.3), channel_id=1, source_target_pairs={{14,0},{15,1},{0,2},{1,3},{2,4},{3,5},{4,6},{5,7},{6,8},{7,9},{8,1... | collective-permute-start | bytes 196616 | tf_op jit(solution)/shard_map/ppermute | solution.py:47
  28.2 1.1 %collective-permute-start.4 = (f32[2,128]{1,0:T(2,128)S(1)}, f32[2,128]{1,0:T(2,128)S(1)}, u32[]{:S(2)}, u32[]{:S(2)}) collective-permute-start(f32[2,128]{1,0:T(2,128)S(1)} %get-tuple-element.58.own), channel_id=1, source_target_pairs={{0,1},{1,0},{2,3},{3,2},{4,5},{5,4},{6,7},{7,6},{8,9},{9,8},{10,11... | collective-permute-start | bytes 3080 | tf_op jit(solution)/shard_map/ppermute | solution.py:41

commit v9 on v8

--- a/solution.py
+++ b/solution.py
@@ -18,7 +18,8 @@
 ROWS = 8
 LANES = 128
 TURNS = 2
-GROUP = 16
+LAG = 1
+GROUP = 8
 PAIRS = CELLS // LANES
 HALF = BLOCK // 2
 NOISE_SCALE = 0.3 * 2.449489742783178 / 16777216.0
@@ -191,21 +192,10 @@
 
 def in_turn(*stages):
     count = PAIRS // GROUP
-    depth = len(stages)
-
-    def one(at, low, high):
-        for s in reversed(range(low, high)):
-            stages[s](at - s)
-
-    def steady(at, carry):
-        one(at, 0, depth)
-        return carry
-
-    for at in range(depth - 1):
-        one(at, 0, at + 1)
-    lax.fori_loop(depth - 1, count, steady, 0, unroll=2)
-    for at in range(count, count + depth - 1):
-        one(at, at - count + 1, depth)
+    for at in range(count + LAG * (len(stages) - 1)):
+        for s in reversed(range(len(stages))):
+            if 0 <= at - s * LAG < count:
+                stages[s](at - s * LAG)
 
 
 def epoch_kernel(
@@ -275,13 +265,13 @@
             product = jnp.dot(four, weights[quad], preferred_element_type=jnp.float32)
             for side in range(2):
                 part = product[2 * side * rows : 2 * (side + 1) * rows, side * LANES : (side + 1) * LANES]
-                coupled[i + side] = jnp.where(lane < BLOCK, part[:rows], part[rows:])
+                coupled[g * GROUP + i + side] = jnp.where(lane < BLOCK, part[:rows], part[rows:])
 
     def propagate(step, g):
         now = current[step]
         gained = jnp.zeros((ROWS, LANES), jnp.float32)
         for i, q in enumerate(members(g)):
-            mixed = 0.6 * natural[q].astype(jnp.float32) + 0.8 * coupled[i]
+            mixed = 0.6 * natural[q].astype(jnp.float32) + 0.8 * coupled[q]
             drawn = (noise_first, noise_second)[step % STEPS_EPOCH][
                 pl.ds(pl.multiple_of(q * rows, rows), rows), :
             ]
@@ -485,7 +475,7 @@
                 pltpu.VMEM((PAIRS, STATES * ROWS, LANES), jnp.bfloat16),
                 pltpu.VMEM((BLOCKS, STATES * ROWS, LANES), jnp.bfloat16),
                 pltpu.VMEM((BLOCKS, STATES * ROWS, LANES), jnp.bfloat16),
-                pltpu.VMEM((GROUP, STATES * ROWS, LANES), jnp.float32),
+                pltpu.VMEM((PAIRS, STATES * ROWS, LANES), jnp.float32),
                 pltpu.VMEM((LANES, 2 * LANES), jnp.bfloat16),
                 pltpu.VMEM((ROWS, LANES), jnp.float32),
             ],

time: 30.3 us -> 30.2 us (level)
  no operation moved by 1% of the time
where the time goes in v9:
time: 30.2 us; the launch traced here: 30 us
  Pallas kernels  22.9 us (76%)
  starting transfers between devices  4.77 us (16%)
  waiting for transfers between devices  1.64 us (5%)
  between operations  0.72 us (2%)
    pallas_call x2, Pallas kernels, on_device(): pl.pallas_call(functools.partial(epoch_kernel, epoch), out_shape=(shape((...  9.31 us
    pallas_call x1, Pallas kernels, on_device(): pl.pallas_call(weights_kernel, out_shape=(shape((BLOCKS // 4, NEIGH * BLO...  5.44 us
    ppermute x2, starting transfers between devices, from_behind(): return lax.ppermute(block, 'island', route)  4.24 us
    pallas_call x1, Pallas kernels, on_device(): pl.pallas_call(migrant_kernel, out_shape=(shape((EPOCHS, LANES), jnp.floa...  2.77 us
    pallas_call x1, Pallas kernels, on_device(): pl.pallas_call(first_kernel, out_shape=(vector, *(pltpu.SMEM(x.shape, x.d...  1.98 us
    pallas_call x1, Pallas kernels, on_device(): pl.pallas_call(noise_kernel, out_shape=(vector, vector), in_specs=[SMEM],...  1.82 us
    ppermute x2, waiting for transfers between devices, from_behind(): return lax.ppermute(block, 'island', route)  1.08 us
    pallas_call x1, Pallas kernels, on_device(): pl.pallas_call(weigh_kernel, out_shape=(shape((EPOCHS, ROWS), jnp.float32...  0.74 us
  transfers between devices with their start and end apart: 5, of which 4 were waited for; matrix products, arithmetic and copies ran while one was open for 0% of the time, Pallas kernels for 50%

profile of v9, /device:TPU:0, one launch (start us, length us, event | category | flops | bytes accessed | tf_op | source)
XLA Modules:
  0.0 30.0 jit_solution(9102263862388448921)
XLA Ops:
  0.6 0.5 %collective-permute-start = (bf16[8,4,8192]{2,1,0:T(4,128)(2,1)}, bf16[8,4,8192]{2,1,0:T(4,128)(2,1)S(1)}, u32[]{:S(2)}, u32[]{:S(2)}) collective-permute-start(bf16[8,4,8192]{2,1,0:T(4,128)(2,1)} %refs_5_.1), channel_id=1, source_target_pairs={{0,1},{1,0},{2,3},{3,2},{4,5},{5,4},{6,7},{7,6},{8,9},{9,8},{10,11... | collective-permute-start | bytes 1572872 | tf_op jit(solution)/shard_map/ppermute | solution.py:42
  1.1 2.0 %first.1 = (f32[2048,128]{1,0:T(8,128)S(1)}, s32[1,4]{1,0:T(1,128)S(4)}, s32[2,1,8]{2,1,0:T(1,128)S(4)}, s32[2,1,8]{2,1,0:T(1,128)S(4)}, s32[5,128]{1,0:T(8,128)...) custom-call(s32[1,4]{1,0:T(1,128)} %refs_0_.1, ...), custom_call_target="tpu_custom_call" | custom-call | flops 15000000 | bytes 6000000 | tf_op jit(solution)/shard_map/first/pallas_call | solution.py:404
  3.1 0.0 copy-start
  3.1 0.0 copy-start.1
  3.2 0.0 collective-permute-done.partner
  3.2 0.1 leaving.2
  3.3 2.6 %collective-permute-start.1 = (bf16[1,4,8192]{2,1,0:T(4,128)(2,1)S(1)}, bf16[1,4,8192]{2,1,0:T(4,128)(2,1)S(1)}, u32[]{:S(2)}, u32[]{:S(2)}) collective-permute-start(bf16[1,4,8192]{2,1,0:T(4,128)(2,1)S(1)} %leaving.2), channel_id=1, source_target_pairs={{14,0},{15,1},{0,2},{1,3},{2,4},{3,5},{4,6},{5,7},{6,8},{7,9},{8,1... | collective-permute-start | bytes 196616 | tf_op jit(solution)/shard_map/ppermute | solution.py:48
  5.9 5.4 %weights.1 = (bf16[32,320,256]{2,1,0:T(8,128)(2,1)S(1)}, f32[2048,128]{1,0:T(8,128)S(1)}) custom-call(s32[1,4]{1,0:T(1,128)S(4)} %get-tuple-element.42.seeds, bf16[5,64,4096]{2,1,0:T(8,128)(2,1)S(1)} %get-tuple-element.43.front, bf16[5,128,4096]{2,1,0:T(8,128)(2,1)} %bitcast.8), custom_call_target="tpu_custom_call" | custom-call | flops 18000000 | bytes 16000000 | tf_op jit(solution)/shard_map/weights/pallas_call | solution.py:449
  11.4 0.3 %collective-permute-done.1.rest_0_ = bf16[1,4,8192]{2,1,0:T(4,128)(2,1)S(1)} collective-permute-done((bf16[1,4,8192]{2,1,0:T(4,128)(2,1)S(1)}, bf16[1,4,8192]{2,1,0:T(4,128)(2,1)S(1)}, u32[]{:S(2)}, u32[]{:S(2)}) %collective-permute-start.1) | collective-permute-done | bytes 65568 | tf_op jit(solution)/shard_map/ppermute | solution.py:48
  11.7 0.0 copy-done
  11.7 0.0 copy-done.1
  11.7 4.3 %epoch.2 = (bf16[8,4,8192]{2,1,0:T(4,128)(2,1)S(1)}, f32[2,128]{1,0:T(2,128)S(1)}) custom-call(s32[2,1,8]{2,1,0:T(1,128)S(4)} %get-tuple-element.36.ancestors, s32[2,1,8]{2,1,0:T(1,128)S(4)} %get-tuple-element.32.migration, s32[1]{0:T(128)S(4)} %get-tuple-element.37.half, s32[5,128]{1,0:T(8,128)S(4)} %get-tuple-element.33.pattern, ...), custom_call_target="tpu_custom_call" | custom-call | flops 400000000 | bytes 20000000 | tf_op jit(solution)/shard_map/epoch/pallas_call | solution.py:464
  16.0 0.0 collective-permute-start.2
  16.0 1.8 %noise.1 = (f32[2048,128]{1,0:T(8,128)S(1)}, f32[2048,128]{1,0:T(8,128)S(1)}) custom-call(s32[1,4]{1,0:T(1,128)S(4)} %get-tuple-element.42.seeds), custom_call_target="tpu_custom_call" | custom-call | flops 15000000 | bytes 6000000 | tf_op jit(solution)/shard_map/noise/pallas_call | solution.py:427
  17.8 0.1 collective-permute-done.2.partner
  17.9 0.1 leaving.3
  18.0 1.6 %collective-permute-start.3 = (bf16[1,4,8192]{2,1,0:T(4,128)(2,1)S(1)}, bf16[1,4,8192]{2,1,0:T(4,128)(2,1)S(1)}, u32[]{:S(2)}, u32[]{:S(2)}) collective-permute-start(bf16[1,4,8192]{2,1,0:T(4,128)(2,1)S(1)} %leaving.3), channel_id=1, source_target_pairs={{14,0},{15,1},{0,2},{1,3},{2,4},{3,5},{4,6},{5,7},{6,8},{7,9},{8,1... | collective-permute-start | bytes 196616 | tf_op jit(solution)/shard_map/ppermute | solution.py:48
  19.6 5.0 %epoch.3 = (bf16[8,4,8192]{2,1,0:T(4,128)(2,1)}, f32[2,128]{1,0:T(2,128)S(1)}, f32[2,64,128]{2,1,0:T(8,128)S(1)}) custom-call(s32[2,1,8]{2,1,0:T(1,128)S(4)} %get-tuple-element.36.ancestors, s32[2,1,8]{2,1,0:T(1,128)S(4)} %get-tuple-element.32.migration, s32[1]{0:T(128)S(4)} %get-tuple-element.37.half, s32[5,128]{1,0:T(8,128)S(4)} %get-tuple-element.33.pattern, ...), custom_call_target="tpu_custom_call" | custom-call | flops 400000000 | bytes 20000000 | tf_op jit(solution)/shard_map/epoch/pallas_call | solution.py:464
  24.6 0.8 %collective-permute-done.3.arriving = bf16[1,4,8192]{2,1,0:T(4,128)(2,1)S(1)} collective-permute-done((bf16[1,4,8192]{2,1,0:T(4,128)(2,1)S(1)}, bf16[1,4,8192]{2,1,0:T(4,128)(2,1)S(1)}, u32[]{:S(2)}, u32[]{:S(2)}) %collective-permute-start.3) | collective-permute-done | bytes 65568 | tf_op jit(solution)/shard_map/ppermute | solution.py:48
  25.4 2.8 %migrant.1 = (f32[2,128]{1,0:T(2,128)S(1)}, f32[512,128]{1,0:T(8,128)S(1)}) custom-call(s32[2,1,8]{2,1,0:T(1,128)S(4)} %get-tuple-element.32.migration, s32[5,128]{1,0:T(8,128)S(4)} %get-tuple-element.33.pattern, f32[4]{0:T(128)S(4)} %get-tuple-element.34.current, f32[1]{0:T(128)S(4)} %get-tuple-element.35.temper, ...), custom_call_target="tpu_custom_call" | custom-call | tf_op jit(solution)/shard_map/migrant/pallas_call | solution.py:500
  28.2 0.0 collective-permute-start.4
  28.2 0.7 %place.1 = bf16[8,4,8192]{2,1,0:T(4,128)(2,1)} custom-call(s32[2,1,8]{2,1,0:T(1,128)S(4)} %get-tuple-element.32.migration, f32[512,128]{1,0:T(8,128)S(1)} %get-tuple-element.56.rows, bf16[8,4,8192]{2,1,0:T(4,128)(2,1)} %get-tuple-element.57._), custom_call_target="tpu_custom_call", output_to_operand_aliasing={{}: (2, {})} | custom-call | flops 1000000 | bytes 2000000 | tf_op jit(solution)/shard_map/place/pallas_call | solution.py:513
  28.8 0.5 %collective-permute-done.4.other = f32[2,128]{1,0:T(2,128)S(1)} collective-permute-done((f32[2,128]{1,0:T(2,128)S(1)}, f32[2,128]{1,0:T(2,128)S(1)}, u32[]{:S(2)}, u32[]{:S(2)}) %collective-permute-start.4) | collective-permute-done | bytes 1056 | tf_op jit(solution)/shard_map/ppermute | solution.py:42
  29.3 0.7 %weigh.1 = (f32[2,8]{1,0:T(2,128)}, f32[1,1]{1,0:T(1,128)}) custom-call(f32[2,128]{1,0:T(2,128)S(1)} %get-tuple-element.58.own, f32[2,128]{1,0:T(2,128)S(1)} %collective-permute-done.4.other), custom_call_target="tpu_custom_call" | custom-call | tf_op jit(solution)/shard_map/weigh/pallas_call | solution.py:524
Async XLA Ops:
  0.6 2.5 %collective-permute-start = (bf16[8,4,8192]{2,1,0:T(4,128)(2,1)}, bf16[8,4,8192]{2,1,0:T(4,128)(2,1)S(1)}, u32[]{:S(2)}, u32[]{:S(2)}) collective-permute-start(bf16[8,4,8192]{2,1,0:T(4,128)(2,1)} %refs_5_.1), channel_id=1, source_target_pairs={{0,1},{1,0},{2,3},{3,2},{4,5},{5,4},{6,7},{7,6},{8,9},{9,8},{10,11... | collective-permute-start | bytes 1572872 | tf_op jit(solution)/shard_map/ppermute | solution.py:42
  3.1 8.5 %copy-start = (f32[4,8192]{1,0:T(4,128)S(1)}, f32[4,8192]{1,0:T(4,128)}, u32[]{:S(2)}) copy-start(f32[4,8192]{1,0:T(4,128)} %observed.3) | copy-start | bytes 393220
  3.1 8.5 %copy-start.1 = (f32[8192]{0:T(1024)S(1)}, f32[8192]{0:T(1024)}, u32[]{:S(2)}) copy-start(f32[8192]{0:T(1024)} %param.14) | copy-start | bytes 98308
  3.3 8.4 %collective-permute-start.1 = (bf16[1,4,8192]{2,1,0:T(4,128)(2,1)S(1)}, bf16[1,4,8192]{2,1,0:T(4,128)(2,1)S(1)}, u32[]{:S(2)}, u32[]{:S(2)}) collective-permute-start(bf16[1,4,8192]{2,1,0:T(4,128)(2,1)S(1)} %leaving.2), channel_id=1, source_target_pairs={{14,0},{15,1},{0,2},{1,3},{2,4},{3,5},{4,6},{5,7},{6,8},{7,9},{8,1... | collective-permute-start | bytes 196616 | tf_op jit(solution)/shard_map/ppermute | solution.py:48
  16.0 1.9 %collective-permute-start.2 = (bf16[8,4,8192]{2,1,0:T(4,128)(2,1)S(1)}, bf16[8,4,8192]{2,1,0:T(4,128)(2,1)S(1)}, u32[]{:S(2)}, u32[]{:S(2)}) collective-permute-start(bf16[8,4,8192]{2,1,0:T(4,128)(2,1)S(1)} %get-tuple-element.47.local), channel_id=1, source_target_pairs={{0,1},{1,0},{2,3},{3,2},{4,5},{5,4},{6,7},{7,6},{8,9},{9,8},{10,11... | collective-permute-start | bytes 1572872 | tf_op jit(solution)/shard_map/ppermute | solution.py:42
  18.0 7.4 %collective-permute-start.3 = (bf16[1,4,8192]{2,1,0:T(4,128)(2,1)S(1)}, bf16[1,4,8192]{2,1,0:T(4,128)(2,1)S(1)}, u32[]{:S(2)}, u32[]{:S(2)}) collective-permute-start(bf16[1,4,8192]{2,1,0:T(4,128)(2,1)S(1)} %leaving.3), channel_id=1, source_target_pairs={{14,0},{15,1},{0,2},{1,3},{2,4},{3,5},{4,6},{5,7},{6,8},{7,9},{8,1... | collective-permute-start | bytes 196616 | tf_op jit(solution)/shard_map/ppermute | solution.py:48
  28.2 1.1 %collective-permute-start.4 = (f32[2,128]{1,0:T(2,128)S(1)}, f32[2,128]{1,0:T(2,128)S(1)}, u32[]{:S(2)}, u32[]{:S(2)}) collective-permute-start(f32[2,128]{1,0:T(2,128)S(1)} %get-tuple-element.58.own), channel_id=1, source_target_pairs={{0,1},{1,0},{2,3},{3,2},{4,5},{5,4},{6,7},{7,6},{8,9},{9,8},{10,11... | collective-permute-start | bytes 3080 | tf_op jit(solution)/shard_map/ppermute | solution.py:42
